TPU v7x, 512 devices: a whole 4x4x16 slice. The times are simulated.
512 devices in a mesh: grp: 16 (over y, x), dev: 32 (over z, core).
Axes of the slice: x: 4, y: 4, z: 16, core: 2. Of those that a mesh axis runs over, the one named last changes fastest.
Arguments:
- points: float32 [3, 524288], P(None, ('grp', 'dev')), may hold values from 0 to 2
- charges: float32 [16, 524288], P(None, ('grp', 'dev')), may hold values from -6 to 6
- morton: int32 [524288], P(('grp', 'dev')), may hold values from 0 to 1023, as said below
- neighbours: int32 [2048, 8], P(('grp', 'dev')), may hold values from 0 to 2047, as said below
- counts: int32 [2048], P(('grp', 'dev')), may hold values from 1 to 8
- skel_leaf: float32 [3, 524288], P(None, ('grp', 'dev')), may hold values from 0 to 2
- skel_block: float32 [3, 131072], P(None, ('grp', 'dev')), may hold values from 0 to 2
- skel_group: float32 [3, 4096], replicated, may hold values from 0 to 2
Outputs:
- potential: float32 [16, 524288], P(None, ('grp', 'dev'))
Inputs may be any that keep to these rules, and one draw needn't show every extreme that they name: `morton`: each aligned run of 1024 entries is a permutation of 0 to 1023. `neighbours`: entry [q, k] is a leaf other than q, at most 4 leaves away from q; only slots k < counts[q] are used.
All inputs are finite; a program needn't handle non-finite values.
Results may differ from a plain program's by a relative error of at most 0.0003.
Values sent between devices are 32-bit elements; how exact they have to be, the bound alone decides.
No kernel may reach another device: no remote copies, remote signals or barrier semaphores. Data moves between devices by JAX's collectives and lax.ppermute only.
A program may use at most 64 MiB of HBM per device.

v0:
```python
import math

import jax
import jax.numpy as jnp
from jax import lax
from jax.sharding import PartitionSpec as P

width_sq = 0.1
gain_factor = 5.0


def extended_2(cells, sides, width):
    for axis, dim in sides:
        count = lax.axis_size(axis)
        ends = count - 1
        head = lax.slice_in_dim(cells, 0, width, axis=dim)
        tail = lax.slice_in_dim(cells, cells.shape[dim] - width, cells.shape[dim], axis=dim)
        cells = jnp.concatenate(
            [
                lax.ppermute(tail, axis, [(i, (i + 1) % count) for i in range(ends)]),
                cells,
                lax.ppermute(head, axis, [((i + 1) % count, i) for i in range(ends)]),
            ],
            axis=dim,
        )
    return cells


def kernel_tile(source, target):
    distance = (source[0][:, None] - target[0][None, :]) ** 2
    distance = distance + (source[1][:, None] - target[1][None, :]) ** 2
    distance = distance + (source[2][:, None] - target[2][None, :]) ** 2
    return jnp.exp(-distance / width_sq)


def translate(values, source, target, term_count):
    product = jnp.dot(
        values,
        kernel_tile(source, target),
        precision=lax.Precision.HIGHEST,
        preferred_element_type=jnp.float32,
    )
    return gain_factor / math.sqrt(term_count) * product


def far_sum(running, weights, skeleton, target, own_member, skel_rank, term_count):
    span_cols = weights.shape[1]
    block_cols = min(skel_rank, span_cols)

    def one_block(block_index, partial_value):
        column = block_index * block_cols
        piece_w = lax.dynamic_slice_in_dim(weights, column, block_cols, 1)
        piece_s = lax.dynamic_slice_in_dim(skeleton, column, block_cols, 1)
        member = column // skel_rank
        keep_mask = jnp.where(member == own_member, 0.0, 1.0)
        return partial_value + keep_mask * translate(piece_w, piece_s, target, term_count)

    return lax.fori_loop(0, span_cols // block_cols, one_block, running)


def body(points, charges, morton, neighbours, counts, skel_leaf, skel_block, skel_group):
    n_groups = lax.axis_size("grp")
    n_blocks = lax.axis_size("dev")
    vectors, block_pts = charges.shape
    leaf_count = counts.shape[0]
    leaf_size = block_pts // leaf_count
    skel_rank = skel_block.shape[1]
    slot_total = neighbours.shape[1]
    group_id = lax.axis_index("grp")
    member_id = lax.axis_index("dev")
    block_id = group_id * n_blocks + member_id
    sorted_pts = jnp.take(points, morton, axis=1)
    sorted_chg = jnp.take(charges, morton, axis=1)
    leaf_pts = sorted_pts.reshape(3, leaf_count, leaf_size).transpose(1, 0, 2)
    leaf_chg = sorted_chg.reshape(vectors, leaf_count, leaf_size).transpose(1, 0, 2)
    leaf_skel = skel_leaf.reshape(3, leaf_count, skel_rank).transpose(1, 0, 2)
    leaf_weights = lax.map(
        lambda inputs: translate(inputs[0], inputs[1], inputs[2], leaf_size),
        (leaf_chg, leaf_pts, leaf_skel),
    )
    lifted = lax.map(
        lambda inputs: translate(inputs[0], inputs[1], skel_block, leaf_count * skel_rank),
        (leaf_weights, leaf_skel),
    )
    block_weights = jnp.sum(lifted, axis=0)
    own_group = lax.dynamic_slice_in_dim(skel_group, group_id * skel_rank, skel_rank, 1)
    raised = translate(block_weights, skel_block, own_group, n_blocks * skel_rank)
    empty = jnp.zeros((vectors, skel_rank), jnp.float32)
    group_terms = (n_groups - 1) * skel_rank
    group_weights = lax.psum(raised, "dev")
    group_field = far_sum(
        empty,
        lax.all_gather(group_weights, "grp", axis=1, tiled=True),
        skel_group,
        own_group,
        group_id,
        skel_rank,
        group_terms,
    )
    peer_field = far_sum(
        empty,
        lax.all_gather(block_weights, "dev", axis=1, tiled=True),
        lax.all_gather(skel_block, "dev", axis=1, tiled=True),
        skel_block,
        member_id,
        skel_rank,
        (n_blocks - 1) * skel_rank,
    )
    block_field = peer_field + translate(group_field, own_group, skel_block, skel_rank)
    leaf_field = lax.map(
        lambda target: translate(block_field, skel_block, target, skel_rank), leaf_skel
    )
    stacked = jnp.concatenate([sorted_pts, sorted_chg], axis=0)
    extended = extended_2(stacked, ((("grp", "dev"), 1),), block_pts)
    ext_leaves = extended.reshape(3 + vectors, 3 * leaf_count, leaf_size).transpose(1, 0, 2)
    first_leaf = block_id * leaf_count - leaf_count

    def near_leaf(inputs):
        own_pts, own_chg, own_field, own_skel, row_nbr, row_count = inputs
        direct = translate(own_chg, own_pts, own_pts, leaf_size)
        direct = direct + translate(own_field, own_skel, own_pts, skel_rank)

        def one_slot(slot_index, running):
            source = lax.dynamic_index_in_dim(
                ext_leaves, row_nbr[slot_index] - first_leaf, 0, keepdims=False
            )
            tile_term = translate(source[3:], source[:3], own_pts, leaf_size)
            return running + jnp.where(slot_index < row_count, tile_term, jnp.zeros_like(tile_term))

        return lax.fori_loop(0, slot_total, one_slot, direct)

    potential = lax.map(near_leaf, (leaf_pts, leaf_chg, leaf_field, leaf_skel, neighbours, counts))
    return potential.transpose(1, 0, 2).reshape(vectors, block_pts)


def solution(mesh):
    return jax.shard_map(
        body,
        mesh=mesh,
        in_specs=(
            P(None, ("grp", "dev")),
            P(None, ("grp", "dev")),
            P(("grp", "dev")),
            P(("grp", "dev"), None),
            P(("grp", "dev")),
            P(None, ("grp", "dev")),
            P(None, ("grp", "dev")),
            P(),
        ),
        out_specs=P(None, ("grp", "dev")),
        check_vma=False,
    )
```

profile of v0, /device:TPU:8, one launch (start us, length us, event | category | flops | bytes accessed | tf_op | source)
XLA Modules:
  0.0 328.9 jit_solution(2411669421259678028)
XLA Ops:
  0.8 0.9 copy.25
  1.7 2.8 gather_fusion.1
  5.8 2.8 gather_fusion
  9.0 12.9 %collective-permute-start.1 = (f32[19,1024]{1,0:T(8,128)S(1)}, f32[19,1024]{1,0:T(8,128)S(1)}, u32[]{:S(2)}, u32[]{:S(2)}) collective-permute-start(f32[19,1024]{1,0:T(8,128)S(1)} %pad_maximum_fusion.1), channel_id=1, source_target_pairs={{1,0},{2,1},{3,2},{4,3},{5,4},{6,5},{7,6},{8,7},{9,8},{10,9},{11,1... | collective-permute-start | bytes 233480 | tf_op jit(solution)/shard_map/ppermute | solution.py:22
  21.9 1.9 collective-permute-start
  24.6 27.1 %all_gather.10 = f32[3,8192]{1,0:T(4,128)S(1)} all-gather(f32[3,256]{1,0:T(4,128)S(1)} %copy-done), channel_id=1, replica_groups=mesh['grp'=16,'dev'=32] {'dev'}, dimensions={1}, use_global_device_ids=true | all-gather | bytes 101376 | tf_op jit(solution)/shard_map/all_gather | solution.py:103
  52.8 1.6 while.85
  54.5 1.7 while.86
  56.2 30.2 %all_gather.9 = f32[16,8192]{1,0:T(8,128)S(1)} all-gather(f32[16,256]{1,0:T(8,128)S(1)} %reduce_sum.9), channel_id=1, replica_groups=mesh['grp'=16,'dev'=32] {'dev'}, dimensions={1}, use_global_device_ids=true | all-gather | bytes 540672 | tf_op jit(solution)/shard_map/all_gather | solution.py:102
  88.3 90.3 %psum.7 = f32[16,256]{1,0:T(8,128)S(1)} all-reduce(f32[16,256]{1,0:T(8,128)S(1)} %convolution_multiply_fusion.7), channel_id=1, replica_groups=mesh['grp'=16,'dev'=32] {'dev'}, use_global_device_ids=true, to_apply=%region_7.8 | all-reduce | flops 4096 | bytes 32768 | tf_op jit(solution)/shard_map/psum | solution.py:90
  178.7 24.5 %all_gather.11 = f32[16,4096]{1,0:T(8,128)S(1)} all-gather(f32[16,256]{1,0:T(8,128)S(1)} %psum.7), channel_id=1, replica_groups=mesh['grp'=16,'dev'=32] {'grp'}, dimensions={1}, use_global_device_ids=true | all-gather | bytes 278528 | tf_op jit(solution)/shard_map/all_gather | solution.py:93
  203.1 21.3 %while.91 = (s32[]{:T(128)}, f32[16,256]{1,0:T(8,128)S(1)}, f32[16,4096]{1,0:T(8,128)S(1)}, f32[3,4096]{1,0:T(4,128)}, f32[3,256]{1,0:T(4,128)S(1)}, /*index=5*/...) while((s32[]{:T(128)}, f32[16,256]{1,0:T(8,128)S(1)}, ...), condition=%wide.region_9.10_spmd.clone, body=%wide.region_8.9_spmd.clone.sunk | while | flops 13250586 | bytes 68032 | solution.py:58
  203.1 0.9 constant_dynamic-slice_fusion.38
  205.8 0.9 constant_dynamic-slice_fusion.38
  207.1 0.9 constant_dynamic-slice_fusion.38
  209.8 0.9 constant_dynamic-slice_fusion.38
  212.5 0.9 constant_dynamic-slice_fusion.38
  224.4 17.1 %while.90 = (s32[]{:T(128)}, f32[16,256]{1,0:T(8,128)S(1)}, f32[16,8192]{1,0:T(8,128)S(1)}, f32[3,8192]{1,0:T(4,128)S(1)}, f32[3,256]{1,0:T(4,128)S(1)}, /*index...) while((s32[]{:T(128)}, f32[16,256]{1,0:T(8,128)S(1)}, ...), condition=%wide.region_6.7_spmd.clone, body=%wide.region_5.6_spmd.clone.sunk | while | flops 13250586 | bytes 68032 | solution.py:58
  241.9 1.8 while.87
  244.7 83.6 %while.89 = (s32[]{:T(128)}, f32[4,16,256]{2,1,0:T(8,128)S(1)}, f32[4,16,256]{2,1,0:T(8,128)S(1)}, f32[4,3,256]{2,1,0:T(4,128)S(1)}, f32[4,16,256]{2,1,0:T(8,128...) while((s32[]{:T(128)}, f32[4,16,256]{2,1,0:T(8,128)S(1)}, ...), condition=%wide.region_15.16_spmd, body=%wide.region_12.15_spmd.sunk | while | flops 39735312 | bytes 213682 | solution.py:132
  246.7 18.8 %while.92 = (s32[]{:T(128)}, f32[16,256]{1,0:T(8,128)S(1)}, s32[]{:T(128)}, s32[8]{0:T(128)S(1)}, s32[]{:T(128)}, /*index=5*/f32[12,19,256]{2,1,0:T(8,128)S(1)},...) while((s32[]{:T(128)}, f32[16,256]{1,0:T(8,128)S(1)}, ...), condition=%wide.region_14.14_spmd, body=%wide.region_13.13_spmd.sunk | while | flops 13250570 | bytes 67841 | solution.py:130
  267.6 18.8 %while.92 = (s32[]{:T(128)}, f32[16,256]{1,0:T(8,128)S(1)}, s32[]{:T(128)}, s32[8]{0:T(128)S(1)}, s32[]{:T(128)}, /*index=5*/f32[12,19,256]{2,1,0:T(8,128)S(1)},...) while((s32[]{:T(128)}, f32[16,256]{1,0:T(8,128)S(1)}, ...), condition=%wide.region_14.14_spmd, body=%wide.region_13.13_spmd.sunk | while | flops 13250570 | bytes 67841 | solution.py:130
  288.5 18.8 %while.92 = (s32[]{:T(128)}, f32[16,256]{1,0:T(8,128)S(1)}, s32[]{:T(128)}, s32[8]{0:T(128)S(1)}, s32[]{:T(128)}, /*index=5*/f32[12,19,256]{2,1,0:T(8,128)S(1)},...) while((s32[]{:T(128)}, f32[16,256]{1,0:T(8,128)S(1)}, ...), condition=%wide.region_14.14_spmd, body=%wide.region_13.13_spmd.sunk | while | flops 13250570 | bytes 67841 | solution.py:130
  309.4 18.8 %while.92 = (s32[]{:T(128)}, f32[16,256]{1,0:T(8,128)S(1)}, s32[]{:T(128)}, s32[8]{0:T(128)S(1)}, s32[]{:T(128)}, /*index=5*/f32[12,19,256]{2,1,0:T(8,128)S(1)},...) while((s32[]{:T(128)}, f32[16,256]{1,0:T(8,128)S(1)}, ...), condition=%wide.region_14.14_spmd, body=%wide.region_13.13_spmd.sunk | while | flops 13250570 | bytes 67841 | solution.py:130
  (320 shorter events, 85.6 us)
Async XLA Ops:
  0.0 0.8 copy-start.3
  4.7 0.8 copy-start.2
  9.0 234.7 %collective-permute-start.1 = (f32[19,1024]{1,0:T(8,128)S(1)}, f32[19,1024]{1,0:T(8,128)S(1)}, u32[]{:S(2)}, u32[]{:S(2)}) collective-permute-start(f32[19,1024]{1,0:T(8,128)S(1)} %pad_maximum_fusion.1), channel_id=1, source_target_pairs={{1,0},{2,1},{3,2},{4,3},{5,4},{6,5},{7,6},{8,7},{9,8},{10,9},{11,1... | collective-permute-start | bytes 233480 | tf_op jit(solution)/shard_map/ppermute | solution.py:22
  21.9 221.8 %collective-permute-start = (f32[19,1024]{1,0:T(8,128)S(1)}, f32[19,1024]{1,0:T(8,128)S(1)}, u32[]{:S(2)}, u32[]{:S(2)}) collective-permute-start(f32[19,1024]{1,0:T(8,128)S(1)} %pad_maximum_fusion.1), channel_id=1, source_target_pairs={{0,1},{1,2},{2,3},{3,4},{4,5},{5,6},{6,7},{7,8},{8,9},{9,10},{10,1... | collective-permute-start | bytes 233480 | tf_op jit(solution)/shard_map/ppermute | solution.py:20
  23.9 0.7 copy-start
  52.1 0.7 copy-start.1
  244.0 0.7 copy-start.4
where the time goes:
time: 331 us; the launch traced here: 329 us
  blocking collectives  172 us (52%)
  local copies, waits for them, and re-layouts  55.4 us (17%)
  loops' own time  45.1 us (14%)
  matrix products  39.9 us (12%)
  starting transfers between devices  14.8 us (4%)
    psum x1, blocking collectives, body(): group_weights = lax.psum(raised, 'dev')  90.3 us
    another operation x4, loops' own time, near_leaf(): return lax.fori_loop(0, slot_total, one_slot, direct)  41.7 us
    dot_general x102, matrix products, translate(): jnp.dot(values, kernel_tile(source, target), precision=lax.Precision.HIGH...  39.9 us
    all_gather x1, blocking collectives, body(): lax.all_gather(block_weights, 'dev', axis=1, tiled=True)  30.2 us
    all_gather x1, blocking collectives, body(): lax.all_gather(skel_block, 'dev', axis=1, tiled=True)  27.1 us
    all_gather x1, blocking collectives, body(): lax.all_gather(group_weights, 'grp', axis=1, tiled=True)  24.5 us
    dynamic_slice x32, local copies, waits for them, and re-layouts, one_slot(): row_nbr[slot_index] - first_leaf  19.9 us
    slice x138, local copies, waits for them, and re-layouts, kernel_tile(): distance = (source[0][:, None] - target[0][None, :]) ** 2  18.6 us
  transfers between devices with their start and end apart: 2, of which 0 were waited for; matrix products, arithmetic and copies ran while one was open for 13% of the time, Pallas kernels for 0%

commit v1 on v0

v1 whole, which is shorter than its diff:
```python
import functools
import math

import jax
import jax.numpy as jnp
from jax import lax
from jax.experimental import pallas as pl
from jax.experimental.pallas import tpu as pltpu
from jax.sharding import PartitionSpec as P

f32 = jnp.float32
bf16 = jnp.bfloat16
width_sq = 0.1
gain_factor = 5.0
coord_scale = math.sqrt(math.log2(math.e) / width_sq)
VEC = 16
ROWS = 24
T = 256
LEAVES_DEV = 4


def dg(a, b, ca, cb):
    return lax.dot_general(a, b, (((ca,), (cb,)), ((), ())), preferred_element_type=f32)


def split2(v):
    h = v.astype(bf16)
    return h, (v - h.astype(f32)).astype(bf16)


def split3(v):
    a = v.astype(bf16).astype(f32)
    r = v - a
    b = r.astype(bf16).astype(f32)
    return a, b, r - b


def centred(x3):
    x = (x3 - 1.0) * coord_scale
    n = jnp.sum(x * x, axis=0, keepdims=True)
    return x, n, jnp.ones_like(n), jnp.zeros((3,) + n.shape[1:], f32)


def feat_src(x3):
    x, n, o, z = centred(x3)
    a, b, c = split3(jnp.concatenate([x, n, o, z], axis=0))
    return jnp.concatenate([a, a, a, b, b, c], axis=0).astype(bf16)


def feat_tgt(x3):
    x, n, o, z = centred(x3)
    a, b, c = split3(jnp.concatenate([2.0 * x, -o, -n, z], axis=0))
    return jnp.concatenate([a, b, c, a, b, a], axis=0).astype(bf16)


def tile(fs, ft):
    return split2(jnp.exp2(dg(fs, ft, 0, 0)))


def stack2(v):
    h, l = split2(v)
    return jnp.concatenate([h, l], axis=0)


def times(vv, kt):
    kh, kl = kt
    r = dg(vv, kh, 1, 0)
    return r[:VEC] + r[VEC:] + dg(vv[:VEC], kl, 1, 0)


def gain(count):
    return gain_factor / math.sqrt(count)


def up_kernel(pts_ref, chg_ref, mor_ref, skl_ref, skb_ref, srt_ref, bws_ref):
    n = chg_ref.shape[1]
    rows = jnp.concatenate([chg_ref[...], pts_ref[...], jnp.zeros((5, n), f32)], axis=0)
    a, b, c = split3(rows)
    parts = jnp.concatenate([a, b, c], axis=0).astype(bf16)
    for i in range(n // T):
        col = slice(i * T, (i + 1) * T)
        hot = (lax.broadcasted_iota(jnp.int32, (n, T), 0) == mor_ref[:, col]).astype(f32).astype(bf16)
        s = dg(parts, hot, 1, 0)
        srt_ref[:, col] = s[:ROWS] + s[ROWS : 2 * ROWS] + s[2 * ROWS :]
    ft_block = feat_tgt(skb_ref[...])
    total = jnp.zeros((VEC, T), f32)
    for q in range(LEAVES_DEV):
        col = slice(q * T, (q + 1) * T)
        skel = skl_ref[:, col]
        lw = times(stack2(srt_ref[:VEC, col]), tile(feat_src(srt_ref[VEC : VEC + 3, col]), feat_tgt(skel)))
        total = total + times(stack2(gain(T) * lw), tile(feat_src(skel), ft_block))
    bws_ref[:VEC, :] = gain(LEAVES_DEV * T) * total
    bws_ref[VEC:, :] = jnp.concatenate([skb_ref[...], jnp.zeros((5, T), f32)], axis=0)


def group_kernel(id_ref, all_ref, skg_ref, gw_ref):
    n = all_ref.shape[0]
    own = pl.ds(pl.multiple_of(id_ref[0] * T, T), T)
    ft = feat_tgt(skg_ref[:, own])
    total = jnp.zeros((VEC, T), f32)
    for c in range(n):
        total = total + times(stack2(all_ref[c, :VEC, :]), tile(feat_src(all_ref[c, VEC : VEC + 3, :]), ft))
    total = gain(n * T) * total
    for g in range(gw_ref.shape[0]):
        gw_ref[g] = total


def near_kernel(id_ref, nbr_ref, cnt_ref, left_ref, mid_ref, right_ref, all_ref, skb_ref, near_ref, peer_ref):
    member = id_ref[1]
    n = all_ref.shape[0]
    ft = feat_tgt(skb_ref[...])
    total = jnp.zeros((VEC, T), f32)
    for c in range(n):
        keep = jnp.where(member == c, 0.0, 1.0)
        total = total + times(stack2(keep * all_ref[c, :VEC, :]), tile(feat_src(all_ref[c, VEC : VEC + 3, :]), ft))
    peer_ref[...] = gain((n - 1) * T) * total
    first = id_ref[2]
    fts = [feat_tgt(mid_ref[VEC : VEC + 3, q * T : (q + 1) * T]) for q in range(LEAVES_DEV)]
    acc = [jnp.zeros((VEC, T), f32) for _ in range(LEAVES_DEV)]
    for s in range(-LEAVES_DEV, 2 * LEAVES_DEV):
        ref = (left_ref, mid_ref, right_ref)[s // LEAVES_DEV + 1]
        j = s % LEAVES_DEV
        v = ref[:VEC, j * T : (j + 1) * T]
        fs = feat_src(ref[VEC : VEC + 3, j * T : (j + 1) * T])
        for q in range(LEAVES_DEV):
            if abs(s - q) > LEAVES_DEV:
                continue
            uses = jnp.int32(1 if s == q else 0)
            for k in range(nbr_ref.shape[1]):
                hit = jnp.logical_and(nbr_ref[q, k] == first + s, cnt_ref[q] > k)
                uses = uses + hit.astype(jnp.int32)
            acc[q] = acc[q] + times(stack2(uses.astype(f32) * v), tile(fs, fts[q]))
    for q in range(LEAVES_DEV):
        near_ref[:, q * T : (q + 1) * T] = gain(T) * acc[q]


def down_kernel(id_ref, gws_ref, skg_ref, peer_ref, skb_ref, skl_ref, mid_ref, near_ref, out_ref):
    group = id_ref[0]
    n = gws_ref.shape[0]
    own = skg_ref[:, pl.ds(pl.multiple_of(group * T, T), T)]
    ft_own = feat_tgt(own)
    total = jnp.zeros((VEC, T), f32)
    for g in range(n):
        keep = jnp.where(group == g, 0.0, 1.0)
        total = total + times(stack2(keep * gws_ref[g]), tile(feat_src(skg_ref[:, g * T : (g + 1) * T]), ft_own))
    field = gain((n - 1) * T) * total
    field = peer_ref[...] + gain(T) * times(stack2(field), tile(feat_src(own), feat_tgt(skb_ref[...])))
    vv = stack2(field)
    fs_block = feat_src(skb_ref[...])
    for q in range(LEAVES_DEV):
        col = slice(q * T, (q + 1) * T)
        lf = gain(T) * times(vv, tile(fs_block, feat_tgt(skl_ref[:, col])))
        far = times(stack2(lf), tile(feat_src(skl_ref[:, col]), feat_tgt(mid_ref[VEC : VEC + 3, col])))
        out_ref[:, col] = near_ref[:, col] + gain(T) * far


VM = pl.BlockSpec(memory_space=pltpu.VMEM)
SM = pl.BlockSpec(memory_space=pltpu.SMEM)


def shape(*dims):
    return jax.ShapeDtypeStruct(dims, f32)


def body(points, charges, morton, neighbours, counts, skel_leaf, skel_block, skel_group):
    n_groups = lax.axis_size("grp")
    n_blocks = lax.axis_size("dev")
    n = points.shape[1]
    group_id = lax.axis_index("grp")
    member_id = lax.axis_index("dev")
    block_id = group_id * n_blocks + member_id
    ids = jnp.stack([group_id, member_id, block_id * LEAVES_DEV]).astype(jnp.int32)
    srt, bws = pl.pallas_call(
        up_kernel,
        out_shape=(shape(ROWS, n), shape(ROWS, T)),
        in_specs=[VM] * 5,
        out_specs=(VM, VM),
        name="up",
    )(points, charges, morton.reshape(1, n), skel_leaf, skel_block)
    whole = n_groups * n_blocks
    left = lax.ppermute(srt, ("grp", "dev"), [(i, i + 1) for i in range(whole - 1)])
    right = lax.ppermute(srt, ("grp", "dev"), [(i + 1, i) for i in range(whole - 1)])
    all_bws = lax.all_gather(bws, "dev", axis=0, tiled=False)
    gw = pl.pallas_call(
        group_kernel,
        out_shape=shape(n_groups, VEC, T),
        in_specs=[SM, VM, VM],
        out_specs=VM,
        name="group",
    )(ids, all_bws, skel_group)
    gws = lax.all_to_all(gw, "grp", 0, 0, tiled=False)
    near, peer = pl.pallas_call(
        near_kernel,
        out_shape=(shape(VEC, n), shape(VEC, T)),
        in_specs=[SM, SM, SM, VM, VM, VM, VM, VM],
        out_specs=(VM, VM),
        name="near",
    )(ids, neighbours, counts, left, srt, right, all_bws, skel_block)
    return pl.pallas_call(
        down_kernel,
        out_shape=shape(VEC, n),
        in_specs=[SM] + [VM] * 7,
        out_specs=VM,
        name="down",
    )(ids, gws, skel_group, peer, skel_block, skel_leaf, srt, near)


def solution(mesh):
    return jax.shard_map(
        body,
        mesh=mesh,
        in_specs=(
            P(None, ("grp", "dev")),
            P(None, ("grp", "dev")),
            P(("grp", "dev")),
            P(("grp", "dev"), None),
            P(("grp", "dev")),
            P(None, ("grp", "dev")),
            P(None, ("grp", "dev")),
            P(),
        ),
        out_specs=P(None, ("grp", "dev")),
        check_vma=False,
    )
```

time: 331 us -> 82.4 us (0.25)
  blocking collectives: 172 us -> 41.3 us
  local copies, waits for them, and re-layouts: 55.4 us -> 1.34 us
  loops' own time: 45.1 us -> 0 us
  matrix products: 39.9 us -> 0 us
  Pallas kernels: 0 us -> 19.3 us
    psum x1 -> x0, blocking collectives: 90.3 us -> none  [body(): group_weights = lax.psum(raised, 'dev')]
    another operation x10 -> x0, loops' own time: 45.1 us -> none  [the longest x4 41.7 us: near_leaf(): return lax.fori_loop(0, slot_total, one_slot, direct)]
    all_gather x3 -> x1, blocking collectives: 81.7 us -> 41.3 us  [body(): all_bws = lax.all_gather(bws, 'dev', axis=0, tiled=False)]
    dot_general x102 -> x0, matrix products: 39.9 us -> none  [translate(): jnp.dot(values, kernel_tile(source, target), precision=lax.Precision.HIGH...]
    dynamic_slice x37 -> x0, local copies, waits for them, and re-layouts: 23 us -> none  [the longest x32 19.9 us: one_slot(): row_nbr[slot_index] - first_leaf]
    pallas_call x0 -> x4, Pallas kernels: none -> 19.3 us  [the longest x1 6.83 us: body(): pl.pallas_call(near_kernel, out_shape=(shape(VEC, n), shape(VEC, T)), in_...]
    slice x138 -> x0, local copies, waits for them, and re-layouts: 18.6 us -> none  [kernel_tile(): distance = (source[0][:, None] - target[0][None, :]) ** 2]
    all_to_all x0 -> x1, starting transfers between devices: none -> 7.53 us  [body(): gws = lax.all_to_all(gw, 'grp', 0, 0, tiled=False)]
  transfers between devices with their start and end apart: 2 -> 3, of which waited for: 0 -> 2; matrix products, arithmetic and copies ran while one was open for 13% -> 0% of each run, Pallas kernels for 0% -> 8%
where the time goes in v1:
time: 82.4 us; the launch traced here: 82.1 us
  blocking collectives  41.3 us (50%)
  Pallas kernels  19.3 us (23%)
  starting transfers between devices  17.5 us (21%)
  waiting for transfers between devices  2.01 us (2%)
  local copies, waits for them, and re-layouts  1.34 us (2%)
    all_gather x1, blocking collectives, body(): all_bws = lax.all_gather(bws, 'dev', axis=0, tiled=False)  41.3 us
    ppermute x1, starting transfers between devices, body(): lax.ppermute(srt, ('grp', 'dev'), [(i + 1, i) for i in range(whole - 1)])  8.04 us
    all_to_all x1, starting transfers between devices, body(): gws = lax.all_to_all(gw, 'grp', 0, 0, tiled=False)  7.53 us
    pallas_call x1, Pallas kernels, body(): pl.pallas_call(near_kernel, out_shape=(shape(VEC, n), shape(VEC, T)), in_...  6.83 us
    pallas_call x1, Pallas kernels, body(): pl.pallas_call(group_kernel, out_shape=shape(n_groups, VEC, T), in_specs=...  4.39 us
    pallas_call x1, Pallas kernels, body(): pl.pallas_call(down_kernel, out_shape=shape(VEC, n), in_specs=[SM] + [VM]...  4.25 us
    pallas_call x1, Pallas kernels, body(): pl.pallas_call(up_kernel, out_shape=(shape(ROWS, n), shape(ROWS, T)), in_...  3.84 us
    ppermute x1, starting transfers between devices, body(): lax.ppermute(srt, ('grp', 'dev'), [(i, i + 1) for i in range(whole - 1)])  1.92 us
  transfers between devices with their start and end apart: 3, of which 2 were waited for; matrix products, arithmetic and copies ran while one was open for 0% of the time, Pallas kernels for 8%

profile of v1, /device:TPU:8, one launch (start us, length us, event | category | flops | bytes accessed | tf_op | source)
XLA Modules:
  0.0 82.1 jit_solution(3297350950778990000)
XLA Ops:
  0.0 3.8 %up.1 = (f32[24,1024]{1,0:T(8,128)}, f32[24,256]{1,0:T(8,128)}) custom-call(f32[3,1024]{1,0:T(4,128)} %pts_ref.1, f32[16,1024]{1,0:T(8,128)} %chg_ref.1, s32[1,1024]{1,0:T(1,128)} %bitcast.7, f32[3,1024]{1,0:T(4,128)} %skl_ref.3, f32[3,256]{1,0:T(4,128)} %skb_ref.5), custom_call_target="tpu_custom_call" | custom-call | tf_op jit(solution)/shard_map/up/pallas_call | solution.py:173
  3.8 41.3 %all-gather = f32[768,256]{1,0:T(8,128)} all-gather(f32[24,256]{1,0:T(8,128)} %get-tuple-element.9), channel_id=2, replica_groups=mesh['grp'=16,'dev'=32] {'dev'}, dimensions={0}, use_global_device_ids=true | all-gather | bytes 811008 | tf_op jit(solution)/shard_map/all_gather | solution.py:183
  45.1 0.7 pad_add_fusion.id_ref
  45.8 4.4 %group.1 = f32[16,16,256]{2,1,0:T(8,128)} custom-call(s32[3]{0:T(128)} %pad_add_fusion.id_ref, f32[32,24,256]{2,1,0:T(8,128)} %bitcast.5, f32[3,4096]{1,0:T(4,128)} %skg_ref.3), custom_call_target="tpu_custom_call" | custom-call | tf_op jit(solution)/shard_map/group/pallas_call | solution.py:184
  50.1 0.0 copy-start.1
  50.1 7.5 %all-to-all-start = ((f32[16,16,256]{2,1,0:T(8,128)}), f32[16,16,256]{2,1,0:T(8,128)S(1)}, u32[]{:S(2)}, u32[]{:S(2)}) async-start(f32[16,16,256]{2,1,0:T(8,128)} %group.1), calls=%async_computation | async-start | bytes 524288 | tf_op jit(solution)/shard_map/all_to_all | solution.py:191
  57.7 0.0 copy-done.1
  57.7 1.9 %collective-permute-start = (f32[24,1024]{1,0:T(8,128)S(1)}, f32[24,1024]{1,0:T(8,128)S(1)}, u32[]{:S(2)}, u32[]{:S(2)}) collective-permute-start(f32[24,1024]{1,0:T(8,128)S(1)} %copy-done.1), channel_id=1, source_target_pairs={{0,1},{1,2},{2,3},{3,4},{4,5},{5,6},{6,7},{7,8},{8,9},{9,10},{10,1... | collective-permute-start | bytes 294920 | tf_op jit(solution)/shard_map/ppermute | solution.py:181
  59.6 8.0 %collective-permute-start.1 = (f32[24,1024]{1,0:T(8,128)S(1)}, f32[24,1024]{1,0:T(8,128)S(1)}, u32[]{:S(2)}, u32[]{:S(2)}) collective-permute-start(f32[24,1024]{1,0:T(8,128)S(1)} %copy-done.1), channel_id=1, source_target_pairs={{1,0},{2,1},{3,2},{4,3},{5,4},{6,5},{7,6},{8,7},{9,8},{10,9},{11,1... | collective-permute-start | bytes 294920 | tf_op jit(solution)/shard_map/ppermute | solution.py:182
  67.7 0.2 collective-permute-done.left_ref
  67.8 0.0 copy-start.2
  67.8 1.8 %collective-permute-done.1.right_ref = f32[24,1024]{1,0:T(8,128)S(1)} collective-permute-done((f32[24,1024]{1,0:T(8,128)S(1)}, f32[24,1024]{1,0:T(8,128)S(1)}, u32[]{:S(2)}, u32[]{:S(2)}) %collective-permute-start.1) | collective-permute-done | bytes 98336 | tf_op jit(solution)/shard_map/ppermute | solution.py:182
  69.7 0.0 copy-done.2
  69.7 0.0 copy-start.3
  69.7 0.6 copy-done.3
  70.3 6.8 %near.1 = (f32[16,1024]{1,0:T(8,128)}, f32[16,256]{1,0:T(8,128)}) custom-call(s32[3]{0:T(128)} %pad_add_fusion.id_ref, s32[4,8]{1,0:T(4,128)} %nbr_ref.1, s32[4]{0:T(128)} %cnt_ref.1, f32[24,1024]{1,0:T(8,128)} %copy-done.2, f32[24,1024]{1,0:T(8,128)} %get-tuple-element.10.mid_ref, f32[24,1024]{1,0:T(8,128)} %copy-done.3, f32[32,24,256]{2,1,0:T(8,128)} %bitcast.6, ...), custom_call_target="tpu_custom_call" | custom-call | tf_op jit(solution)/shard_map/near/pallas_call | solution.py:192
  77.1 0.0 all-to-all-done.gws_ref
  77.1 0.0 copy-start
  77.1 0.7 copy-done
  77.8 4.2 %down.1 = f32[16,1024]{1,0:T(8,128)} custom-call(s32[3]{0:T(128)} %pad_add_fusion.id_ref, f32[16,16,256]{2,1,0:T(8,128)} %copy-done, f32[3,4096]{1,0:T(4,128)} %skg_ref.3, f32[16,256]{1,0:T(8,128)} %get-tuple-element.11.peer_ref, f32[3,256]{1,0:T(4,128)} %skb_ref.5, f32[3,1024]{1,0:T(4,128)} %skl_ref.3, f32[24,1024]{1,0:T(8,128)} %get-tuple-element.10.mid_ref, ...), custom_call_target="tpu_custom_call" | custom-call | tf_op jit(solution)/shard_map/down/pallas_call | solution.py:199
Async XLA Ops:
  50.1 7.5 %copy-start.1 = (f32[24,1024]{1,0:T(8,128)S(1)}, f32[24,1024]{1,0:T(8,128)}, u32[]{:S(2)}) copy-start(f32[24,1024]{1,0:T(8,128)} %get-tuple-element.10.mid_ref) | copy-start | bytes 294916
  50.1 27.0 %all-to-all-start = ((f32[16,16,256]{2,1,0:T(8,128)}), f32[16,16,256]{2,1,0:T(8,128)S(1)}, u32[]{:S(2)}, u32[]{:S(2)}) async-start(f32[16,16,256]{2,1,0:T(8,128)} %group.1), calls=%async_computation | async-start | bytes 524288 | tf_op jit(solution)/shard_map/all_to_all | solution.py:191
  57.7 10.2 %collective-permute-start = (f32[24,1024]{1,0:T(8,128)S(1)}, f32[24,1024]{1,0:T(8,128)S(1)}, u32[]{:S(2)}, u32[]{:S(2)}) collective-permute-start(f32[24,1024]{1,0:T(8,128)S(1)} %copy-done.1), channel_id=1, source_target_pairs={{0,1},{1,2},{2,3},{3,4},{4,5},{5,6},{6,7},{7,8},{8,9},{9,10},{10,1... | collective-permute-start | bytes 294920 | tf_op jit(solution)/shard_map/ppermute | solution.py:181
  59.6 10.1 %collective-permute-start.1 = (f32[24,1024]{1,0:T(8,128)S(1)}, f32[24,1024]{1,0:T(8,128)S(1)}, u32[]{:S(2)}, u32[]{:S(2)}) collective-permute-start(f32[24,1024]{1,0:T(8,128)S(1)} %copy-done.1), channel_id=1, source_target_pairs={{1,0},{2,1},{3,2},{4,3},{5,4},{6,5},{7,6},{8,7},{9,8},{10,9},{11,1... | collective-permute-start | bytes 294920 | tf_op jit(solution)/shard_map/ppermute | solution.py:182
  67.8 1.8 %copy-start.2 = (f32[24,1024]{1,0:T(8,128)}, f32[24,1024]{1,0:T(8,128)S(1)}, u32[]{:S(2)}) copy-start(f32[24,1024]{1,0:T(8,128)S(1)} %collective-permute-done.left_ref) | copy-start | bytes 294916
  69.7 0.6 copy-start.3
  77.1 0.7 copy-start

commit v2 on v1

v2 whole, which is shorter than its diff:
```python
import math

import jax
import jax.numpy as jnp
from jax import lax
from jax.experimental import pallas as pl
from jax.experimental.pallas import tpu as pltpu
from jax.sharding import Mesh, PartitionSpec as P

f32 = jnp.float32
bf16 = jnp.bfloat16
width_sq = 0.1
gain_factor = 5.0
coord_scale = math.sqrt(math.log2(math.e) / width_sq)
VEC = 16
ROWS = 24
T = 256
LEAVES_DEV = 4
PACK = 40
HALF = 128


def dg(a, b, ca, cb):
    return lax.dot_general(a, b, (((ca,), (cb,)), ((), ())), preferred_element_type=f32)


def split2(v):
    h = v.astype(bf16)
    return h, (v - h.astype(f32)).astype(bf16)


def split3(v):
    a = v.astype(bf16).astype(f32)
    r = v - a
    b = r.astype(bf16).astype(f32)
    return a, b, r - b


def centred(x3):
    x = (x3 - 1.0) * coord_scale
    n = jnp.sum(x * x, axis=0, keepdims=True)
    return x, n, jnp.ones_like(n), jnp.zeros((3,) + n.shape[1:], f32)


def feat_src(x3):
    x, n, o, z = centred(x3)
    a, b, c = split3(jnp.concatenate([x, n, o, z], axis=0))
    return jnp.concatenate([a, a, a, b, b, c], axis=0).astype(bf16)


def feat_tgt(x3):
    x, n, o, z = centred(x3)
    a, b, c = split3(jnp.concatenate([2.0 * x, -o, -n, z], axis=0))
    return jnp.concatenate([a, b, c, a, b, a], axis=0).astype(bf16)


def tile(fs, ft):
    return split2(jnp.exp2(dg(fs, ft, 0, 0)))


def stack2(v):
    h, l = split2(v)
    return jnp.concatenate([h, l], axis=0)


def times(vv, kt):
    kh, kl = kt
    r = dg(vv, kh, 1, 0)
    return r[:VEC] + r[VEC:] + dg(vv[:VEC], kl, 1, 0)


def gain(count):
    return gain_factor / math.sqrt(count)


def pack(w, skel):
    z = jnp.zeros((1, HALF), f32)
    return jnp.concatenate([w[:, :HALF], w[:, HALF:], skel[:, :HALF], z, skel[:, HALF:], z], axis=0)


def unpack(p):
    w = jnp.concatenate([p[:VEC], p[VEC : 2 * VEC]], axis=1)
    skel = jnp.concatenate([p[2 * VEC : 2 * VEC + 3], p[2 * VEC + 4 : 2 * VEC + 7]], axis=1)
    return w, skel


def up_kernel(pts_hbm, chg_hbm, mor_hbm, skl_hbm, skb_hbm, srt_ref, pack_ref, *scratch):
    pts_ref, chg_ref, mor_ref, skl_ref, skb_ref, sems = scratch
    copies = [
        pltpu.make_async_copy(src, dst, sems.at[i])
        for i, (src, dst) in enumerate(
            ((pts_hbm, pts_ref), (chg_hbm, chg_ref), (mor_hbm, mor_ref), (skl_hbm, skl_ref), (skb_hbm, skb_ref))
        )
    ]
    for c in copies:
        c.start()
    for c in copies:
        c.wait()
    n = chg_ref.shape[1]
    rows = jnp.concatenate([chg_ref[...], pts_ref[...], jnp.zeros((5, n), f32)], axis=0)
    a, b, c = split3(rows)
    parts = jnp.concatenate([a, b, c], axis=0).astype(bf16)
    for i in range(n // T):
        col = slice(i * T, (i + 1) * T)
        hot = (lax.broadcasted_iota(jnp.int32, (n, T), 0) == mor_ref[:, col]).astype(f32).astype(bf16)
        s = dg(parts, hot, 1, 0)
        srt_ref[:, col] = s[:ROWS] + s[ROWS : 2 * ROWS] + s[2 * ROWS :]
    srt_ref[VEC + 3 : VEC + 6, :T] = skb_ref[...]
    ft_block = feat_tgt(skb_ref[...])
    total = jnp.zeros((VEC, T), f32)
    for q in range(LEAVES_DEV):
        col = slice(q * T, (q + 1) * T)
        skel = skl_ref[:, col]
        lw = times(stack2(srt_ref[:VEC, col]), tile(feat_src(srt_ref[VEC : VEC + 3, col]), feat_tgt(skel)))
        total = total + times(stack2(gain(T) * lw), tile(feat_src(skel), ft_block))
    packed = pack(gain(LEAVES_DEV * T) * total, skb_ref[...])
    for z in range(pack_ref.shape[0]):
        pack_ref[z] = packed


def group_kernel(id_ref, all_ref, skg_ref, gw_ref):
    n = all_ref.shape[0]
    own = pl.ds(pl.multiple_of(id_ref[0] * T, T), T)
    ft = feat_tgt(skg_ref[:, own])
    total = jnp.zeros((VEC, T), f32)
    for c in range(n):
        w, skel = unpack(all_ref[c])
        total = total + times(stack2(w), tile(feat_src(skel), ft))
    total = gain(2 * n * T) * total
    for g in range(gw_ref.shape[0]):
        gw_ref[g] = total


def near_kernel(id_ref, nbr_ref, cnt_ref, left_ref, mid_ref, right_ref, near_ref):
    first = id_ref[3]
    fts = [feat_tgt(mid_ref[VEC : VEC + 3, q * T : (q + 1) * T]) for q in range(LEAVES_DEV)]
    acc = [jnp.zeros((VEC, T), f32) for _ in range(LEAVES_DEV)]
    for s in range(-LEAVES_DEV, 2 * LEAVES_DEV):
        ref = (left_ref, mid_ref, right_ref)[s // LEAVES_DEV + 1]
        j = s % LEAVES_DEV
        v = ref[:VEC, j * T : (j + 1) * T]
        fs = feat_src(ref[VEC : VEC + 3, j * T : (j + 1) * T])
        for q in range(LEAVES_DEV):
            if abs(s - q) > LEAVES_DEV:
                continue
            uses = jnp.int32(1 if s == q else 0)
            for k in range(nbr_ref.shape[1]):
                hit = jnp.logical_and(nbr_ref[q, k] == first + s, cnt_ref[q] > k)
                uses = uses + hit.astype(jnp.int32)
            acc[q] = acc[q] + times(stack2(uses.astype(f32) * v), tile(fs, fts[q]))
    for q in range(LEAVES_DEV):
        near_ref[:, q * T : (q + 1) * T] = gain(T) * acc[q]


def sibling(core, left_ref, right_ref):
    rows = slice(VEC + 3, VEC + 6)
    return jnp.where(core == 0, right_ref[rows, :T], left_ref[rows, :T])


def peer_kernel(id_ref, all_ref, skb_ref, left_ref, right_ref, peer_ref):
    n = all_ref.shape[0]
    ft_own = feat_tgt(skb_ref[...])
    ft_sib = feat_tgt(sibling(id_ref[2], left_ref, right_ref))
    own = jnp.zeros((VEC, T), f32)
    sib = jnp.zeros((VEC, T), f32)
    for c in range(n):
        w, skel = unpack(all_ref[c])
        fs = feat_src(skel)
        keep = jnp.where(id_ref[1] == c, 0.0, 1.0)
        own = own + times(stack2(keep * w), tile(fs, ft_own))
        sib = sib + times(stack2(w), tile(fs, ft_sib))
    peer_ref[0] = gain((2 * n - 1) * T) * own
    peer_ref[1] = gain((2 * n - 1) * T) * sib


def field_kernel(id_ref, gws_ref, skg_ref, peer_ref, skb_ref, left_ref, right_ref, own_ref, sib_ref):
    group = id_ref[0]
    n = gws_ref.shape[0]
    own = skg_ref[:, pl.ds(pl.multiple_of(group * T, T), T)]
    ft_own = feat_tgt(own)
    total = jnp.zeros((VEC, T), f32)
    for g in range(n):
        keep = jnp.where(group == g, 0.0, 1.0)
        total = total + times(stack2(keep * gws_ref[g]), tile(feat_src(skg_ref[:, g * T : (g + 1) * T]), ft_own))
    vv = stack2(gain((n - 1) * T) * total)
    fs = feat_src(own)
    own_ref[...] = peer_ref[0] + gain(T) * times(vv, tile(fs, feat_tgt(skb_ref[...])))
    sib_ref[...] = peer_ref[1] + gain(T) * times(vv, tile(fs, feat_tgt(sibling(id_ref[2], left_ref, right_ref))))


def down_kernel(id_ref, own_ref, both_ref, skb_ref, skl_ref, mid_ref, near_ref, out_ref):
    field = own_ref[...] + both_ref[1 - id_ref[2]]
    vv = stack2(field)
    fs_block = feat_src(skb_ref[...])
    for q in range(LEAVES_DEV):
        col = slice(q * T, (q + 1) * T)
        lf = gain(T) * times(vv, tile(fs_block, feat_tgt(skl_ref[:, col])))
        far = times(stack2(lf), tile(feat_src(skl_ref[:, col]), feat_tgt(mid_ref[VEC : VEC + 3, col])))
        out_ref[:, col] = near_ref[:, col] + gain(T) * far


VM = pl.BlockSpec(memory_space=pltpu.VMEM)
SM = pl.BlockSpec(memory_space=pltpu.SMEM)


def shape(*dims):
    return jax.ShapeDtypeStruct(dims, f32)


def kernel(fn, name, out, scalars, arrays):
    return pl.pallas_call(
        fn,
        out_shape=out,
        in_specs=[SM] * scalars + [VM] * arrays,
        out_specs=jax.tree.map(lambda _: VM, out),
        compiler_params=pltpu.CompilerParams(vmem_limit_bytes=24 << 20),
        name=name,
    )


def body(points, charges, morton, neighbours, counts, skel_leaf, skel_block, skel_group):
    n_groups = lax.axis_size("grp")
    n_z = lax.axis_size("z")
    n = points.shape[1]
    group_id = lax.axis_index("grp")
    z_id = lax.axis_index("z")
    core_id = lax.axis_index("core")
    block_id = (group_id * n_z + z_id) * 2 + core_id
    ids = jnp.stack([group_id, z_id, core_id, block_id * LEAVES_DEV]).astype(jnp.int32)
    inputs = (points, charges, morton.reshape(1, n), skel_leaf, skel_block)
    srt, packed = pl.pallas_call(
        up_kernel,
        out_shape=(shape(ROWS, n), shape(n_z, PACK, HALF)),
        in_specs=[pl.BlockSpec(memory_space=pltpu.HBM)] * 5,
        out_specs=(VM, VM),
        scratch_shapes=[pltpu.VMEM(x.shape, x.dtype) for x in inputs] + [pltpu.SemaphoreType.DMA((5,))],
        compiler_params=pltpu.CompilerParams(vmem_limit_bytes=60 << 20),
        name="up",
    )(*inputs)
    all_z = lax.all_to_all(packed, "z", 0, 0, tiled=False)
    whole = n_groups * n_z * 2
    axes = ("grp", "z", "core")
    left = lax.ppermute(srt, axes, [(i, i + 1) for i in range(whole - 1)])
    right = lax.ppermute(srt, axes, [(i + 1, i) for i in range(whole - 1)])
    near = kernel(near_kernel, "near", shape(VEC, n), 3, 3)(ids, neighbours, counts, left, srt, right)
    all_z, near = lax.optimization_barrier((all_z, near))
    gw = kernel(group_kernel, "group", shape(n_groups, VEC, T), 1, 2)(ids, all_z, skel_group)
    gws = lax.all_to_all(gw, "grp", 0, 0, tiled=False)
    peer = kernel(peer_kernel, "peer", shape(2, VEC, T), 1, 4)(ids, all_z, skel_block, left, right)
    own, sib = kernel(field_kernel, "field", (shape(VEC, T), shape(VEC, T)), 1, 6)(
        ids, gws, skel_group, peer, skel_block, left, right
    )
    both = lax.all_gather(sib, "core", axis=0, tiled=False)
    return kernel(down_kernel, "down", shape(VEC, n), 1, 6)(ids, own, both, skel_block, skel_leaf, srt, near)


def solution(mesh):
    fine = Mesh(mesh.devices.reshape(mesh.shape["grp"], mesh.shape["dev"] // 2, 2), ("grp", "z", "core"))
    all_axes = ("grp", "z", "core")
    return jax.shard_map(
        body,
        mesh=fine,
        in_specs=(
            P(None, all_axes),
            P(None, all_axes),
            P(all_axes),
            P(all_axes, None),
            P(all_axes),
            P(None, all_axes),
            P(None, all_axes),
            P(),
        ),
        out_specs=P(None, all_axes),
        check_vma=False,
    )
```

time: 82.4 us -> 69.3 us (0.84)
  the two profiles are of different devices: /device:TPU:8 before, /device:TPU:1 now
where the time goes in v2:
time: 69.3 us; the launch traced here: 68.9 us
  starting transfers between devices  29.1 us (42%)
  Pallas kernels  17.7 us (26%)
  waiting for transfers between devices  15.4 us (22%)
  blocking collectives  6.48 us (9%)
    all_to_all x1, starting transfers between devices, body(): all_z = lax.all_to_all(packed, 'z', 0, 0, tiled=False)  15.9 us
    ppermute x1, waiting for transfers between devices, body(): right = lax.ppermute(srt, axes, [(i + 1, i) for i in range(whole - 1)])  10.9 us
    all_to_all x1, starting transfers between devices, body(): gws = lax.all_to_all(gw, 'grp', 0, 0, tiled=False)  6.88 us
    all_gather x1, blocking collectives, body(): both = lax.all_gather(sib, 'core', axis=0, tiled=False)  6.48 us
    all_to_all x1, waiting for transfers between devices, body(): gws = lax.all_to_all(gw, 'grp', 0, 0, tiled=False)  4.47 us
    pallas_call x1, Pallas kernels, body(): pl.pallas_call(up_kernel, out_shape=(shape(ROWS, n), shape(n_z, PACK, HAL...  4.03 us
    ppermute x1, starting transfers between devices, body(): left = lax.ppermute(srt, axes, [(i, i + 1) for i in range(whole - 1)])  3.45 us
    pallas_call x1, Pallas kernels, body(): kernel(near_kernel, 'near', shape(VEC, n), 3, 3)  3.37 us
  transfers between devices with their start and end apart: 4, of which 2 were waited for; matrix products, arithmetic and copies ran while one was open for 0% of the time, Pallas kernels for 9%

profile of v2, /device:TPU:1, one launch (start us, length us, event | category | flops | bytes accessed | tf_op | source)
XLA Modules:
  0.0 68.9 jit_solution(14108863873238261444)
XLA Ops:
  0.0 4.0 %up.1 = (f32[24,1024]{1,0:T(8,128)}, f32[16,40,128]{2,1,0:T(8,128)}) custom-call(f32[3,1024]{1,0:T(4,128)} %pts_hbm.1, f32[16,1024]{1,0:T(8,128)} %chg_hbm.1, s32[1,1024]{1,0:T(1,128)} %bitcast.7, f32[3,1024]{1,0:T(4,128)} %skl_ref.1, f32[3,256]{1,0:T(4,128)} %skb_ref.5), custom_call_target="tpu_custom_call" | custom-call | tf_op jit(solution)/shard_map/up/pallas_call | solution.py:231
  4.0 0.0 copy-start
  4.0 15.9 %all-to-all-start = ((f32[16,40,128]{2,1,0:T(8,128)}), f32[16,40,128]{2,1,0:T(8,128)S(1)}, u32[]{:S(2)}, u32[]{:S(2)}) async-start(f32[16,40,128]{2,1,0:T(8,128)} %get-tuple-element.11), calls=%async_computation | async-start | bytes 655360 | tf_op jit(solution)/shard_map/all_to_all | solution.py:240
  19.9 0.0 copy-done
  20.0 2.9 %collective-permute-start.1 = (f32[24,1024]{1,0:T(8,128)S(1)}, f32[24,1024]{1,0:T(8,128)S(1)}, u32[]{:S(2)}, u32[]{:S(2)}) collective-permute-start(f32[24,1024]{1,0:T(8,128)S(1)} %copy-done), channel_id=1, source_target_pairs={{1,0},{2,1},{3,2},{4,3},{5,4},{6,5},{7,6},{8,7},{9,8},{10,9},{11,1... | collective-permute-start | bytes 294920 | tf_op jit(solution)/shard_map/ppermute | solution.py:244
  22.8 3.4 %collective-permute-start = (f32[24,1024]{1,0:T(8,128)S(1)}, f32[24,1024]{1,0:T(8,128)S(1)}, u32[]{:S(2)}, u32[]{:S(2)}) collective-permute-start(f32[24,1024]{1,0:T(8,128)S(1)} %copy-done), channel_id=1, source_target_pairs={{0,1},{1,2},{2,3},{3,4},{4,5},{5,6},{6,7},{7,8},{8,9},{9,10},{10,1... | collective-permute-start | bytes 294920 | tf_op jit(solution)/shard_map/ppermute | solution.py:243
  26.3 0.0 copy-start.4
  26.3 0.0 copy-start.5
  26.3 0.1 pad_add_fusion.id_ref
  26.4 10.9 %collective-permute-done.1.right_ref = f32[24,1024]{1,0:T(8,128)S(1)} collective-permute-done((f32[24,1024]{1,0:T(8,128)S(1)}, f32[24,1024]{1,0:T(8,128)S(1)}, u32[]{:S(2)}, u32[]{:S(2)}) %collective-permute-start.1) | collective-permute-done | bytes 98336 | tf_op jit(solution)/shard_map/ppermute | solution.py:244
  37.3 0.0 collective-permute-done.left_ref
  37.3 0.0 copy-done.4
  37.3 3.4 %near.1.near_ref = f32[16,1024]{1,0:T(8,128)S(1)} custom-call(s32[4]{0:T(128)S(1)} %pad_add_fusion.id_ref, s32[4,8]{1,0:T(4,128)S(1)} %copy-done.4, s32[4]{0:T(128)S(1)} %copy-done.5, f32[24,1024]{1,0:T(8,128)S(1)} %collective-permute-done.left_ref, f32[24,1024]{1,0:T(8,128)S(1)} %copy-done, f32[24,1024]{1,0:T(8,128)S(1)} %collective-permute-done.1.right_ref), custom_call_target="tpu_custom_call" | custom-call | tf_op jit(solution)/shard_map/near/pallas_call | solution.py:245
  40.7 0.0 all-to-all-done.all_ref
  40.7 0.0 copy-done.1
  40.7 2.7 %group.1 = f32[16,16,256]{2,1,0:T(8,128)} custom-call(s32[4]{0:T(128)S(1)} %pad_add_fusion.id_ref, f32[16,40,128]{2,1,0:T(8,128)S(1)} %all-to-all-done.all_ref, f32[3,4096]{1,0:T(4,128)S(1)} %copy-done.1), custom_call_target="tpu_custom_call" | custom-call | tf_op jit(solution)/shard_map/group/pallas_call | solution.py:247
  43.4 6.9 %all-to-all-start.1 = ((f32[16,16,256]{2,1,0:T(8,128)}), f32[16,16,256]{2,1,0:T(8,128)S(1)}, u32[]{:S(2)}, u32[]{:S(2)}) async-start(f32[16,16,256]{2,1,0:T(8,128)} %group.1), calls=%async_computation.1 | async-start | bytes 524288 | tf_op jit(solution)/shard_map/all_to_all | solution.py:248
  50.3 0.0 copy-done.2
  50.3 3.1 %peer.1.peer_ref = f32[2,16,256]{2,1,0:T(8,128)S(1)} custom-call(s32[4]{0:T(128)S(1)} %pad_add_fusion.id_ref, f32[16,40,128]{2,1,0:T(8,128)S(1)} %all-to-all-done.all_ref, f32[3,256]{1,0:T(4,128)S(1)} %copy-done.2, f32[24,1024]{1,0:T(8,128)S(1)} %collective-permute-done.left_ref, f32[24,1024]{1,0:T(8,128)S(1)} %collective-permute-done.1.right_ref), custom_call_target="tpu_custom_call" | custom-call | tf_op jit(solution)/shard_map/peer/pallas_call | solution.py:249
  53.3 4.5 %all-to-all-done.1.gws_ref = f32[16,16,256]{2,1,0:T(8,128)S(1)} async-done(((f32[16,16,256]{2,1,0:T(8,128)}), f32[16,16,256]{2,1,0:T(8,128)S(1)}, u32[]{:S(2)}, u32[]{:S(2)}) %all-to-all-start.1) | async-done | bytes 262176 | tf_op jit(solution)/shard_map/all_to_all | solution.py:248
  57.8 2.2 %field.1 = (f32[16,256]{1,0:T(8,128)S(1)}, f32[16,256]{1,0:T(8,128)S(1)}) custom-call(s32[4]{0:T(128)S(1)} %pad_add_fusion.id_ref, f32[16,16,256]{2,1,0:T(8,128)S(1)} %all-to-all-done.1.gws_ref, f32[3,4096]{1,0:T(4,128)S(1)} %copy-done.1, f32[2,16,256]{2,1,0:T(8,128)S(1)} %peer.1.peer_ref, f32[3,256]{1,0:T(4,128)S(1)} %copy-done.2, ...), custom_call_target="tpu_custom_call" | custom-call | tf_op jit(solution)/shard_map/field/pallas_call | solution.py:250
  60.0 6.5 %all-gather = f32[32,256]{1,0:T(8,128)S(1)} all-gather(f32[16,256]{1,0:T(8,128)S(1)} %get-tuple-element.15), channel_id=2, replica_groups=mesh['grp'=16,'z'=16,'core'=2] {'core'}, dimensions={0}, use_global_device_ids=true | all-gather | bytes 49152 | tf_op jit(solution)/shard_map/all_gather | solution.py:253
  66.5 0.0 copy-done.3
  66.5 2.4 %down.1 = f32[16,1024]{1,0:T(8,128)} custom-call(s32[4]{0:T(128)S(1)} %pad_add_fusion.id_ref, f32[16,256]{1,0:T(8,128)S(1)} %get-tuple-element.14.own_ref, f32[2,16,256]{2,1,0:T(8,128)S(1)} %bitcast.6, f32[3,256]{1,0:T(4,128)S(1)} %copy-done.2, f32[3,1024]{1,0:T(4,128)S(1)} %copy-done.3, f32[24,1024]{1,0:T(8,128)S(1)} %copy-done, f32[16,1024]{1,0:T(8,128)S(1)} %near.1.near_ref), custom_call_target="tpu_custom_call" | custom-call | tf_op jit(solution)/shard_map/down/pallas_call | solution.py:254
  (4 shorter events, 0.0 us)
Async XLA Ops:
  4.0 15.9 %copy-start = (f32[24,1024]{1,0:T(8,128)S(1)}, f32[24,1024]{1,0:T(8,128)}, u32[]{:S(2)}) copy-start(f32[24,1024]{1,0:T(8,128)} %get-tuple-element.12.mid_ref) | copy-start | bytes 294916
  4.0 36.6 %all-to-all-start = ((f32[16,40,128]{2,1,0:T(8,128)}), f32[16,40,128]{2,1,0:T(8,128)S(1)}, u32[]{:S(2)}, u32[]{:S(2)}) async-start(f32[16,40,128]{2,1,0:T(8,128)} %get-tuple-element.11), calls=%async_computation | async-start | bytes 655360 | tf_op jit(solution)/shard_map/all_to_all | solution.py:240
  20.0 17.3 %collective-permute-start.1 = (f32[24,1024]{1,0:T(8,128)S(1)}, f32[24,1024]{1,0:T(8,128)S(1)}, u32[]{:S(2)}, u32[]{:S(2)}) collective-permute-start(f32[24,1024]{1,0:T(8,128)S(1)} %copy-done), channel_id=1, source_target_pairs={{1,0},{2,1},{3,2},{4,3},{5,4},{6,5},{7,6},{8,7},{9,8},{10,9},{11,1... | collective-permute-start | bytes 294920 | tf_op jit(solution)/shard_map/ppermute | solution.py:244
  22.8 14.5 %collective-permute-start = (f32[24,1024]{1,0:T(8,128)S(1)}, f32[24,1024]{1,0:T(8,128)S(1)}, u32[]{:S(2)}, u32[]{:S(2)}) collective-permute-start(f32[24,1024]{1,0:T(8,128)S(1)} %copy-done), channel_id=1, source_target_pairs={{0,1},{1,2},{2,3},{3,4},{4,5},{5,6},{6,7},{7,8},{8,9},{9,10},{10,1... | collective-permute-start | bytes 294920 | tf_op jit(solution)/shard_map/ppermute | solution.py:243
  26.3 11.0 %copy-start.4 = (s32[4,8]{1,0:T(4,128)S(1)}, s32[4,8]{1,0:T(4,128)}, u32[]{:S(2)}) copy-start(s32[4,8]{1,0:T(4,128)} %nbr_ref.1) | copy-start | bytes 388
  26.3 11.0 %copy-start.5 = (s32[4]{0:T(128)S(1)}, s32[4]{0:T(128)}, u32[]{:S(2)}) copy-start(s32[4]{0:T(128)} %cnt_ref.1) | copy-start | bytes 52
  26.4 14.3 %copy-start.1 = (f32[3,4096]{1,0:T(4,128)S(1)}, f32[3,4096]{1,0:T(4,128)}, u32[]{:S(2)}) copy-start(f32[3,4096]{1,0:T(4,128)} %skg_ref.3) | copy-start | bytes 147460
  43.4 6.9 %copy-start.2 = (f32[3,256]{1,0:T(4,128)S(1)}, f32[3,256]{1,0:T(4,128)}, u32[]{:S(2)}) copy-start(f32[3,256]{1,0:T(4,128)} %skb_ref.5) | copy-start | bytes 9220
  43.4 14.4 %all-to-all-start.1 = ((f32[16,16,256]{2,1,0:T(8,128)}), f32[16,16,256]{2,1,0:T(8,128)S(1)}, u32[]{:S(2)}, u32[]{:S(2)}) async-start(f32[16,16,256]{2,1,0:T(8,128)} %group.1), calls=%async_computation.1 | async-start | bytes 524288 | tf_op jit(solution)/shard_map/all_to_all | solution.py:248
  60.0 6.5 %copy-start.3 = (f32[3,1024]{1,0:T(4,128)S(1)}, f32[3,1024]{1,0:T(4,128)}, u32[]{:S(2)}) copy-start(f32[3,1024]{1,0:T(4,128)} %skl_ref.1) | copy-start | bytes 36868

commit v3 on v2

--- a/solution.py
+++ b/solution.py
@@ -118,17 +118,38 @@
         pack_ref[z] = packed
 
 
-def group_kernel(id_ref, all_ref, skg_ref, gw_ref):
-    n = all_ref.shape[0]
-    own = pl.ds(pl.multiple_of(id_ref[0] * T, T), T)
-    ft = feat_tgt(skg_ref[:, own])
+def own_group(id_ref, skg_ref):
+    return skg_ref[:, pl.ds(pl.multiple_of(id_ref[0] * T, T), T)]
+
+
+def raised(id_ref, packs_ref, skg_ref):
+    ft = feat_tgt(own_group(id_ref, skg_ref))
     total = jnp.zeros((VEC, T), f32)
-    for c in range(n):
-        w, skel = unpack(all_ref[c])
+    for c in range(packs_ref.shape[0]):
+        w, skel = unpack(packs_ref[c])
         total = total + times(stack2(w), tile(feat_src(skel), ft))
-    total = gain(2 * n * T) * total
+    return total
+
+
+def half_kernel(id_ref, part_ref, skg_ref, half_ref):
+    half_ref[...] = raised(id_ref, part_ref, skg_ref)
+
+
+def group_kernel(id_ref, part_ref, skg_ref, half_ref, gw_ref):
+    total = half_ref[...] + raised(id_ref, part_ref, skg_ref)
+    total = gain(4 * part_ref.shape[0] * T) * total
     for g in range(gw_ref.shape[0]):
         gw_ref[g] = total
+
+
+def pre_kernel(skb_ref, skl_ref, mid_ref, mh_ref, ml_ref):
+    fs_block = feat_src(skb_ref[...])
+    for q in range(LEAVES_DEV):
+        col = slice(q * T, (q + 1) * T)
+        ah, al = tile(fs_block, feat_tgt(skl_ref[:, col]))
+        bh, bl = tile(feat_src(skl_ref[:, col]), feat_tgt(mid_ref[VEC : VEC + 3, col]))
+        both = dg(ah, bh, 1, 0) + dg(al, bh, 1, 0) + dg(ah, bl, 1, 0)
+        mh_ref[:, col], ml_ref[:, col] = split2(gain(T) * gain(T) * both)
 
 
 def near_kernel(id_ref, nbr_ref, cnt_ref, left_ref, mid_ref, right_ref, near_ref):
@@ -157,54 +178,54 @@
     return jnp.where(core == 0, right_ref[rows, :T], left_ref[rows, :T])
 
 
-def peer_kernel(id_ref, all_ref, skb_ref, left_ref, right_ref, peer_ref):
-    n = all_ref.shape[0]
+def peer_kernel(id_ref, part_ref, other_ref, skb_ref, left_ref, right_ref, skg_ref, peer_ref, bh_ref, bl_ref):
+    n = part_ref.shape[0]
     ft_own = feat_tgt(skb_ref[...])
     ft_sib = feat_tgt(sibling(id_ref[2], left_ref, right_ref))
     own = jnp.zeros((VEC, T), f32)
     sib = jnp.zeros((VEC, T), f32)
-    for c in range(n):
-        w, skel = unpack(all_ref[c])
+    for c in range(2 * n):
+        w, skel = unpack((part_ref if c < n else other_ref)[c % n])
         fs = feat_src(skel)
-        keep = jnp.where(id_ref[1] == c, 0.0, 1.0)
-        own = own + times(stack2(keep * w), tile(fs, ft_own))
-        sib = sib + times(stack2(w), tile(fs, ft_sib))
-    peer_ref[0] = gain((2 * n - 1) * T) * own
-    peer_ref[1] = gain((2 * n - 1) * T) * sib
-
-
-def field_kernel(id_ref, gws_ref, skg_ref, peer_ref, skb_ref, left_ref, right_ref, own_ref, sib_ref):
-    group = id_ref[0]
+        if c < n:
+            vv = stack2(jnp.where(id_ref[1] == c, 0.0, 1.0) * w)
+            own = own + times(vv, tile(fs, ft_own))
+            sib = sib + times(stack2(w), tile(fs, ft_sib))
+        else:
+            vv = stack2(w)
+            own = own + times(vv, tile(fs, ft_own))
+            sib = sib + times(vv, tile(fs, ft_sib))
+    peer_ref[0] = gain((4 * n - 1) * T) * own
+    peer_ref[1] = gain((4 * n - 1) * T) * sib
+    fs = feat_src(own_group(id_ref, skg_ref))
+    bh_ref[:, :T], bl_ref[:, :T] = tile(fs, ft_own)
+    bh_ref[:, T:], bl_ref[:, T:] = tile(fs, ft_sib)
+
+
+def field_kernel(id_ref, gws_ref, skg_ref, bh_ref, bl_ref, peer_ref, own_ref, sib_ref):
     n = gws_ref.shape[0]
-    own = skg_ref[:, pl.ds(pl.multiple_of(group * T, T), T)]
-    ft_own = feat_tgt(own)
+    ft_own = feat_tgt(own_group(id_ref, skg_ref))
     total = jnp.zeros((VEC, T), f32)
     for g in range(n):
-        keep = jnp.where(group == g, 0.0, 1.0)
-        total = total + times(stack2(keep * gws_ref[g]), tile(feat_src(skg_ref[:, g * T : (g + 1) * T]), ft_own))
-    vv = stack2(gain((n - 1) * T) * total)
-    fs = feat_src(own)
-    own_ref[...] = peer_ref[0] + gain(T) * times(vv, tile(fs, feat_tgt(skb_ref[...])))
-    sib_ref[...] = peer_ref[1] + gain(T) * times(vv, tile(fs, feat_tgt(sibling(id_ref[2], left_ref, right_ref))))
-
-
-def down_kernel(id_ref, own_ref, both_ref, skb_ref, skl_ref, mid_ref, near_ref, out_ref):
+        keep = jnp.where(id_ref[0] == g, 0.0, 1.0)
+        col = slice(g * T, (g + 1) * T)
+        total = total + times(stack2(keep * gws_ref[g]), tile(feat_src(skg_ref[:, col]), ft_own))
+    lowered = gain(T) * times(stack2(gain((n - 1) * T) * total), (bh_ref[...], bl_ref[...]))
+    own_ref[...] = peer_ref[0] + lowered[:, :T]
+    sib_ref[...] = peer_ref[1] + lowered[:, T:]
+
+
+def down_kernel(id_ref, own_ref, both_ref, mh_ref, ml_ref, near_ref, out_ref):
     field = own_ref[...] + both_ref[1 - id_ref[2]]
-    vv = stack2(field)
-    fs_block = feat_src(skb_ref[...])
-    for q in range(LEAVES_DEV):
-        col = slice(q * T, (q + 1) * T)
-        lf = gain(T) * times(vv, tile(fs_block, feat_tgt(skl_ref[:, col])))
-        far = times(stack2(lf), tile(feat_src(skl_ref[:, col]), feat_tgt(mid_ref[VEC : VEC + 3, col])))
-        out_ref[:, col] = near_ref[:, col] + gain(T) * far
+    out_ref[...] = near_ref[...] + times(stack2(field), (mh_ref[...], ml_ref[...]))
 
 
 VM = pl.BlockSpec(memory_space=pltpu.VMEM)
 SM = pl.BlockSpec(memory_space=pltpu.SMEM)
 
 
-def shape(*dims):
-    return jax.ShapeDtypeStruct(dims, f32)
+def shape(*dims, dtype=f32):
+    return jax.ShapeDtypeStruct(dims, dtype)
 
 
 def kernel(fn, name, out, scalars, arrays):
@@ -220,43 +241,47 @@
 
 def body(points, charges, morton, neighbours, counts, skel_leaf, skel_block, skel_group):
     n_groups = lax.axis_size("grp")
-    n_z = lax.axis_size("z")
+    n_z8 = lax.axis_size("z8")
     n = points.shape[1]
+    axes = ("grp", "z8", "zp", "core")
     group_id = lax.axis_index("grp")
-    z_id = lax.axis_index("z")
+    z8_id = lax.axis_index("z8")
     core_id = lax.axis_index("core")
-    block_id = (group_id * n_z + z_id) * 2 + core_id
-    ids = jnp.stack([group_id, z_id, core_id, block_id * LEAVES_DEV]).astype(jnp.int32)
+    block_id = ((group_id * n_z8 + z8_id) * 2 + lax.axis_index("zp")) * 2 + core_id
+    ids = jnp.stack([group_id, z8_id, core_id, block_id * LEAVES_DEV]).astype(jnp.int32)
     inputs = (points, charges, morton.reshape(1, n), skel_leaf, skel_block)
     srt, packed = pl.pallas_call(
         up_kernel,
-        out_shape=(shape(ROWS, n), shape(n_z, PACK, HALF)),
+        out_shape=(shape(ROWS, n), shape(n_z8, PACK, HALF)),
         in_specs=[pl.BlockSpec(memory_space=pltpu.HBM)] * 5,
         out_specs=(VM, VM),
         scratch_shapes=[pltpu.VMEM(x.shape, x.dtype) for x in inputs] + [pltpu.SemaphoreType.DMA((5,))],
         compiler_params=pltpu.CompilerParams(vmem_limit_bytes=60 << 20),
         name="up",
     )(*inputs)
-    all_z = lax.all_to_all(packed, "z", 0, 0, tiled=False)
-    whole = n_groups * n_z * 2
-    axes = ("grp", "z", "core")
+    part = lax.all_to_all(packed, "z8", 0, 0, tiled=False)
+    whole = n_groups * n_z8 * 4
     left = lax.ppermute(srt, axes, [(i, i + 1) for i in range(whole - 1)])
     right = lax.ppermute(srt, axes, [(i + 1, i) for i in range(whole - 1)])
+    half_shape = shape(T, n, dtype=bf16)
+    mh, ml = kernel(pre_kernel, "pre", (half_shape, half_shape), 0, 3)(skel_block, skel_leaf, srt)
     near = kernel(near_kernel, "near", shape(VEC, n), 3, 3)(ids, neighbours, counts, left, srt, right)
-    all_z, near = lax.optimization_barrier((all_z, near))
-    gw = kernel(group_kernel, "group", shape(n_groups, VEC, T), 1, 2)(ids, all_z, skel_group)
+    part, near, mh, ml = lax.optimization_barrier((part, near, mh, ml))
+    other = lax.ppermute(part, "zp", [(0, 1), (1, 0)])
+    half = kernel(half_kernel, "half", shape(VEC, T), 1, 2)(ids, part, skel_group)
+    gw = kernel(group_kernel, "group", shape(n_groups, VEC, T), 1, 3)(ids, other, skel_group, half)
     gws = lax.all_to_all(gw, "grp", 0, 0, tiled=False)
-    peer = kernel(peer_kernel, "peer", shape(2, VEC, T), 1, 4)(ids, all_z, skel_block, left, right)
-    own, sib = kernel(field_kernel, "field", (shape(VEC, T), shape(VEC, T)), 1, 6)(
-        ids, gws, skel_group, peer, skel_block, left, right
-    )
+    peer, bh, bl = kernel(
+        peer_kernel, "peer", (shape(2, VEC, T), shape(T, 2 * T, dtype=bf16), shape(T, 2 * T, dtype=bf16)), 1, 6
+    )(ids, part, other, skel_block, left, right, skel_group)
+    own, sib = kernel(field_kernel, "field", (shape(VEC, T), shape(VEC, T)), 1, 5)(ids, gws, skel_group, bh, bl, peer)
     both = lax.all_gather(sib, "core", axis=0, tiled=False)
-    return kernel(down_kernel, "down", shape(VEC, n), 1, 6)(ids, own, both, skel_block, skel_leaf, srt, near)
+    return kernel(down_kernel, "down", shape(VEC, n), 1, 5)(ids, own, both, mh, ml, near)
 
 
 def solution(mesh):
-    fine = Mesh(mesh.devices.reshape(mesh.shape["grp"], mesh.shape["dev"] // 2, 2), ("grp", "z", "core"))
-    all_axes = ("grp", "z", "core")
+    fine = Mesh(mesh.devices.reshape(mesh.shape["grp"], mesh.shape["dev"] // 4, 2, 2), ("grp", "z8", "zp", "core"))
+    all_axes = ("grp", "z8", "zp", "core")
     return jax.shard_map(
         body,
         mesh=fine,

time: 69.3 us -> 70.1 us (1.012)
  waiting for transfers between devices: 15.4 us -> 9.37 us
  starting transfers between devices: 29.1 us -> 32.2 us
  Pallas kernels: 17.7 us -> 19.6 us
  blocking collectives: 6.48 us -> 8.25 us
    ppermute x1, waiting for transfers between devices: 10.9 us -> 1.52 us  [body(): right = lax.ppermute(srt, axes, [(i + 1, i) for i in range(whole - 1)])]
    ppermute x0 -> x1, starting transfers between devices: none -> 4.25 us  [body(): other = lax.ppermute(part, 'zp', [(0, 1), (1, 0)])]
    ppermute x1, waiting for transfers between devices: 0.01 us -> 2.2 us  [body(): left = lax.ppermute(srt, axes, [(i, i + 1) for i in range(whole - 1)])]
    pallas_call x5 -> x7, Pallas kernels: 14.4 us -> 16.2 us  [the longest x1 3.98 us: body(): pl.pallas_call(up_kernel, out_shape=(shape(ROWS, n), shape(n_z8, PACK, HA...]
    all_gather x1, blocking collectives: 6.48 us -> 8.25 us  [body(): both = lax.all_gather(sib, 'core', axis=0, tiled=False)]
    ppermute x0 -> x1, waiting for transfers between devices: none -> 1.27 us  [body(): other = lax.ppermute(part, 'zp', [(0, 1), (1, 0)])]
    ppermute x1, starting transfers between devices: 2.86 us -> 1.92 us  [body(): right = lax.ppermute(srt, axes, [(i + 1, i) for i in range(whole - 1)])]
  transfers between devices with their start and end apart: 4 -> 5, of which waited for: 2 -> 4; matrix products, arithmetic and copies ran while one was open for 0% -> 0% of each run, Pallas kernels for 9% -> 13%
where the time goes in v3:
time: 70.1 us; the launch traced here: 69.7 us
  starting transfers between devices  32.2 us (46%)
  Pallas kernels  19.6 us (28%)
  waiting for transfers between devices  9.37 us (13%)
  blocking collectives  8.25 us (12%)
    all_to_all x1, starting transfers between devices, body(): part = lax.all_to_all(packed, 'z8', 0, 0, tiled=False)  15.8 us
    all_gather x1, blocking collectives, body(): both = lax.all_gather(sib, 'core', axis=0, tiled=False)  8.25 us
    all_to_all x1, starting transfers between devices, body(): gws = lax.all_to_all(gw, 'grp', 0, 0, tiled=False)  6.76 us
    all_to_all x1, waiting for transfers between devices, body(): gws = lax.all_to_all(gw, 'grp', 0, 0, tiled=False)  4.38 us
    ppermute x1, starting transfers between devices, body(): other = lax.ppermute(part, 'zp', [(0, 1), (1, 0)])  4.25 us
    pallas_call x1, Pallas kernels, body(): pl.pallas_call(up_kernel, out_shape=(shape(ROWS, n), shape(n_z8, PACK, HA...  3.98 us
    ppermute x1, starting transfers between devices, body(): left = lax.ppermute(srt, axes, [(i, i + 1) for i in range(whole - 1)])  3.48 us
    pallas_call x1, Pallas kernels, body(): kernel(near_kernel, 'near', shape(VEC, n), 3, 3)  3.37 us
  transfers between devices with their start and end apart: 5, of which 4 were waited for; matrix products, arithmetic and copies ran while one was open for 0% of the time, Pallas kernels for 13%

profile of v3, /device:TPU:1, one launch (start us, length us, event | category | flops | bytes accessed | tf_op | source)
XLA Modules:
  0.0 69.7 jit_solution(5001620024706768173)
XLA Ops:
  0.0 4.0 %up.1 = (f32[24,1024]{1,0:T(8,128)}, f32[8,40,128]{2,1,0:T(8,128)}) custom-call(f32[3,1024]{1,0:T(4,128)} %pts_hbm.1, f32[16,1024]{1,0:T(8,128)} %chg_hbm.1, s32[1,1024]{1,0:T(1,128)} %bitcast.7, f32[3,1024]{1,0:T(4,128)} %skl_ref.1, f32[3,256]{1,0:T(4,128)} %skb_ref.3), custom_call_target="tpu_custom_call" | custom-call | tf_op jit(solution)/shard_map/up/pallas_call | solution.py:253
  4.0 0.0 copy-start.1
  4.0 0.0 copy-start.2
  4.0 15.8 %all-to-all-start = ((f32[8,40,128]{2,1,0:T(8,128)}), f32[8,40,128]{2,1,0:T(8,128)S(1)}, u32[]{:S(2)}, u32[]{:S(2)}) async-start(f32[8,40,128]{2,1,0:T(8,128)} %get-tuple-element.18), calls=%async_computation | async-start | bytes 327680 | tf_op jit(solution)/shard_map/all_to_all | solution.py:262
  19.8 3.5 %collective-permute-start = (f32[24,1024]{1,0:T(8,128)S(1)}, f32[24,1024]{1,0:T(8,128)S(1)}, u32[]{:S(2)}, u32[]{:S(2)}) collective-permute-start(f32[24,1024]{1,0:T(8,128)S(1)} %copy-done.1), channel_id=1, source_target_pairs={{0,1},{1,2},{2,3},{3,4},{4,5},{5,6},{6,7},{7,8},{8,9},{9,10},{10,1... | collective-permute-start | bytes 294920 | tf_op jit(solution)/shard_map/ppermute | solution.py:264
  23.3 1.9 %collective-permute-start.1 = (f32[24,1024]{1,0:T(8,128)S(1)}, f32[24,1024]{1,0:T(8,128)S(1)}, u32[]{:S(2)}, u32[]{:S(2)}) collective-permute-start(f32[24,1024]{1,0:T(8,128)S(1)} %copy-done.1), channel_id=1, source_target_pairs={{1,0},{2,1},{3,2},{4,3},{5,4},{6,5},{7,6},{8,7},{9,8},{10,9},{11,1... | collective-permute-start | bytes 294920 | tf_op jit(solution)/shard_map/ppermute | solution.py:265
  25.3 1.2 %pre.1 = (bf16[256,1024]{1,0:T(8,128)(2,1)S(1)}, bf16[256,1024]{1,0:T(8,128)(2,1)S(1)}) custom-call(f32[3,256]{1,0:T(4,128)S(1)} %copy-done.3, f32[3,1024]{1,0:T(4,128)S(1)} %copy-done.2, f32[24,1024]{1,0:T(8,128)S(1)} %copy-done.1), custom_call_target="tpu_custom_call" | custom-call | tf_op jit(solution)/shard_map/pre/pallas_call | solution.py:267
  26.5 0.0 copy-start.4
  26.5 0.0 copy-start.5
  26.5 0.1 pad_add_fusion.id_ref
  26.6 2.2 %collective-permute-done.left_ref = f32[24,1024]{1,0:T(8,128)S(1)} collective-permute-done((f32[24,1024]{1,0:T(8,128)S(1)}, f32[24,1024]{1,0:T(8,128)S(1)}, u32[]{:S(2)}, u32[]{:S(2)}) %collective-permute-start) | collective-permute-done | bytes 98336 | tf_op jit(solution)/shard_map/ppermute | solution.py:264
  28.8 1.5 %collective-permute-done.1.right_ref = f32[24,1024]{1,0:T(8,128)S(1)} collective-permute-done((f32[24,1024]{1,0:T(8,128)S(1)}, f32[24,1024]{1,0:T(8,128)S(1)}, u32[]{:S(2)}, u32[]{:S(2)}) %collective-permute-start.1) | collective-permute-done | bytes 98336 | tf_op jit(solution)/shard_map/ppermute | solution.py:265
  30.3 3.4 %near.1.near_ref = f32[16,1024]{1,0:T(8,128)S(1)} custom-call(s32[4]{0:T(128)S(1)} %pad_add_fusion.id_ref, s32[4,8]{1,0:T(4,128)S(1)} %copy-done.4, s32[4]{0:T(128)S(1)} %copy-done.5, f32[24,1024]{1,0:T(8,128)S(1)} %collective-permute-done.left_ref, f32[24,1024]{1,0:T(8,128)S(1)} %copy-done.1, f32[24,1024]{1,0:T(8,128)S(1)} %collective-permute-done.1.right_ref), custom_call_target="tpu_custom_call" | custom-call | tf_op jit(solution)/shard_map/near/pallas_call | solution.py:268
  33.7 0.0 all-to-all-done.part_ref
  33.7 4.3 %collective-permute-start.2 = (f32[8,40,128]{2,1,0:T(8,128)S(1)}, f32[8,40,128]{2,1,0:T(8,128)S(1)}, u32[]{:S(2)}, u32[]{:S(2)}) collective-permute-start(f32[8,40,128]{2,1,0:T(8,128)S(1)} %all-to-all-done.part_ref), channel_id=1, source_target_pairs={{0,2},{2,0},{1,3},{3,1},{4,6},{6,4},{5,7},{7,5},{8,10},{10,8},{9,1... | collective-permute-start | bytes 491528 | tf_op jit(solution)/shard_map/ppermute | solution.py:270
  38.0 1.4 %half.1.half_ref = f32[16,256]{1,0:T(8,128)S(1)} custom-call(s32[4]{0:T(128)S(1)} %pad_add_fusion.id_ref, f32[8,40,128]{2,1,0:T(8,128)S(1)} %all-to-all-done.part_ref, f32[3,4096]{1,0:T(4,128)S(1)} %copy-done), custom_call_target="tpu_custom_call" | custom-call | tf_op jit(solution)/shard_map/half/pallas_call | solution.py:271
  39.4 1.3 %collective-permute-done.2.part_ref.other_ref = f32[8,40,128]{2,1,0:T(8,128)S(1)} collective-permute-done((f32[8,40,128]{2,1,0:T(8,128)S(1)}, f32[8,40,128]{2,1,0:T(8,128)S(1)}, u32[]{:S(2)}, u32[]{:S(2)}) %collective-permute-start.2) | collective-permute-done | bytes 163872 | tf_op jit(solution)/shard_map/ppermute | solution.py:270
  40.6 2.1 %group.1 = f32[16,16,256]{2,1,0:T(8,128)} custom-call(s32[4]{0:T(128)S(1)} %pad_add_fusion.id_ref, f32[8,40,128]{2,1,0:T(8,128)S(1)} %collective-permute-done.2.part_ref.other_ref, f32[3,4096]{1,0:T(4,128)S(1)} %copy-done, f32[16,256]{1,0:T(8,128)S(1)} %half.1.half_ref), custom_call_target="tpu_custom_call" | custom-call | tf_op jit(solution)/shard_map/group/pallas_call | solution.py:272
  42.8 6.8 %all-to-all-start.1 = ((f32[16,16,256]{2,1,0:T(8,128)}), f32[16,16,256]{2,1,0:T(8,128)S(1)}, u32[]{:S(2)}, u32[]{:S(2)}) async-start(f32[16,16,256]{2,1,0:T(8,128)} %group.1), calls=%async_computation.1 | async-start | bytes 524288 | tf_op jit(solution)/shard_map/all_to_all | solution.py:273
  49.6 3.2 %peer.1 = (f32[2,16,256]{2,1,0:T(8,128)S(1)}, bf16[256,512]{1,0:T(8,128)(2,1)S(1)}, bf16[256,512]{1,0:T(8,128)(2,1)S(1)}) custom-call(s32[4]{0:T(128)S(1)} %pad_add_fusion.id_ref, f32[8,40,128]{2,1,0:T(8,128)S(1)} %all-to-all-done.part_ref, f32[8,40,128]{2,1,0:T(8,128)S(1)} %collective-permute-done.2.part_ref.other_ref, f32[3,256]{1,0:T(4,128)S(1)} %copy-done.3, ...), custom_call_target="tpu_custom_call" | custom-call | tf_op jit(solution)/shard_map/peer/pallas_call | solution.py:274
  52.7 4.4 %all-to-all-done.1.gws_ref = f32[16,16,256]{2,1,0:T(8,128)S(1)} async-done(((f32[16,16,256]{2,1,0:T(8,128)}), f32[16,16,256]{2,1,0:T(8,128)S(1)}, u32[]{:S(2)}, u32[]{:S(2)}) %all-to-all-start.1) | async-done | bytes 262176 | tf_op jit(solution)/shard_map/all_to_all | solution.py:273
  57.1 2.9 %field.1 = (f32[16,256]{1,0:T(8,128)S(1)}, f32[16,256]{1,0:T(8,128)S(1)}) custom-call(s32[4]{0:T(128)S(1)} %pad_add_fusion.id_ref, f32[16,16,256]{2,1,0:T(8,128)S(1)} %all-to-all-done.1.gws_ref, f32[3,4096]{1,0:T(4,128)S(1)} %copy-done, bf16[256,512]{1,0:T(8,128)(2,1)S(1)} %get-tuple-element.23.bh_ref, bf16[256,512]{1,0:T(8,128)(2,1)S(1)} %get-tuple-element.24.bl_ref, ...), custom_call_target="tpu_custom_call" | custom-call | tf_op jit(solution)/shard_map/field/pallas_call | solution.py:277
  60.0 8.3 %all-gather = f32[32,256]{1,0:T(8,128)S(1)} all-gather(f32[16,256]{1,0:T(8,128)S(1)} %get-tuple-element.27), channel_id=2, replica_groups=mesh['grp'=16,'z8'=8,'zp'=2,'core'=2] {'core'}, dimensions={0}, use_global_device_ids=true | all-gather | bytes 49152 | tf_op jit(solution)/shard_map/all_gather | solution.py:278
  68.3 1.4 %down.1 = f32[16,1024]{1,0:T(8,128)} custom-call(s32[4]{0:T(128)S(1)} %pad_add_fusion.id_ref, f32[16,256]{1,0:T(8,128)S(1)} %get-tuple-element.26.own_ref, f32[2,16,256]{2,1,0:T(8,128)S(1)} %bitcast.6, bf16[256,1024]{1,0:T(8,128)(2,1)S(1)} %get-tuple-element.28.mh_ref, bf16[256,1024]{1,0:T(8,128)(2,1)S(1)} %get-tuple-element.29.ml_ref, ...), custom_call_target="tpu_custom_call" | custom-call | tf_op jit(solution)/shard_map/down/pallas_call | solution.py:279
  (8 shorter events, 0.0 us)
Async XLA Ops:
  4.0 15.8 %copy-start.1 = (f32[24,1024]{1,0:T(8,128)S(1)}, f32[24,1024]{1,0:T(8,128)}, u32[]{:S(2)}) copy-start(f32[24,1024]{1,0:T(8,128)} %get-tuple-element.19.mid_ref) | copy-start | bytes 294916
  4.0 21.2 %copy-start.2 = (f32[3,1024]{1,0:T(4,128)S(1)}, f32[3,1024]{1,0:T(4,128)}, u32[]{:S(2)}) copy-start(f32[3,1024]{1,0:T(4,128)} %skl_ref.1) | copy-start | bytes 36868
  4.0 29.7 %all-to-all-start = ((f32[8,40,128]{2,1,0:T(8,128)}), f32[8,40,128]{2,1,0:T(8,128)S(1)}, u32[]{:S(2)}, u32[]{:S(2)}) async-start(f32[8,40,128]{2,1,0:T(8,128)} %get-tuple-element.18), calls=%async_computation | async-start | bytes 327680 | tf_op jit(solution)/shard_map/all_to_all | solution.py:262
  19.8 5.5 %copy-start.3 = (f32[3,256]{1,0:T(4,128)S(1)}, f32[3,256]{1,0:T(4,128)}, u32[]{:S(2)}) copy-start(f32[3,256]{1,0:T(4,128)} %skb_ref.3) | copy-start | bytes 9220
  19.8 9.0 %collective-permute-start = (f32[24,1024]{1,0:T(8,128)S(1)}, f32[24,1024]{1,0:T(8,128)S(1)}, u32[]{:S(2)}, u32[]{:S(2)}) collective-permute-start(f32[24,1024]{1,0:T(8,128)S(1)} %copy-done.1), channel_id=1, source_target_pairs={{0,1},{1,2},{2,3},{3,4},{4,5},{5,6},{6,7},{7,8},{8,9},{9,10},{10,1... | collective-permute-start | bytes 294920 | tf_op jit(solution)/shard_map/ppermute | solution.py:264
  23.3 7.0 %collective-permute-start.1 = (f32[24,1024]{1,0:T(8,128)S(1)}, f32[24,1024]{1,0:T(8,128)S(1)}, u32[]{:S(2)}, u32[]{:S(2)}) collective-permute-start(f32[24,1024]{1,0:T(8,128)S(1)} %copy-done.1), channel_id=1, source_target_pairs={{1,0},{2,1},{3,2},{4,3},{5,4},{6,5},{7,6},{8,7},{9,8},{10,9},{11,1... | collective-permute-start | bytes 294920 | tf_op jit(solution)/shard_map/ppermute | solution.py:265
  26.5 3.8 %copy-start.4 = (s32[4,8]{1,0:T(4,128)S(1)}, s32[4,8]{1,0:T(4,128)}, u32[]{:S(2)}) copy-start(s32[4,8]{1,0:T(4,128)} %nbr_ref.1) | copy-start | bytes 388
  26.5 3.8 %copy-start.5 = (s32[4]{0:T(128)S(1)}, s32[4]{0:T(128)}, u32[]{:S(2)}) copy-start(s32[4]{0:T(128)} %cnt_ref.1) | copy-start | bytes 52
  26.6 11.4 %copy-start = (f32[3,4096]{1,0:T(4,128)S(1)}, f32[3,4096]{1,0:T(4,128)}, u32[]{:S(2)}) copy-start(f32[3,4096]{1,0:T(4,128)} %skg_ref.7) | copy-start | bytes 147460
  33.7 7.0 %collective-permute-start.2 = (f32[8,40,128]{2,1,0:T(8,128)S(1)}, f32[8,40,128]{2,1,0:T(8,128)S(1)}, u32[]{:S(2)}, u32[]{:S(2)}) collective-permute-start(f32[8,40,128]{2,1,0:T(8,128)S(1)} %all-to-all-done.part_ref), channel_id=1, source_target_pairs={{0,2},{2,0},{1,3},{3,1},{4,6},{6,4},{5,7},{7,5},{8,10},{10,8},{9,1... | collective-permute-start | bytes 491528 | tf_op jit(solution)/shard_map/ppermute | solution.py:270
  42.8 14.3 %all-to-all-start.1 = ((f32[16,16,256]{2,1,0:T(8,128)}), f32[16,16,256]{2,1,0:T(8,128)S(1)}, u32[]{:S(2)}, u32[]{:S(2)}) async-start(f32[16,16,256]{2,1,0:T(8,128)} %group.1), calls=%async_computation.1 | async-start | bytes 524288 | tf_op jit(solution)/shard_map/all_to_all | solution.py:273

commit v4 on v3

--- a/solution.py
+++ b/solution.py
@@ -131,13 +131,8 @@
     return total
 
 
-def half_kernel(id_ref, part_ref, skg_ref, half_ref):
-    half_ref[...] = raised(id_ref, part_ref, skg_ref)
-
-
-def group_kernel(id_ref, part_ref, skg_ref, half_ref, gw_ref):
-    total = half_ref[...] + raised(id_ref, part_ref, skg_ref)
-    total = gain(4 * part_ref.shape[0] * T) * total
+def group_kernel(id_ref, part_ref, skg_ref, gw_ref):
+    total = gain(4 * part_ref.shape[0] * T) * raised(id_ref, part_ref, skg_ref)
     for g in range(gw_ref.shape[0]):
         gw_ref[g] = total
 
@@ -152,8 +147,11 @@
         mh_ref[:, col], ml_ref[:, col] = split2(gain(T) * gain(T) * both)
 
 
-def near_kernel(id_ref, nbr_ref, cnt_ref, left_ref, mid_ref, right_ref, near_ref):
+def near_kernel(id_ref, nbr_ref, cnt_ref, sib_ref, adj_ref, mid_ref, near_ref, left_ref, right_ref):
     first = id_ref[3]
+    on_left = id_ref[2] == 1
+    left_ref[...] = jnp.where(on_left, sib_ref[...], adj_ref[...])
+    right_ref[...] = jnp.where(on_left, adj_ref[...], sib_ref[...])
     fts = [feat_tgt(mid_ref[VEC : VEC + 3, q * T : (q + 1) * T]) for q in range(LEAVES_DEV)]
     acc = [jnp.zeros((VEC, T), f32) for _ in range(LEAVES_DEV)]
     for s in range(-LEAVES_DEV, 2 * LEAVES_DEV):
@@ -173,36 +171,28 @@
         near_ref[:, q * T : (q + 1) * T] = gain(T) * acc[q]
 
 
-def sibling(core, left_ref, right_ref):
-    rows = slice(VEC + 3, VEC + 6)
-    return jnp.where(core == 0, right_ref[rows, :T], left_ref[rows, :T])
-
-
-def peer_kernel(id_ref, part_ref, other_ref, skb_ref, left_ref, right_ref, skg_ref, peer_ref, bh_ref, bl_ref):
+def peer_kernel(id_ref, part_ref, other_ref, skb_ref, sibling_ref, skg_ref, peer_ref, bh_ref, bl_ref):
     n = part_ref.shape[0]
     ft_own = feat_tgt(skb_ref[...])
-    ft_sib = feat_tgt(sibling(id_ref[2], left_ref, right_ref))
+    ft_sib = feat_tgt(sibling_ref[VEC + 3 : VEC + 6, :T])
     own = jnp.zeros((VEC, T), f32)
     sib = jnp.zeros((VEC, T), f32)
     for c in range(2 * n):
         w, skel = unpack((part_ref if c < n else other_ref)[c % n])
         fs = feat_src(skel)
+        vv = stack2(w)
+        sib = sib + times(vv, tile(fs, ft_sib))
         if c < n:
             vv = stack2(jnp.where(id_ref[1] == c, 0.0, 1.0) * w)
-            own = own + times(vv, tile(fs, ft_own))
-            sib = sib + times(stack2(w), tile(fs, ft_sib))
-        else:
-            vv = stack2(w)
-            own = own + times(vv, tile(fs, ft_own))
-            sib = sib + times(vv, tile(fs, ft_sib))
+        own = own + times(vv, tile(fs, ft_own))
     peer_ref[0] = gain((4 * n - 1) * T) * own
     peer_ref[1] = gain((4 * n - 1) * T) * sib
-    fs = feat_src(own_group(id_ref, skg_ref))
-    bh_ref[:, :T], bl_ref[:, :T] = tile(fs, ft_own)
-    bh_ref[:, T:], bl_ref[:, T:] = tile(fs, ft_sib)
-
-
-def field_kernel(id_ref, gws_ref, skg_ref, bh_ref, bl_ref, peer_ref, own_ref, sib_ref):
+    kh, kl = tile(feat_src(own_group(id_ref, skg_ref)), ft_own)
+    bh_ref[...] = kh
+    bl_ref[...] = kl
+
+
+def field_kernel(id_ref, gws_ref, skg_ref, peer_ref, part_ref):
     n = gws_ref.shape[0]
     ft_own = feat_tgt(own_group(id_ref, skg_ref))
     total = jnp.zeros((VEC, T), f32)
@@ -210,13 +200,14 @@
         keep = jnp.where(id_ref[0] == g, 0.0, 1.0)
         col = slice(g * T, (g + 1) * T)
         total = total + times(stack2(keep * gws_ref[g]), tile(feat_src(skg_ref[:, col]), ft_own))
-    lowered = gain(T) * times(stack2(gain((n - 1) * T) * total), (bh_ref[...], bl_ref[...]))
-    own_ref[...] = peer_ref[0] + lowered[:, :T]
-    sib_ref[...] = peer_ref[1] + lowered[:, T:]
-
-
-def down_kernel(id_ref, own_ref, both_ref, mh_ref, ml_ref, near_ref, out_ref):
-    field = own_ref[...] + both_ref[1 - id_ref[2]]
+    part_ref[:VEC, :] = gain((n - 1) * T) * total
+    part_ref[VEC:, :] = peer_ref[1]
+
+
+def down_kernel(id_ref, cell_ref, peer_ref, bh_ref, bl_ref, mh_ref, ml_ref, near_ref, out_ref):
+    group = jnp.sum(cell_ref[:, :VEC, :], axis=0)
+    field = gain(T) * times(stack2(group), (bh_ref[...], bl_ref[...]))
+    field = field + peer_ref[0] + cell_ref[id_ref[4], VEC:, :]
     out_ref[...] = near_ref[...] + times(stack2(field), (mh_ref[...], ml_ref[...]))
 
 
@@ -228,12 +219,18 @@
     return jax.ShapeDtypeStruct(dims, dtype)
 
 
-def kernel(fn, name, out, scalars, arrays):
+def cost(tiles):
+    return pl.CostEstimate(flops=tiles * 10**8, bytes_accessed=tiles * 2**18, transcendentals=tiles * T * T)
+
+
+def kernel(fn, name, out, scalars, arrays, scratch=(), tiles=1):
     return pl.pallas_call(
         fn,
         out_shape=out,
         in_specs=[SM] * scalars + [VM] * arrays,
         out_specs=jax.tree.map(lambda _: VM, out),
+        scratch_shapes=scratch,
+        cost_estimate=cost(tiles),
         compiler_params=pltpu.CompilerParams(vmem_limit_bytes=24 << 20),
         name=name,
     )
@@ -246,9 +243,11 @@
     axes = ("grp", "z8", "zp", "core")
     group_id = lax.axis_index("grp")
     z8_id = lax.axis_index("z8")
+    zp_id = lax.axis_index("zp")
     core_id = lax.axis_index("core")
-    block_id = ((group_id * n_z8 + z8_id) * 2 + lax.axis_index("zp")) * 2 + core_id
-    ids = jnp.stack([group_id, z8_id, core_id, block_id * LEAVES_DEV]).astype(jnp.int32)
+    block_id = ((group_id * n_z8 + z8_id) * 2 + zp_id) * 2 + core_id
+    ids = [group_id, z8_id, core_id, block_id * LEAVES_DEV, zp_id * 2 + 1 - core_id]
+    ids = jnp.stack(ids).astype(jnp.int32)
     inputs = (points, charges, morton.reshape(1, n), skel_leaf, skel_block)
     srt, packed = pl.pallas_call(
         up_kernel,
@@ -261,22 +260,25 @@
     )(*inputs)
     part = lax.all_to_all(packed, "z8", 0, 0, tiled=False)
     whole = n_groups * n_z8 * 4
-    left = lax.ppermute(srt, axes, [(i, i + 1) for i in range(whole - 1)])
-    right = lax.ppermute(srt, axes, [(i + 1, i) for i in range(whole - 1)])
+    swap = [(0, 1), (1, 0)]
+    sib = lax.ppermute(srt, "core", swap)
+    odd = range(1, whole - 1, 2)
+    adj = lax.ppermute(srt, axes, [(i, i + 1) for i in odd] + [(i + 1, i) for i in odd])
     half_shape = shape(T, n, dtype=bf16)
-    mh, ml = kernel(pre_kernel, "pre", (half_shape, half_shape), 0, 3)(skel_block, skel_leaf, srt)
-    near = kernel(near_kernel, "near", shape(VEC, n), 3, 3)(ids, neighbours, counts, left, srt, right)
+    mh, ml = kernel(pre_kernel, "pre", (half_shape, half_shape), 0, 3, tiles=12)(skel_block, skel_leaf, srt)
+    block = pltpu.VMEM((ROWS, n), f32)
+    near = kernel(near_kernel, "near", shape(VEC, n), 3, 3, (block, block), 40)(ids, neighbours, counts, sib, adj, srt)
     part, near, mh, ml = lax.optimization_barrier((part, near, mh, ml))
-    other = lax.ppermute(part, "zp", [(0, 1), (1, 0)])
-    half = kernel(half_kernel, "half", shape(VEC, T), 1, 2)(ids, part, skel_group)
-    gw = kernel(group_kernel, "group", shape(n_groups, VEC, T), 1, 3)(ids, other, skel_group, half)
+    other = lax.ppermute(part, "zp", swap)
+    gw = kernel(group_kernel, "group", shape(n_groups, VEC, T), 1, 2, tiles=30)(ids, part, skel_group)
     gws = lax.all_to_all(gw, "grp", 0, 0, tiled=False)
-    peer, bh, bl = kernel(
-        peer_kernel, "peer", (shape(2, VEC, T), shape(T, 2 * T, dtype=bf16), shape(T, 2 * T, dtype=bf16)), 1, 6
-    )(ids, part, other, skel_block, left, right, skel_group)
-    own, sib = kernel(field_kernel, "field", (shape(VEC, T), shape(VEC, T)), 1, 5)(ids, gws, skel_group, bh, bl, peer)
-    both = lax.all_gather(sib, "core", axis=0, tiled=False)
-    return kernel(down_kernel, "down", shape(VEC, n), 1, 5)(ids, own, both, mh, ml, near)
+    square = shape(T, T, dtype=bf16)
+    peer, bh, bl = kernel(peer_kernel, "peer", (shape(2, VEC, T), square, square), 1, 5, tiles=33)(
+        ids, part, other, skel_block, sib, skel_group
+    )
+    mine = kernel(field_kernel, "field", shape(2 * VEC, T), 1, 3, tiles=20)(ids, gws, skel_group, peer)
+    cell = lax.all_gather(mine, ("zp", "core"), axis=0, tiled=False)
+    return kernel(down_kernel, "down", shape(VEC, n), 1, 7)(ids, cell, peer, bh, bl, mh, ml, near)
 
 
 def solution(mesh):

time: 70.1 us -> 68.1 us (0.971)
  Pallas kernels: 19.6 us -> 17.4 us
  blocking collectives: 8.25 us -> 10.4 us
  waiting for transfers between devices: 9.37 us -> 7.55 us
  starting transfers between devices: 32.2 us -> 31.4 us
    ppermute x3, waiting for transfers between devices: 4.99 us -> 1.65 us  [the longest x1 1.65 us: body(): lax.ppermute(srt, axes, [(i, i + 1) for i in odd] + [(i + 1, i) for i in...]
    pallas_call x7 -> x6, Pallas kernels: 15.6 us -> 13.4 us  [the longest x1 3.39 us: body(): kernel(near_kernel, 'near', shape(VEC, n), 3, 3, (block, block), 40)]
    all_gather x1, blocking collectives: 8.25 us -> 10.4 us  [body(): cell = lax.all_gather(mine, ('zp', 'core'), axis=0, tiled=False)]
    all_to_all x1, waiting for transfers between devices: 0.01 us -> 1.44 us  [body(): part = lax.all_to_all(packed, 'z8', 0, 0, tiled=False)]
    ppermute x3, starting transfers between devices: 9.66 us -> 8.85 us  [the longest x1 3.48 us: body(): lax.ppermute(srt, axes, [(i, i + 1) for i in odd] + [(i + 1, i) for i in...]
  transfers between devices with their start and end apart: 5 -> 5, of which waited for: 4 -> 3; matrix products, arithmetic and copies ran while one was open for 0% -> 0% of each run, Pallas kernels for 13% -> 15%
where the time goes in v4:
time: 68.1 us; the launch traced here: 67.5 us
  starting transfers between devices  31.4 us (46%)
  Pallas kernels  17.4 us (26%)
  blocking collectives  10.4 us (15%)
  waiting for transfers between devices  7.55 us (11%)
  local copies, waits for them, and re-layouts  0.72 us (1%)
    all_to_all x1, starting transfers between devices, body(): part = lax.all_to_all(packed, 'z8', 0, 0, tiled=False)  15.8 us
    all_gather x1, blocking collectives, body(): cell = lax.all_gather(mine, ('zp', 'core'), axis=0, tiled=False)  10.4 us
    all_to_all x1, starting transfers between devices, body(): gws = lax.all_to_all(gw, 'grp', 0, 0, tiled=False)  6.76 us
    all_to_all x1, waiting for transfers between devices, body(): gws = lax.all_to_all(gw, 'grp', 0, 0, tiled=False)  4.45 us
    pallas_call x1, Pallas kernels, body(): pl.pallas_call(up_kernel, out_shape=(shape(ROWS, n), shape(n_z8, PACK, HA...  3.97 us
    ppermute x1, starting transfers between devices, body(): lax.ppermute(srt, axes, [(i, i + 1) for i in odd] + [(i + 1, i) for i in...  3.48 us
    ppermute x1, starting transfers between devices, body(): other = lax.ppermute(part, 'zp', swap)  3.45 us
    pallas_call x1, Pallas kernels, body(): kernel(near_kernel, 'near', shape(VEC, n), 3, 3, (block, block), 40)  3.39 us
  transfers between devices with their start and end apart: 5, of which 3 were waited for; matrix products, arithmetic and copies ran while one was open for 0% of the time, Pallas kernels for 15%

profile of v4, /device:TPU:1, one launch (start us, length us, event | category | flops | bytes accessed | tf_op | source)
XLA Modules:
  0.0 67.5 jit_solution(14465032452919841308)
XLA Ops:
  0.0 4.0 %up.1 = (f32[24,1024]{1,0:T(8,128)}, f32[8,40,128]{2,1,0:T(8,128)}) custom-call(f32[3,1024]{1,0:T(4,128)} %pts_hbm.1, f32[16,1024]{1,0:T(8,128)} %chg_hbm.1, s32[1,1024]{1,0:T(1,128)} %bitcast.8, f32[3,1024]{1,0:T(4,128)} %skl_ref.1, f32[3,256]{1,0:T(4,128)} %skb_ref.3), custom_call_target="tpu_custom_call" | custom-call | tf_op jit(solution)/shard_map/up/pallas_call | solution.py:252
  4.0 0.0 copy-start.2
  4.0 15.8 %all-to-all-start = ((f32[8,40,128]{2,1,0:T(8,128)}), f32[8,40,128]{2,1,0:T(8,128)S(1)}, u32[]{:S(2)}, u32[]{:S(2)}) async-start(f32[8,40,128]{2,1,0:T(8,128)} %get-tuple-element.16), calls=%async_computation | async-start | bytes 327680 | tf_op jit(solution)/shard_map/all_to_all | solution.py:261
  19.8 3.5 %collective-permute-start.1 = (f32[24,1024]{1,0:T(8,128)S(1)}, f32[24,1024]{1,0:T(8,128)S(1)}, u32[]{:S(2)}, u32[]{:S(2)}) collective-permute-start(f32[24,1024]{1,0:T(8,128)S(1)} %copy-done.2), channel_id=1, source_target_pairs={{1,2},{3,4},{5,6},{7,8},{9,10},{11,12},{13,14},{15,16},{17,18},{19... | collective-permute-start | bytes 294920 | tf_op jit(solution)/shard_map/ppermute | solution.py:266
  23.3 1.9 %collective-permute-start = (f32[24,1024]{1,0:T(8,128)S(1)}, f32[24,1024]{1,0:T(8,128)S(1)}, u32[]{:S(2)}, u32[]{:S(2)}) collective-permute-start(f32[24,1024]{1,0:T(8,128)S(1)} %copy-done.2), channel_id=1, source_target_pairs={{0,1},{1,0},{2,3},{3,2},{4,5},{5,4},{6,7},{7,6},{8,9},{9,8},{10,11... | collective-permute-start | bytes 294920 | tf_op jit(solution)/shard_map/ppermute | solution.py:264
  25.2 0.0 copy-start
  25.2 0.0 copy-start.1
  25.2 0.1 stack.23.id_ref
  25.3 0.6 copy-done
  25.9 1.2 %pre.1 = (bf16[256,1024]{1,0:T(8,128)(2,1)S(1)}, bf16[256,1024]{1,0:T(8,128)(2,1)S(1)}) custom-call(f32[3,256]{1,0:T(4,128)S(1)} %copy-done.1, f32[3,1024]{1,0:T(4,128)S(1)} %copy-done, f32[24,1024]{1,0:T(8,128)S(1)} %copy-done.2), custom_call_target="tpu_custom_call" | custom-call | flops 1200000000 | bytes 3145728 | tf_op jit(solution)/shard_map/pre/pallas_call | solution.py:268
  27.1 0.0 copy-start.3
  27.2 1.6 %collective-permute-done.1.adj_ref = f32[24,1024]{1,0:T(8,128)S(1)} collective-permute-done((f32[24,1024]{1,0:T(8,128)S(1)}, f32[24,1024]{1,0:T(8,128)S(1)}, u32[]{:S(2)}, u32[]{:S(2)}) %collective-permute-start.1) | collective-permute-done | bytes 98336 | tf_op jit(solution)/shard_map/ppermute | solution.py:266
  28.8 0.0 collective-permute-done.sib_ref.sibling_ref
  28.8 3.4 %near.1.near_ref = f32[16,1024]{1,0:T(8,128)S(1)} custom-call(s32[5]{0:T(128)S(1)} %stack.23.id_ref, s32[4,8]{1,0:T(4,128)S(1)} %copy-done.4, s32[4]{0:T(128)S(1)} %copy-done.5, f32[24,1024]{1,0:T(8,128)S(1)} %collective-permute-done.sib_ref.sibling_ref, f32[24,1024]{1,0:T(8,128)S(1)} %collective-permute-done.1.adj_ref, f32[24,1024]{1,0:T(8,128)S(1)} %copy-done.2), custom_call_target="tpu_custom_call" | custom-call | flops 4000000000 | bytes 10485760 | tf_op jit(solution)/shard_map/near/pallas_call | solution.py:270
  32.2 1.4 %all-to-all-done.part_ref = f32[8,40,128]{2,1,0:T(8,128)S(1)} async-done(((f32[8,40,128]{2,1,0:T(8,128)}), f32[8,40,128]{2,1,0:T(8,128)S(1)}, u32[]{:S(2)}, u32[]{:S(2)}) %all-to-all-start) | async-done | bytes 163872 | tf_op jit(solution)/shard_map/all_to_all | solution.py:261
  33.6 3.4 %collective-permute-start.2 = (f32[8,40,128]{2,1,0:T(8,128)S(1)}, f32[8,40,128]{2,1,0:T(8,128)S(1)}, u32[]{:S(2)}, u32[]{:S(2)}) collective-permute-start(f32[8,40,128]{2,1,0:T(8,128)S(1)} %all-to-all-done.part_ref), channel_id=1, source_target_pairs={{0,2},{2,0},{1,3},{3,1},{4,6},{6,4},{5,7},{7,5},{8,10},{10,8},{9,1... | collective-permute-start | bytes 491528 | tf_op jit(solution)/shard_map/ppermute | solution.py:272
  37.1 2.2 %group.1 = f32[16,16,256]{2,1,0:T(8,128)} custom-call(s32[5]{0:T(128)S(1)} %stack.23.id_ref, f32[8,40,128]{2,1,0:T(8,128)S(1)} %all-to-all-done.part_ref, f32[3,4096]{1,0:T(4,128)S(1)} %copy-done.3), custom_call_target="tpu_custom_call" | custom-call | flops 3000000000 | bytes 7864320 | tf_op jit(solution)/shard_map/group/pallas_call | solution.py:273
  39.3 6.8 %all-to-all-start.1 = ((f32[16,16,256]{2,1,0:T(8,128)}), f32[16,16,256]{2,1,0:T(8,128)S(1)}, u32[]{:S(2)}, u32[]{:S(2)}) async-start(f32[16,16,256]{2,1,0:T(8,128)} %group.1), calls=%async_computation.1 | async-start | bytes 524288 | tf_op jit(solution)/shard_map/all_to_all | solution.py:274
  46.0 0.0 collective-permute-done.2.other_ref
  46.0 3.1 %peer.1 = (f32[2,16,256]{2,1,0:T(8,128)S(1)}, bf16[256,256]{1,0:T(8,128)(2,1)S(1)}, bf16[256,256]{1,0:T(8,128)(2,1)S(1)}) custom-call(s32[5]{0:T(128)S(1)} %stack.23.id_ref, f32[8,40,128]{2,1,0:T(8,128)S(1)} %all-to-all-done.part_ref, f32[8,40,128]{2,1,0:T(8,128)S(1)} %collective-permute-done.2.other_ref, f32[3,256]{1,0:T(4,128)S(1)} %copy-done.1, ...), custom_call_target="tpu_custom_call" | custom-call | flops 3300000000 | bytes 8650752 | tf_op jit(solution)/shard_map/peer/pallas_call | solution.py:276
  49.1 4.5 %all-to-all-done.1.gws_ref = f32[16,16,256]{2,1,0:T(8,128)S(1)} async-done(((f32[16,16,256]{2,1,0:T(8,128)}), f32[16,16,256]{2,1,0:T(8,128)S(1)}, u32[]{:S(2)}, u32[]{:S(2)}) %all-to-all-start.1) | async-done | bytes 262176 | tf_op jit(solution)/shard_map/all_to_all | solution.py:274
  53.6 2.0 %field.1 = f32[32,256]{1,0:T(8,128)S(1)} custom-call(s32[5]{0:T(128)S(1)} %stack.23.id_ref, f32[16,16,256]{2,1,0:T(8,128)S(1)} %all-to-all-done.1.gws_ref, f32[3,4096]{1,0:T(4,128)S(1)} %copy-done.3, f32[2,16,256]{2,1,0:T(8,128)S(1)} %get-tuple-element.21.peer_ref), custom_call_target="tpu_custom_call" | custom-call | flops 2000000000 | bytes 5242880 | tf_op jit(solution)/shard_map/field/pallas_call | solution.py:279
  55.5 10.4 %all-gather = f32[128,256]{1,0:T(8,128)S(1)} all-gather(f32[32,256]{1,0:T(8,128)S(1)} %field.1), channel_id=2, replica_groups=mesh['grp'=16,'z8'=8,'zp'=2,'core'=2] {'zp','core'}, dimensions={0}, use_global_device_ids=true | all-gather | bytes 163840 | tf_op jit(solution)/shard_map/all_gather | solution.py:280
  65.9 1.6 %down.1 = f32[16,1024]{1,0:T(8,128)} custom-call(s32[5]{0:T(128)S(1)} %stack.23.id_ref, f32[4,32,256]{2,1,0:T(8,128)S(1)} %bitcast.7, f32[2,16,256]{2,1,0:T(8,128)S(1)} %get-tuple-element.21.peer_ref, bf16[256,256]{1,0:T(8,128)(2,1)S(1)} %get-tuple-element.22.bh_ref, bf16[256,256]{1,0:T(8,128)(2,1)S(1)} %get-tuple-element.23.bl_ref, ...), custom_call_target="tpu_custom_call" | custom-call | flops 100000000 | bytes 262144 | tf_op jit(solution)/shard_map/down/pallas_call | solution.py:281
  (7 shorter events, 0.0 us)
Async XLA Ops:
  4.0 15.8 %copy-start.2 = (f32[24,1024]{1,0:T(8,128)S(1)}, f32[24,1024]{1,0:T(8,128)}, u32[]{:S(2)}) copy-start(f32[24,1024]{1,0:T(8,128)} %get-tuple-element.17.mid_ref) | copy-start | bytes 294916
  4.0 29.7 %all-to-all-start = ((f32[8,40,128]{2,1,0:T(8,128)}), f32[8,40,128]{2,1,0:T(8,128)S(1)}, u32[]{:S(2)}, u32[]{:S(2)}) async-start(f32[8,40,128]{2,1,0:T(8,128)} %get-tuple-element.16), calls=%async_computation | async-start | bytes 327680 | tf_op jit(solution)/shard_map/all_to_all | solution.py:261
  19.8 9.0 %collective-permute-start.1 = (f32[24,1024]{1,0:T(8,128)S(1)}, f32[24,1024]{1,0:T(8,128)S(1)}, u32[]{:S(2)}, u32[]{:S(2)}) collective-permute-start(f32[24,1024]{1,0:T(8,128)S(1)} %copy-done.2), channel_id=1, source_target_pairs={{1,2},{3,4},{5,6},{7,8},{9,10},{11,12},{13,14},{15,16},{17,18},{19... | collective-permute-start | bytes 294920 | tf_op jit(solution)/shard_map/ppermute | solution.py:266
  23.3 5.5 %collective-permute-start = (f32[24,1024]{1,0:T(8,128)S(1)}, f32[24,1024]{1,0:T(8,128)S(1)}, u32[]{:S(2)}, u32[]{:S(2)}) collective-permute-start(f32[24,1024]{1,0:T(8,128)S(1)} %copy-done.2), channel_id=1, source_target_pairs={{0,1},{1,0},{2,3},{3,2},{4,5},{5,4},{6,7},{7,6},{8,9},{9,8},{10,11... | collective-permute-start | bytes 294920 | tf_op jit(solution)/shard_map/ppermute | solution.py:264
  25.2 0.7 %copy-start = (f32[3,1024]{1,0:T(4,128)S(1)}, f32[3,1024]{1,0:T(4,128)}, u32[]{:S(2)}) copy-start(f32[3,1024]{1,0:T(4,128)} %skl_ref.1) | copy-start | bytes 36868
  25.2 0.7 %copy-start.1 = (f32[3,256]{1,0:T(4,128)S(1)}, f32[3,256]{1,0:T(4,128)}, u32[]{:S(2)}) copy-start(f32[3,256]{1,0:T(4,128)} %skb_ref.3) | copy-start | bytes 9220
  25.9 2.9 %copy-start.4 = (s32[4,8]{1,0:T(4,128)S(1)}, s32[4,8]{1,0:T(4,128)}, u32[]{:S(2)}) copy-start(s32[4,8]{1,0:T(4,128)} %nbr_ref.1) | copy-start | bytes 388
  25.9 2.9 %copy-start.5 = (s32[4]{0:T(128)S(1)}, s32[4]{0:T(128)}, u32[]{:S(2)}) copy-start(s32[4]{0:T(128)} %cnt_ref.1) | copy-start | bytes 52
  27.1 10.0 %copy-start.3 = (f32[3,4096]{1,0:T(4,128)S(1)}, f32[3,4096]{1,0:T(4,128)}, u32[]{:S(2)}) copy-start(f32[3,4096]{1,0:T(4,128)} %skg_ref.5) | copy-start | bytes 147460
  33.6 12.4 %collective-permute-start.2 = (f32[8,40,128]{2,1,0:T(8,128)S(1)}, f32[8,40,128]{2,1,0:T(8,128)S(1)}, u32[]{:S(2)}, u32[]{:S(2)}) collective-permute-start(f32[8,40,128]{2,1,0:T(8,128)S(1)} %all-to-all-done.part_ref), channel_id=1, source_target_pairs={{0,2},{2,0},{1,3},{3,1},{4,6},{6,4},{5,7},{7,5},{8,10},{10,8},{9,1... | collective-permute-start | bytes 491528 | tf_op jit(solution)/shard_map/ppermute | solution.py:272
  39.3 14.3 %all-to-all-start.1 = ((f32[16,16,256]{2,1,0:T(8,128)}), f32[16,16,256]{2,1,0:T(8,128)S(1)}, u32[]{:S(2)}, u32[]{:S(2)}) async-start(f32[16,16,256]{2,1,0:T(8,128)} %group.1), calls=%async_computation.1 | async-start | bytes 524288 | tf_op jit(solution)/shard_map/all_to_all | solution.py:274

commit v5 on v4

--- a/solution.py
+++ b/solution.py
@@ -89,7 +89,7 @@
     copies = [
         pltpu.make_async_copy(src, dst, sems.at[i])
         for i, (src, dst) in enumerate(
-            ((pts_hbm, pts_ref), (chg_hbm, chg_ref), (mor_hbm, mor_ref), (skl_hbm, skl_ref), (skb_hbm, skb_ref))
+            ((skl_hbm, skl_ref), (skb_hbm, skb_ref), (pts_hbm, pts_ref), (mor_hbm, mor_ref), (chg_hbm, chg_ref))
         )
     ]
     for c in copies:
@@ -100,30 +100,31 @@
     rows = jnp.concatenate([chg_ref[...], pts_ref[...], jnp.zeros((5, n), f32)], axis=0)
     a, b, c = split3(rows)
     parts = jnp.concatenate([a, b, c], axis=0).astype(bf16)
-    for i in range(n // T):
-        col = slice(i * T, (i + 1) * T)
-        hot = (lax.broadcasted_iota(jnp.int32, (n, T), 0) == mor_ref[:, col]).astype(f32).astype(bf16)
-        s = dg(parts, hot, 1, 0)
-        srt_ref[:, col] = s[:ROWS] + s[ROWS : 2 * ROWS] + s[2 * ROWS :]
-    srt_ref[VEC + 3 : VEC + 6, :T] = skb_ref[...]
+    row = lax.broadcasted_iota(jnp.int32, (n, T), 0)
     ft_block = feat_tgt(skb_ref[...])
     total = jnp.zeros((VEC, T), f32)
     for q in range(LEAVES_DEV):
         col = slice(q * T, (q + 1) * T)
         skel = skl_ref[:, col]
-        lw = times(stack2(srt_ref[:VEC, col]), tile(feat_src(srt_ref[VEC : VEC + 3, col]), feat_tgt(skel)))
+        hot = (row == mor_ref[:, col]).astype(f32).astype(bf16)
+        s = dg(parts, hot, 1, 0)
+        srt = s[:ROWS] + s[ROWS : 2 * ROWS] + s[2 * ROWS :]
+        srt_ref[:, col] = srt
+        vv = jnp.concatenate([s[:VEC], s[ROWS : ROWS + VEC] + s[2 * ROWS : 2 * ROWS + VEC]], axis=0).astype(bf16)
+        lw = times(vv, tile(feat_src(srt[VEC : VEC + 3]), feat_tgt(skel)))
         total = total + times(stack2(gain(T) * lw), tile(feat_src(skel), ft_block))
+    srt_ref[VEC + 3 : VEC + 6, :T] = skb_ref[...]
     packed = pack(gain(LEAVES_DEV * T) * total, skb_ref[...])
     for z in range(pack_ref.shape[0]):
         pack_ref[z] = packed
 
 
-def own_group(id_ref, skg_ref):
-    return skg_ref[:, pl.ds(pl.multiple_of(id_ref[0] * T, T), T)]
-
-
-def raised(id_ref, packs_ref, skg_ref):
-    ft = feat_tgt(own_group(id_ref, skg_ref))
+def own_group(skg_ref):
+    return skg_ref[:, pl.ds(pl.multiple_of(lax.axis_index("grp") * T, T), T)]
+
+
+def raised(packs_ref, skg_ref):
+    ft = feat_tgt(own_group(skg_ref))
     total = jnp.zeros((VEC, T), f32)
     for c in range(packs_ref.shape[0]):
         w, skel = unpack(packs_ref[c])
@@ -131,8 +132,8 @@
     return total
 
 
-def group_kernel(id_ref, part_ref, skg_ref, gw_ref):
-    total = gain(4 * part_ref.shape[0] * T) * raised(id_ref, part_ref, skg_ref)
+def group_kernel(part_ref, skg_ref, gw_ref):
+    total = gain(4 * part_ref.shape[0] * T) * raised(part_ref, skg_ref)
     for g in range(gw_ref.shape[0]):
         gw_ref[g] = total
 
@@ -147,9 +148,11 @@
         mh_ref[:, col], ml_ref[:, col] = split2(gain(T) * gain(T) * both)
 
 
-def near_kernel(id_ref, nbr_ref, cnt_ref, sib_ref, adj_ref, mid_ref, near_ref, left_ref, right_ref):
-    first = id_ref[3]
-    on_left = id_ref[2] == 1
+def near_kernel(nbr_ref, cnt_ref, sib_ref, adj_ref, mid_ref, near_ref, left_ref, right_ref):
+    core = lax.axis_index("core")
+    pair = (lax.axis_index("grp") * lax.axis_size("z8") + lax.axis_index("z8")) * 2 + lax.axis_index("zp")
+    first = (pair * 2 + core) * LEAVES_DEV
+    on_left = core == 1
     left_ref[...] = jnp.where(on_left, sib_ref[...], adj_ref[...])
     right_ref[...] = jnp.where(on_left, adj_ref[...], sib_ref[...])
     fts = [feat_tgt(mid_ref[VEC : VEC + 3, q * T : (q + 1) * T]) for q in range(LEAVES_DEV)]
@@ -171,7 +174,7 @@
         near_ref[:, q * T : (q + 1) * T] = gain(T) * acc[q]
 
 
-def peer_kernel(id_ref, part_ref, other_ref, skb_ref, sibling_ref, skg_ref, peer_ref, bh_ref, bl_ref):
+def peer_kernel(part_ref, other_ref, skb_ref, sibling_ref, skg_ref, peer_ref, bh_ref, bl_ref):
     n = part_ref.shape[0]
     ft_own = feat_tgt(skb_ref[...])
     ft_sib = feat_tgt(sibling_ref[VEC + 3 : VEC + 6, :T])
@@ -183,31 +186,31 @@
         vv = stack2(w)
         sib = sib + times(vv, tile(fs, ft_sib))
         if c < n:
-            vv = stack2(jnp.where(id_ref[1] == c, 0.0, 1.0) * w)
+            vv = stack2(jnp.where(lax.axis_index("z8") == c, 0.0, 1.0) * w)
         own = own + times(vv, tile(fs, ft_own))
     peer_ref[0] = gain((4 * n - 1) * T) * own
     peer_ref[1] = gain((4 * n - 1) * T) * sib
-    kh, kl = tile(feat_src(own_group(id_ref, skg_ref)), ft_own)
+    kh, kl = tile(feat_src(own_group(skg_ref)), ft_own)
     bh_ref[...] = kh
     bl_ref[...] = kl
 
 
-def field_kernel(id_ref, gws_ref, skg_ref, peer_ref, part_ref):
+def field_kernel(gws_ref, skg_ref, peer_ref, part_ref):
     n = gws_ref.shape[0]
-    ft_own = feat_tgt(own_group(id_ref, skg_ref))
+    ft_own = feat_tgt(own_group(skg_ref))
     total = jnp.zeros((VEC, T), f32)
     for g in range(n):
-        keep = jnp.where(id_ref[0] == g, 0.0, 1.0)
+        keep = jnp.where(lax.axis_index("grp") == g, 0.0, 1.0)
         col = slice(g * T, (g + 1) * T)
         total = total + times(stack2(keep * gws_ref[g]), tile(feat_src(skg_ref[:, col]), ft_own))
     part_ref[:VEC, :] = gain((n - 1) * T) * total
     part_ref[VEC:, :] = peer_ref[1]
 
 
-def down_kernel(id_ref, cell_ref, peer_ref, bh_ref, bl_ref, mh_ref, ml_ref, near_ref, out_ref):
+def down_kernel(cell_ref, peer_ref, bh_ref, bl_ref, mh_ref, ml_ref, near_ref, out_ref):
     group = jnp.sum(cell_ref[:, :VEC, :], axis=0)
     field = gain(T) * times(stack2(group), (bh_ref[...], bl_ref[...]))
-    field = field + peer_ref[0] + cell_ref[id_ref[4], VEC:, :]
+    field = field + peer_ref[0] + cell_ref[lax.axis_index("zp") * 2 + 1 - lax.axis_index("core"), VEC:, :]
     out_ref[...] = near_ref[...] + times(stack2(field), (mh_ref[...], ml_ref[...]))
 
 
@@ -241,13 +244,6 @@
     n_z8 = lax.axis_size("z8")
     n = points.shape[1]
     axes = ("grp", "z8", "zp", "core")
-    group_id = lax.axis_index("grp")
-    z8_id = lax.axis_index("z8")
-    zp_id = lax.axis_index("zp")
-    core_id = lax.axis_index("core")
-    block_id = ((group_id * n_z8 + z8_id) * 2 + zp_id) * 2 + core_id
-    ids = [group_id, z8_id, core_id, block_id * LEAVES_DEV, zp_id * 2 + 1 - core_id]
-    ids = jnp.stack(ids).astype(jnp.int32)
     inputs = (points, charges, morton.reshape(1, n), skel_leaf, skel_block)
     srt, packed = pl.pallas_call(
         up_kernel,
@@ -267,18 +263,18 @@
     half_shape = shape(T, n, dtype=bf16)
     mh, ml = kernel(pre_kernel, "pre", (half_shape, half_shape), 0, 3, tiles=12)(skel_block, skel_leaf, srt)
     block = pltpu.VMEM((ROWS, n), f32)
-    near = kernel(near_kernel, "near", shape(VEC, n), 3, 3, (block, block), 40)(ids, neighbours, counts, sib, adj, srt)
+    near = kernel(near_kernel, "near", shape(VEC, n), 2, 3, (block, block), 40)(neighbours, counts, sib, adj, srt)
     part, near, mh, ml = lax.optimization_barrier((part, near, mh, ml))
     other = lax.ppermute(part, "zp", swap)
-    gw = kernel(group_kernel, "group", shape(n_groups, VEC, T), 1, 2, tiles=30)(ids, part, skel_group)
+    gw = kernel(group_kernel, "group", shape(n_groups, VEC, T), 0, 2, tiles=30)(part, skel_group)
     gws = lax.all_to_all(gw, "grp", 0, 0, tiled=False)
     square = shape(T, T, dtype=bf16)
-    peer, bh, bl = kernel(peer_kernel, "peer", (shape(2, VEC, T), square, square), 1, 5, tiles=33)(
-        ids, part, other, skel_block, sib, skel_group
+    peer, bh, bl = kernel(peer_kernel, "peer", (shape(2, VEC, T), square, square), 0, 5, tiles=33)(
+        part, other, skel_block, sib, skel_group
     )
-    mine = kernel(field_kernel, "field", shape(2 * VEC, T), 1, 3, tiles=20)(ids, gws, skel_group, peer)
+    mine = kernel(field_kernel, "field", shape(2 * VEC, T), 0, 3, tiles=20)(gws, skel_group, peer)
     cell = lax.all_gather(mine, ("zp", "core"), axis=0, tiled=False)
-    return kernel(down_kernel, "down", shape(VEC, n), 1, 7)(ids, cell, peer, bh, bl, mh, ml, near)
+    return kernel(down_kernel, "down", shape(VEC, n), 0, 7)(cell, peer, bh, bl, mh, ml, near)
 
 
 def solution(mesh):

time: 68.1 us -> 66.4 us (0.975)
  Pallas kernels: 17.4 us -> 15.2 us
  waiting for transfers between devices: 7.55 us -> 8.79 us
    pallas_call x5, Pallas kernels: 12.2 us -> 10.1 us  [the longest x1 3.39 us: body(): kernel(near_kernel, 'near', shape(VEC, n), 2, 3, (block, block), 40)]
    ppermute x1, waiting for transfers between devices: 1.65 us -> 2.34 us  [body(): lax.ppermute(srt, axes, [(i, i + 1) for i in odd] + [(i + 1, i) for i in...]
  transfers between devices with their start and end apart: 5 -> 5, of which waited for: 3 -> 3; matrix products, arithmetic and copies ran while one was open for 0% -> 0% of each run, Pallas kernels for 15% -> 13%
where the time goes in v5:
time: 66.4 us; the launch traced here: 65.9 us
  starting transfers between devices  31.4 us (47%)
  Pallas kernels  15.2 us (23%)
  blocking collectives  10.4 us (16%)
  waiting for transfers between devices  8.79 us (13%)
    all_to_all x1, starting transfers between devices, body(): part = lax.all_to_all(packed, 'z8', 0, 0, tiled=False)  15.8 us
    all_gather x1, blocking collectives, body(): cell = lax.all_gather(mine, ('zp', 'core'), axis=0, tiled=False)  10.4 us
    all_to_all x1, starting transfers between devices, body(): gws = lax.all_to_all(gw, 'grp', 0, 0, tiled=False)  6.77 us
    all_to_all x1, waiting for transfers between devices, body(): gws = lax.all_to_all(gw, 'grp', 0, 0, tiled=False)  4.99 us
    pallas_call x1, Pallas kernels, body(): pl.pallas_call(up_kernel, out_shape=(shape(ROWS, n), shape(n_z8, PACK, HA...  3.95 us
    ppermute x1, starting transfers between devices, body(): lax.ppermute(srt, axes, [(i, i + 1) for i in odd] + [(i + 1, i) for i in...  3.49 us
    ppermute x1, starting transfers between devices, body(): other = lax.ppermute(part, 'zp', swap)  3.42 us
    pallas_call x1, Pallas kernels, body(): kernel(near_kernel, 'near', shape(VEC, n), 2, 3, (block, block), 40)  3.39 us
  transfers between devices with their start and end apart: 5, of which 3 were waited for; matrix products, arithmetic and copies ran while one was open for 0% of the time, Pallas kernels for 13%

profile of v5, /device:TPU:1, one launch (start us, length us, event | category | flops | bytes accessed | tf_op | source)
XLA Modules:
  0.0 65.9 jit_solution(18086264926528696974)
XLA Ops:
  0.0 4.0 %up.1 = (f32[24,1024]{1,0:T(8,128)}, f32[8,40,128]{2,1,0:T(8,128)}) custom-call(f32[3,1024]{1,0:T(4,128)} %pts_hbm.1, f32[16,1024]{1,0:T(8,128)} %chg_hbm.1, s32[1,1024]{1,0:T(1,128)} %bitcast.3, f32[3,1024]{1,0:T(4,128)} %skl_ref.1, f32[3,256]{1,0:T(4,128)} %skb_ref.3), custom_call_target="tpu_custom_call" | custom-call | tf_op jit(solution)/shard_map/up/pallas_call | solution.py:248
  4.0 0.0 copy-start
  4.0 0.0 copy-start.1
  4.0 15.8 %all-to-all-start = ((f32[8,40,128]{2,1,0:T(8,128)}), f32[8,40,128]{2,1,0:T(8,128)S(1)}, u32[]{:S(2)}, u32[]{:S(2)}) async-start(f32[8,40,128]{2,1,0:T(8,128)} %get-tuple-element.16), calls=%async_computation | async-start | bytes 327680 | tf_op jit(solution)/shard_map/all_to_all | solution.py:257
  19.8 0.0 copy-start.4
  19.8 0.0 copy-start.5
  19.8 3.5 %collective-permute-start.1 = (f32[24,1024]{1,0:T(8,128)S(1)}, f32[24,1024]{1,0:T(8,128)S(1)}, u32[]{:S(2)}, u32[]{:S(2)}) collective-permute-start(f32[24,1024]{1,0:T(8,128)S(1)} %copy-done.2), channel_id=1, source_target_pairs={{1,2},{3,4},{5,6},{7,8},{9,10},{11,12},{13,14},{15,16},{17,18},{19... | collective-permute-start | bytes 294920 | tf_op jit(solution)/shard_map/ppermute | solution.py:262
  23.3 1.9 %collective-permute-start = (f32[24,1024]{1,0:T(8,128)S(1)}, f32[24,1024]{1,0:T(8,128)S(1)}, u32[]{:S(2)}, u32[]{:S(2)}) collective-permute-start(f32[24,1024]{1,0:T(8,128)S(1)} %copy-done.2), channel_id=1, source_target_pairs={{0,1},{1,0},{2,3},{3,2},{4,5},{5,4},{6,7},{7,6},{8,9},{9,8},{10,11... | collective-permute-start | bytes 294920 | tf_op jit(solution)/shard_map/ppermute | solution.py:260
  25.3 1.2 %pre.1 = (bf16[256,1024]{1,0:T(8,128)(2,1)S(1)}, bf16[256,1024]{1,0:T(8,128)(2,1)S(1)}) custom-call(f32[3,256]{1,0:T(4,128)S(1)} %copy-done.1, f32[3,1024]{1,0:T(4,128)S(1)} %copy-done, f32[24,1024]{1,0:T(8,128)S(1)} %copy-done.2), custom_call_target="tpu_custom_call" | custom-call | flops 1200000000 | bytes 3145728 | tf_op jit(solution)/shard_map/pre/pallas_call | solution.py:264
  26.5 0.0 copy-start.3
  26.5 2.3 %collective-permute-done.1.adj_ref = f32[24,1024]{1,0:T(8,128)S(1)} collective-permute-done((f32[24,1024]{1,0:T(8,128)S(1)}, f32[24,1024]{1,0:T(8,128)S(1)}, u32[]{:S(2)}, u32[]{:S(2)}) %collective-permute-start.1) | collective-permute-done | bytes 98336 | tf_op jit(solution)/shard_map/ppermute | solution.py:262
  28.8 0.0 collective-permute-done.sib_ref.sibling_ref
  28.8 3.4 %near.1.near_ref = f32[16,1024]{1,0:T(8,128)S(1)} custom-call(s32[4,8]{1,0:T(4,128)S(1)} %copy-done.4, s32[4]{0:T(128)S(1)} %copy-done.5, f32[24,1024]{1,0:T(8,128)S(1)} %collective-permute-done.sib_ref.sibling_ref, f32[24,1024]{1,0:T(8,128)S(1)} %collective-permute-done.1.adj_ref, f32[24,1024]{1,0:T(8,128)S(1)} %copy-done.2), custom_call_target="tpu_custom_call" | custom-call | flops 4000000000 | bytes 10485760 | tf_op jit(solution)/shard_map/near/pallas_call | solution.py:266
  32.2 1.5 %all-to-all-done.part_ref = f32[8,40,128]{2,1,0:T(8,128)S(1)} async-done(((f32[8,40,128]{2,1,0:T(8,128)}), f32[8,40,128]{2,1,0:T(8,128)S(1)}, u32[]{:S(2)}, u32[]{:S(2)}) %all-to-all-start) | async-done | bytes 163872 | tf_op jit(solution)/shard_map/all_to_all | solution.py:257
  33.7 3.4 %collective-permute-start.2 = (f32[8,40,128]{2,1,0:T(8,128)S(1)}, f32[8,40,128]{2,1,0:T(8,128)S(1)}, u32[]{:S(2)}, u32[]{:S(2)}) collective-permute-start(f32[8,40,128]{2,1,0:T(8,128)S(1)} %all-to-all-done.part_ref), channel_id=1, source_target_pairs={{0,2},{2,0},{1,3},{3,1},{4,6},{6,4},{5,7},{7,5},{8,10},{10,8},{9,1... | collective-permute-start | bytes 491528 | tf_op jit(solution)/shard_map/ppermute | solution.py:268
  37.1 0.0 copy-done.3
  37.1 1.6 %group.1 = f32[16,16,256]{2,1,0:T(8,128)} custom-call(f32[8,40,128]{2,1,0:T(8,128)S(1)} %all-to-all-done.part_ref, f32[3,4096]{1,0:T(4,128)S(1)} %copy-done.3), custom_call_target="tpu_custom_call" | custom-call | flops 3000000000 | bytes 7864320 | tf_op jit(solution)/shard_map/group/pallas_call | solution.py:269
  38.7 6.8 %all-to-all-start.1 = ((f32[16,16,256]{2,1,0:T(8,128)}), f32[16,16,256]{2,1,0:T(8,128)S(1)}, u32[]{:S(2)}, u32[]{:S(2)}) async-start(f32[16,16,256]{2,1,0:T(8,128)} %group.1), calls=%async_computation.1 | async-start | bytes 524288 | tf_op jit(solution)/shard_map/all_to_all | solution.py:270
  45.5 0.0 collective-permute-done.2.other_ref
  45.5 2.5 %peer.1 = (f32[2,16,256]{2,1,0:T(8,128)S(1)}, bf16[256,256]{1,0:T(8,128)(2,1)S(1)}, bf16[256,256]{1,0:T(8,128)(2,1)S(1)}) custom-call(f32[8,40,128]{2,1,0:T(8,128)S(1)} %all-to-all-done.part_ref, f32[8,40,128]{2,1,0:T(8,128)S(1)} %collective-permute-done.2.other_ref, f32[3,256]{1,0:T(4,128)S(1)} %copy-done.1, ...), custom_call_target="tpu_custom_call" | custom-call | flops 3300000000 | bytes 8650752 | tf_op jit(solution)/shard_map/peer/pallas_call | solution.py:272
  48.0 5.0 %all-to-all-done.1.gws_ref = f32[16,16,256]{2,1,0:T(8,128)S(1)} async-done(((f32[16,16,256]{2,1,0:T(8,128)}), f32[16,16,256]{2,1,0:T(8,128)S(1)}, u32[]{:S(2)}, u32[]{:S(2)}) %all-to-all-start.1) | async-done | bytes 262176 | tf_op jit(solution)/shard_map/all_to_all | solution.py:270
  53.0 1.4 %field.1 = f32[32,256]{1,0:T(8,128)S(1)} custom-call(f32[16,16,256]{2,1,0:T(8,128)S(1)} %all-to-all-done.1.gws_ref, f32[3,4096]{1,0:T(4,128)S(1)} %copy-done.3, f32[2,16,256]{2,1,0:T(8,128)S(1)} %get-tuple-element.21.peer_ref), custom_call_target="tpu_custom_call" | custom-call | flops 2000000000 | bytes 5242880 | tf_op jit(solution)/shard_map/field/pallas_call | solution.py:275
  54.5 10.4 %all-gather = f32[128,256]{1,0:T(8,128)S(1)} all-gather(f32[32,256]{1,0:T(8,128)S(1)} %field.1), channel_id=2, replica_groups=mesh['grp'=16,'z8'=8,'zp'=2,'core'=2] {'zp','core'}, dimensions={0}, use_global_device_ids=true | all-gather | bytes 163840 | tf_op jit(solution)/shard_map/all_gather | solution.py:276
  64.8 1.1 %down.1 = f32[16,1024]{1,0:T(8,128)} custom-call(f32[4,32,256]{2,1,0:T(8,128)S(1)} %bitcast.2, f32[2,16,256]{2,1,0:T(8,128)S(1)} %get-tuple-element.21.peer_ref, bf16[256,256]{1,0:T(8,128)(2,1)S(1)} %get-tuple-element.22.bh_ref, bf16[256,256]{1,0:T(8,128)(2,1)S(1)} %get-tuple-element.23.bl_ref, bf16[256,1024]{1,0:T(8,128)(2,1)S(1)} %get-tuple-element.24.mh_ref, ...), custom_call_target="tpu_custom_call" | custom-call | flops 100000000 | bytes 262144 | tf_op jit(solution)/shard_map/down/pallas_call | solution.py:277
  (6 shorter events, 0.0 us)
Async XLA Ops:
  4.0 15.8 %copy-start.2 = (f32[24,1024]{1,0:T(8,128)S(1)}, f32[24,1024]{1,0:T(8,128)}, u32[]{:S(2)}) copy-start(f32[24,1024]{1,0:T(8,128)} %get-tuple-element.17.mid_ref) | copy-start | bytes 294916
  4.0 21.3 %copy-start = (f32[3,1024]{1,0:T(4,128)S(1)}, f32[3,1024]{1,0:T(4,128)}, u32[]{:S(2)}) copy-start(f32[3,1024]{1,0:T(4,128)} %skl_ref.1) | copy-start | bytes 36868
  4.0 21.3 %copy-start.1 = (f32[3,256]{1,0:T(4,128)S(1)}, f32[3,256]{1,0:T(4,128)}, u32[]{:S(2)}) copy-start(f32[3,256]{1,0:T(4,128)} %skb_ref.3) | copy-start | bytes 9220
  4.0 29.7 %all-to-all-start = ((f32[8,40,128]{2,1,0:T(8,128)}), f32[8,40,128]{2,1,0:T(8,128)S(1)}, u32[]{:S(2)}, u32[]{:S(2)}) async-start(f32[8,40,128]{2,1,0:T(8,128)} %get-tuple-element.16), calls=%async_computation | async-start | bytes 327680 | tf_op jit(solution)/shard_map/all_to_all | solution.py:257
  19.8 9.0 %copy-start.4 = (s32[4,8]{1,0:T(4,128)S(1)}, s32[4,8]{1,0:T(4,128)}, u32[]{:S(2)}) copy-start(s32[4,8]{1,0:T(4,128)} %nbr_ref.1) | copy-start | bytes 388
  19.8 9.0 %copy-start.5 = (s32[4]{0:T(128)S(1)}, s32[4]{0:T(128)}, u32[]{:S(2)}) copy-start(s32[4]{0:T(128)} %cnt_ref.1) | copy-start | bytes 52
  19.8 9.0 %collective-permute-start.1 = (f32[24,1024]{1,0:T(8,128)S(1)}, f32[24,1024]{1,0:T(8,128)S(1)}, u32[]{:S(2)}, u32[]{:S(2)}) collective-permute-start(f32[24,1024]{1,0:T(8,128)S(1)} %copy-done.2), channel_id=1, source_target_pairs={{1,2},{3,4},{5,6},{7,8},{9,10},{11,12},{13,14},{15,16},{17,18},{19... | collective-permute-start | bytes 294920 | tf_op jit(solution)/shard_map/ppermute | solution.py:262
  23.3 5.5 %collective-permute-start = (f32[24,1024]{1,0:T(8,128)S(1)}, f32[24,1024]{1,0:T(8,128)S(1)}, u32[]{:S(2)}, u32[]{:S(2)}) collective-permute-start(f32[24,1024]{1,0:T(8,128)S(1)} %copy-done.2), channel_id=1, source_target_pairs={{0,1},{1,0},{2,3},{3,2},{4,5},{5,4},{6,7},{7,6},{8,9},{9,8},{10,11... | collective-permute-start | bytes 294920 | tf_op jit(solution)/shard_map/ppermute | solution.py:260
  26.5 10.6 %copy-start.3 = (f32[3,4096]{1,0:T(4,128)S(1)}, f32[3,4096]{1,0:T(4,128)}, u32[]{:S(2)}) copy-start(f32[3,4096]{1,0:T(4,128)} %skg_ref.5) | copy-start | bytes 147460
  33.7 11.8 %collective-permute-start.2 = (f32[8,40,128]{2,1,0:T(8,128)S(1)}, f32[8,40,128]{2,1,0:T(8,128)S(1)}, u32[]{:S(2)}, u32[]{:S(2)}) collective-permute-start(f32[8,40,128]{2,1,0:T(8,128)S(1)} %all-to-all-done.part_ref), channel_id=1, source_target_pairs={{0,2},{2,0},{1,3},{3,1},{4,6},{6,4},{5,7},{7,5},{8,10},{10,8},{9,1... | collective-permute-start | bytes 491528 | tf_op jit(solution)/shard_map/ppermute | solution.py:268
  38.7 14.3 %all-to-all-start.1 = ((f32[16,16,256]{2,1,0:T(8,128)}), f32[16,16,256]{2,1,0:T(8,128)S(1)}, u32[]{:S(2)}, u32[]{:S(2)}) async-start(f32[16,16,256]{2,1,0:T(8,128)} %group.1), calls=%async_computation.1 | async-start | bytes 524288 | tf_op jit(solution)/shard_map/all_to_all | solution.py:270

commit v6 on v5

--- a/solution.py
+++ b/solution.py
@@ -148,33 +148,59 @@
         mh_ref[:, col], ml_ref[:, col] = split2(gain(T) * gain(T) * both)
 
 
-def near_kernel(nbr_ref, cnt_ref, sib_ref, adj_ref, mid_ref, near_ref, left_ref, right_ref):
-    core = lax.axis_index("core")
+def first_leaf():
     pair = (lax.axis_index("grp") * lax.axis_size("z8") + lax.axis_index("z8")) * 2 + lax.axis_index("zp")
-    first = (pair * 2 + core) * LEAVES_DEV
-    on_left = core == 1
-    left_ref[...] = jnp.where(on_left, sib_ref[...], adj_ref[...])
-    right_ref[...] = jnp.where(on_left, adj_ref[...], sib_ref[...])
-    fts = [feat_tgt(mid_ref[VEC : VEC + 3, q * T : (q + 1) * T]) for q in range(LEAVES_DEV)]
+    return (pair * 2 + lax.axis_index("core")) * LEAVES_DEV
+
+
+def leaf(ref, j):
+    col = slice(j * T, (j + 1) * T)
+    return ref[:VEC, col], ref[VEC : VEC + 3, col]
+
+
+def uses(nbr_ref, cnt_ref, q, source):
+    count = jnp.int32(0)
+    for k in range(nbr_ref.shape[1]):
+        hit = jnp.logical_and(nbr_ref[q, k] == source, cnt_ref[q] > k)
+        count = count + hit.astype(jnp.int32)
+    return count
+
+
+def side_near(nbr_ref, cnt_ref, blk_ref, on_right, fts, acc):
+    first = first_leaf() + jnp.where(on_right, LEAVES_DEV, -LEAVES_DEV)
+    for d in range(LEAVES_DEV):
+        (v0, x0), (v1, x1) = leaf(blk_ref, d), leaf(blk_ref, LEAVES_DEV - 1 - d)
+        v = jnp.where(on_right, v0, v1)
+        fs = feat_src(jnp.where(on_right, x0, x1))
+        source = first + jnp.where(on_right, d, LEAVES_DEV - 1 - d)
+        for e in range(d, LEAVES_DEV):
+            q0, q1 = e, LEAVES_DEV - 1 - e
+            m = jnp.where(on_right, uses(nbr_ref, cnt_ref, q0, source), uses(nbr_ref, cnt_ref, q1, source))
+            r = times(stack2(m.astype(f32) * v), tile(fs, jnp.where(on_right, fts[q0], fts[q1])))
+            acc[q0] = acc[q0] + jnp.where(on_right, r, 0.0)
+            acc[q1] = acc[q1] + jnp.where(on_right, 0.0, r)
+
+
+def near_kernel(nbr_ref, cnt_ref, sib_ref, mid_ref, near_ref):
+    on_right = lax.axis_index("core") == 0
+    first = first_leaf()
+    fts = [feat_tgt(leaf(mid_ref, q)[1]) for q in range(LEAVES_DEV)]
     acc = [jnp.zeros((VEC, T), f32) for _ in range(LEAVES_DEV)]
-    for s in range(-LEAVES_DEV, 2 * LEAVES_DEV):
-        ref = (left_ref, mid_ref, right_ref)[s // LEAVES_DEV + 1]
-        j = s % LEAVES_DEV
-        v = ref[:VEC, j * T : (j + 1) * T]
-        fs = feat_src(ref[VEC : VEC + 3, j * T : (j + 1) * T])
+    for j in range(LEAVES_DEV):
+        v, x = leaf(mid_ref, j)
+        fs = feat_src(x)
         for q in range(LEAVES_DEV):
-            if abs(s - q) > LEAVES_DEV:
-                continue
-            uses = jnp.int32(1 if s == q else 0)
-            for k in range(nbr_ref.shape[1]):
-                hit = jnp.logical_and(nbr_ref[q, k] == first + s, cnt_ref[q] > k)
-                uses = uses + hit.astype(jnp.int32)
-            acc[q] = acc[q] + times(stack2(uses.astype(f32) * v), tile(fs, fts[q]))
+            m = 1 if j == q else uses(nbr_ref, cnt_ref, q, first + j)
+            vv = stack2(v if j == q else m.astype(f32) * v)
+            acc[q] = acc[q] + times(vv, tile(fs, fts[q]))
+    side_near(nbr_ref, cnt_ref, sib_ref, on_right, fts, acc)
     for q in range(LEAVES_DEV):
         near_ref[:, q * T : (q + 1) * T] = gain(T) * acc[q]
 
 
-def peer_kernel(part_ref, other_ref, skb_ref, sibling_ref, skg_ref, peer_ref, bh_ref, bl_ref):
+def peer_kernel(
+    nbr_ref, cnt_ref, part_ref, other_ref, skb_ref, sibling_ref, skg_ref, adj_ref, mid_ref, near_ref, peer_ref, bh_ref, bl_ref, all_ref
+):
     n = part_ref.shape[0]
     ft_own = feat_tgt(skb_ref[...])
     ft_sib = feat_tgt(sibling_ref[VEC + 3 : VEC + 6, :T])
@@ -193,6 +219,12 @@
     kh, kl = tile(feat_src(own_group(skg_ref)), ft_own)
     bh_ref[...] = kh
     bl_ref[...] = kl
+    fts = [feat_tgt(leaf(mid_ref, q)[1]) for q in range(LEAVES_DEV)]
+    acc = [jnp.zeros((VEC, T), f32) for _ in range(LEAVES_DEV)]
+    side_near(nbr_ref, cnt_ref, adj_ref, lax.axis_index("core") == 1, fts, acc)
+    for q in range(LEAVES_DEV):
+        col = slice(q * T, (q + 1) * T)
+        all_ref[:, col] = near_ref[:, col] + gain(T) * acc[q]
 
 
 def field_kernel(gws_ref, skg_ref, peer_ref, part_ref):
@@ -258,19 +290,19 @@
     whole = n_groups * n_z8 * 4
     swap = [(0, 1), (1, 0)]
     sib = lax.ppermute(srt, "core", swap)
+    half_shape = shape(T, n, dtype=bf16)
+    mh, ml = kernel(pre_kernel, "pre", (half_shape, half_shape), 0, 3, tiles=12)(skel_block, skel_leaf, srt)
+    near = kernel(near_kernel, "near", shape(VEC, n), 2, 2, tiles=26)(neighbours, counts, sib, srt)
+    srt, near, mh, ml = lax.optimization_barrier((srt, near, mh, ml))
     odd = range(1, whole - 1, 2)
     adj = lax.ppermute(srt, axes, [(i, i + 1) for i in odd] + [(i + 1, i) for i in odd])
-    half_shape = shape(T, n, dtype=bf16)
-    mh, ml = kernel(pre_kernel, "pre", (half_shape, half_shape), 0, 3, tiles=12)(skel_block, skel_leaf, srt)
-    block = pltpu.VMEM((ROWS, n), f32)
-    near = kernel(near_kernel, "near", shape(VEC, n), 2, 3, (block, block), 40)(neighbours, counts, sib, adj, srt)
     part, near, mh, ml = lax.optimization_barrier((part, near, mh, ml))
     other = lax.ppermute(part, "zp", swap)
     gw = kernel(group_kernel, "group", shape(n_groups, VEC, T), 0, 2, tiles=30)(part, skel_group)
     gws = lax.all_to_all(gw, "grp", 0, 0, tiled=False)
     square = shape(T, T, dtype=bf16)
-    peer, bh, bl = kernel(peer_kernel, "peer", (shape(2, VEC, T), square, square), 0, 5, tiles=33)(
-        part, other, skel_block, sib, skel_group
+    peer, bh, bl, near = kernel(peer_kernel, "peer", (shape(2, VEC, T), square, square, shape(VEC, n)), 2, 8, tiles=43)(
+        neighbours, counts, part, other, skel_block, sib, skel_group, adj, srt, near
     )
     mine = kernel(field_kernel, "field", shape(2 * VEC, T), 0, 3, tiles=20)(gws, skel_group, peer)
     cell = lax.all_gather(mine, ("zp", "core"), axis=0, tiled=False)

time: 66.4 us -> 65.9 us (level)
  waiting for transfers between devices: 8.79 us -> 7.9 us
  Pallas kernels: 15.2 us -> 16 us
    all_to_all x1, waiting for transfers between devices: 1.46 us -> 4.45 us  [body(): part = lax.all_to_all(packed, 'z8', 0, 0, tiled=False)]
    ppermute x1, waiting for transfers between devices: 2.34 us -> 0.01 us  [body(): lax.ppermute(srt, axes, [(i, i + 1) for i in odd] + [(i + 1, i) for i in...]
    all_to_all x1, waiting for transfers between devices: 4.99 us -> 3.45 us  [body(): gws = lax.all_to_all(gw, 'grp', 0, 0, tiled=False)]
    ppermute x1, starting transfers between devices: 1.92 us -> 2.86 us  [body(): sib = lax.ppermute(srt, 'core', swap)]
    ppermute x1, starting transfers between devices: 3.49 us -> 2.55 us  [body(): lax.ppermute(srt, axes, [(i, i + 1) for i in odd] + [(i + 1, i) for i in...]
    pallas_call x2, Pallas kernels: 5.93 us -> 6.76 us  [the longest x1 4.08 us: body(): kernel(peer_kernel, 'peer', (shape(2, VEC, T), square, square, shape(VEC,...]
  transfers between devices with their start and end apart: 5 -> 5, of which waited for: 3 -> 2; matrix products, arithmetic and copies ran while one was open for 0% -> 0% of each run, Pallas kernels for 13% -> 15%
where the time goes in v6:
time: 65.9 us; the launch traced here: 65.5 us
  starting transfers between devices  31.4 us (48%)
  Pallas kernels  16 us (24%)
  blocking collectives  9.9 us (15%)
  waiting for transfers between devices  7.9 us (12%)
    all_to_all x1, starting transfers between devices, body(): part = lax.all_to_all(packed, 'z8', 0, 0, tiled=False)  15.8 us
    all_gather x1, blocking collectives, body(): cell = lax.all_gather(mine, ('zp', 'core'), axis=0, tiled=False)  9.9 us
    all_to_all x1, starting transfers between devices, body(): gws = lax.all_to_all(gw, 'grp', 0, 0, tiled=False)  6.72 us
    all_to_all x1, waiting for transfers between devices, body(): part = lax.all_to_all(packed, 'z8', 0, 0, tiled=False)  4.45 us
    pallas_call x1, Pallas kernels, body(): kernel(peer_kernel, 'peer', (shape(2, VEC, T), square, square, shape(VEC,...  4.08 us
    pallas_call x1, Pallas kernels, body(): pl.pallas_call(up_kernel, out_shape=(shape(ROWS, n), shape(n_z8, PACK, HA...  3.95 us
    ppermute x1, starting transfers between devices, body(): other = lax.ppermute(part, 'zp', swap)  3.51 us
    all_to_all x1, waiting for transfers between devices, body(): gws = lax.all_to_all(gw, 'grp', 0, 0, tiled=False)  3.45 us
  transfers between devices with their start and end apart: 5, of which 2 were waited for; matrix products, arithmetic and copies ran while one was open for 0% of the time, Pallas kernels for 15%

profile of v6, /device:TPU:1, one launch (start us, length us, event | category | flops | bytes accessed | tf_op | source)
XLA Modules:
  0.0 65.5 jit_solution(8105466140420102599)
XLA Ops:
  0.0 4.0 %up.1 = (f32[24,1024]{1,0:T(8,128)}, f32[8,40,128]{2,1,0:T(8,128)}) custom-call(f32[3,1024]{1,0:T(4,128)} %pts_hbm.1, f32[16,1024]{1,0:T(8,128)} %chg_hbm.1, s32[1,1024]{1,0:T(1,128)} %bitcast.3, f32[3,1024]{1,0:T(4,128)} %skl_ref.1, f32[3,256]{1,0:T(4,128)} %skb_ref.3), custom_call_target="tpu_custom_call" | custom-call | tf_op jit(solution)/shard_map/up/pallas_call | solution.py:280
  4.0 0.0 copy-start
  4.0 0.0 copy-start.1
  4.0 15.8 %all-to-all-start = ((f32[8,40,128]{2,1,0:T(8,128)}), f32[8,40,128]{2,1,0:T(8,128)S(1)}, u32[]{:S(2)}, u32[]{:S(2)}) async-start(f32[8,40,128]{2,1,0:T(8,128)} %get-tuple-element.21), calls=%async_computation | async-start | bytes 327680 | tf_op jit(solution)/shard_map/all_to_all | solution.py:289
  19.8 0.0 copy-start.4
  19.8 0.0 copy-start.5
  19.8 2.9 %collective-permute-start = (f32[24,1024]{1,0:T(8,128)S(1)}, f32[24,1024]{1,0:T(8,128)S(1)}, u32[]{:S(2)}, u32[]{:S(2)}) collective-permute-start(f32[24,1024]{1,0:T(8,128)S(1)} %copy-done.2), channel_id=1, source_target_pairs={{0,1},{1,0},{2,3},{3,2},{4,5},{5,4},{6,7},{7,6},{8,9},{9,8},{10,11... | collective-permute-start | bytes 294920 | tf_op jit(solution)/shard_map/ppermute | solution.py:292
  22.7 0.0 copy-done
  22.7 1.2 %pre.1 = (bf16[256,1024]{1,0:T(8,128)(2,1)S(1)}, bf16[256,1024]{1,0:T(8,128)(2,1)S(1)}) custom-call(f32[3,256]{1,0:T(4,128)S(1)} %copy-done.1, f32[3,1024]{1,0:T(4,128)S(1)} %copy-done, f32[24,1024]{1,0:T(8,128)S(1)} %copy-done.2), custom_call_target="tpu_custom_call" | custom-call | flops 1200000000 | bytes 3145728 | tf_op jit(solution)/shard_map/pre/pallas_call | solution.py:294
  23.9 0.0 copy-start.3
  23.9 0.0 collective-permute-done.sib_ref.sibling_ref
  23.9 2.7 %near.1.near_ref = f32[16,1024]{1,0:T(8,128)S(1)} custom-call(s32[4,8]{1,0:T(4,128)S(1)} %copy-done.4, s32[4]{0:T(128)S(1)} %copy-done.5, f32[24,1024]{1,0:T(8,128)S(1)} %collective-permute-done.sib_ref.sibling_ref, f32[24,1024]{1,0:T(8,128)S(1)} %copy-done.2), custom_call_target="tpu_custom_call" | custom-call | flops 2600000000 | bytes 6815744 | tf_op jit(solution)/shard_map/near/pallas_call | solution.py:295
  26.6 2.6 %collective-permute-start.2 = (f32[24,1024]{1,0:T(8,128)S(1)}, f32[24,1024]{1,0:T(8,128)S(1)}, u32[]{:S(2)}, u32[]{:S(2)}) collective-permute-start(f32[24,1024]{1,0:T(8,128)S(1)} %copy-done.2), channel_id=1, source_target_pairs={{1,2},{3,4},{5,6},{7,8},{9,10},{11,12},{13,14},{15,16},{17,18},{19... | collective-permute-start | bytes 294920 | tf_op jit(solution)/shard_map/ppermute | solution.py:298
  29.2 4.4 %all-to-all-done.part_ref = f32[8,40,128]{2,1,0:T(8,128)S(1)} async-done(((f32[8,40,128]{2,1,0:T(8,128)}), f32[8,40,128]{2,1,0:T(8,128)S(1)}, u32[]{:S(2)}, u32[]{:S(2)}) %all-to-all-start) | async-done | bytes 163872 | tf_op jit(solution)/shard_map/all_to_all | solution.py:289
  33.6 3.5 %collective-permute-start.1 = (f32[8,40,128]{2,1,0:T(8,128)S(1)}, f32[8,40,128]{2,1,0:T(8,128)S(1)}, u32[]{:S(2)}, u32[]{:S(2)}) collective-permute-start(f32[8,40,128]{2,1,0:T(8,128)S(1)} %all-to-all-done.part_ref), channel_id=1, source_target_pairs={{0,2},{2,0},{1,3},{3,1},{4,6},{6,4},{5,7},{7,5},{8,10},{10,8},{9,1... | collective-permute-start | bytes 491528 | tf_op jit(solution)/shard_map/ppermute | solution.py:300
  37.2 1.6 %group.1 = f32[16,16,256]{2,1,0:T(8,128)} custom-call(f32[8,40,128]{2,1,0:T(8,128)S(1)} %all-to-all-done.part_ref, f32[3,4096]{1,0:T(4,128)S(1)} %copy-done.3), custom_call_target="tpu_custom_call" | custom-call | flops 3000000000 | bytes 7864320 | tf_op jit(solution)/shard_map/group/pallas_call | solution.py:301
  38.8 6.7 %all-to-all-start.1 = ((f32[16,16,256]{2,1,0:T(8,128)}), f32[16,16,256]{2,1,0:T(8,128)S(1)}, u32[]{:S(2)}, u32[]{:S(2)}) async-start(f32[16,16,256]{2,1,0:T(8,128)} %group.1), calls=%async_computation.1 | async-start | bytes 524288 | tf_op jit(solution)/shard_map/all_to_all | solution.py:302
  45.5 0.0 collective-permute-done.2.adj_ref
  45.5 0.0 collective-permute-done.1.other_ref
  45.5 4.1 %peer.1 = (f32[2,16,256]{2,1,0:T(8,128)S(1)}, bf16[256,256]{1,0:T(8,128)(2,1)S(1)}, bf16[256,256]{1,0:T(8,128)(2,1)S(1)}, f32[16,1024]{1,0:T(8,128)S(1)}) custom-call(s32[4,8]{1,0:T(4,128)S(1)} %copy-done.4, s32[4]{0:T(128)S(1)} %copy-done.5, f32[8,40,128]{2,1,0:T(8,128)S(1)} %all-to-all-done.part_ref, f32[8,40,128]{2,1,0:T(8,128)S(1)} %collective-permute-done.1.other_ref, ...), custom_call_target="tpu_custom_call" | custom-call | flops 4300000256 | bytes 11272192 | tf_op jit(solution)/shard_map/peer/pallas_call | solution.py:304
  49.6 3.4 %all-to-all-done.1.gws_ref = f32[16,16,256]{2,1,0:T(8,128)S(1)} async-done(((f32[16,16,256]{2,1,0:T(8,128)}), f32[16,16,256]{2,1,0:T(8,128)S(1)}, u32[]{:S(2)}, u32[]{:S(2)}) %all-to-all-start.1) | async-done | bytes 262176 | tf_op jit(solution)/shard_map/all_to_all | solution.py:302
  53.0 1.4 %field.1 = f32[32,256]{1,0:T(8,128)S(1)} custom-call(f32[16,16,256]{2,1,0:T(8,128)S(1)} %all-to-all-done.1.gws_ref, f32[3,4096]{1,0:T(4,128)S(1)} %copy-done.3, f32[2,16,256]{2,1,0:T(8,128)S(1)} %get-tuple-element.31.peer_ref), custom_call_target="tpu_custom_call" | custom-call | flops 2000000000 | bytes 5242880 | tf_op jit(solution)/shard_map/field/pallas_call | solution.py:307
  54.5 9.9 %all-gather = f32[128,256]{1,0:T(8,128)S(1)} all-gather(f32[32,256]{1,0:T(8,128)S(1)} %field.1), channel_id=2, replica_groups=mesh['grp'=16,'z8'=8,'zp'=2,'core'=2] {'zp','core'}, dimensions={0}, use_global_device_ids=true | all-gather | bytes 163840 | tf_op jit(solution)/shard_map/all_gather | solution.py:308
  64.4 1.1 %down.1 = f32[16,1024]{1,0:T(8,128)} custom-call(f32[4,32,256]{2,1,0:T(8,128)S(1)} %bitcast.2, f32[2,16,256]{2,1,0:T(8,128)S(1)} %get-tuple-element.31.peer_ref, bf16[256,256]{1,0:T(8,128)(2,1)S(1)} %get-tuple-element.32.bh_ref, bf16[256,256]{1,0:T(8,128)(2,1)S(1)} %get-tuple-element.33.bl_ref, bf16[256,1024]{1,0:T(8,128)(2,1)S(1)} %get-tuple-element.34.mh_ref, ...), custom_call_target="tpu_custom_call" | custom-call | flops 100000000 | bytes 262144 | tf_op jit(solution)/shard_map/down/pallas_call | solution.py:309
  (6 shorter events, 0.0 us)
Async XLA Ops:
  4.0 15.8 %copy-start.2 = (f32[24,1024]{1,0:T(8,128)S(1)}, f32[24,1024]{1,0:T(8,128)}, u32[]{:S(2)}) copy-start(f32[24,1024]{1,0:T(8,128)} %get-tuple-element.29.mid_ref) | copy-start | bytes 294916
  4.0 18.7 %copy-start = (f32[3,1024]{1,0:T(4,128)S(1)}, f32[3,1024]{1,0:T(4,128)}, u32[]{:S(2)}) copy-start(f32[3,1024]{1,0:T(4,128)} %skl_ref.1) | copy-start | bytes 36868
  4.0 18.7 %copy-start.1 = (f32[3,256]{1,0:T(4,128)S(1)}, f32[3,256]{1,0:T(4,128)}, u32[]{:S(2)}) copy-start(f32[3,256]{1,0:T(4,128)} %skb_ref.3) | copy-start | bytes 9220
  4.0 29.6 %all-to-all-start = ((f32[8,40,128]{2,1,0:T(8,128)}), f32[8,40,128]{2,1,0:T(8,128)S(1)}, u32[]{:S(2)}, u32[]{:S(2)}) async-start(f32[8,40,128]{2,1,0:T(8,128)} %get-tuple-element.21), calls=%async_computation | async-start | bytes 327680 | tf_op jit(solution)/shard_map/all_to_all | solution.py:289
  19.8 4.1 %copy-start.4 = (s32[4,8]{1,0:T(4,128)S(1)}, s32[4,8]{1,0:T(4,128)}, u32[]{:S(2)}) copy-start(s32[4,8]{1,0:T(4,128)} %nbr_ref.3) | copy-start | bytes 388
  19.8 4.1 %copy-start.5 = (s32[4]{0:T(128)S(1)}, s32[4]{0:T(128)}, u32[]{:S(2)}) copy-start(s32[4]{0:T(128)} %cnt_ref.3) | copy-start | bytes 52
  19.8 4.1 %collective-permute-start = (f32[24,1024]{1,0:T(8,128)S(1)}, f32[24,1024]{1,0:T(8,128)S(1)}, u32[]{:S(2)}, u32[]{:S(2)}) collective-permute-start(f32[24,1024]{1,0:T(8,128)S(1)} %copy-done.2), channel_id=1, source_target_pairs={{0,1},{1,0},{2,3},{3,2},{4,5},{5,4},{6,7},{7,6},{8,9},{9,8},{10,11... | collective-permute-start | bytes 294920 | tf_op jit(solution)/shard_map/ppermute | solution.py:292
  23.9 13.3 %copy-start.3 = (f32[3,4096]{1,0:T(4,128)S(1)}, f32[3,4096]{1,0:T(4,128)}, u32[]{:S(2)}) copy-start(f32[3,4096]{1,0:T(4,128)} %skg_ref.5) | copy-start | bytes 147460
  26.6 18.9 %collective-permute-start.2 = (f32[24,1024]{1,0:T(8,128)S(1)}, f32[24,1024]{1,0:T(8,128)S(1)}, u32[]{:S(2)}, u32[]{:S(2)}) collective-permute-start(f32[24,1024]{1,0:T(8,128)S(1)} %copy-done.2), channel_id=1, source_target_pairs={{1,2},{3,4},{5,6},{7,8},{9,10},{11,12},{13,14},{15,16},{17,18},{19... | collective-permute-start | bytes 294920 | tf_op jit(solution)/shard_map/ppermute | solution.py:298
  33.6 11.9 %collective-permute-start.1 = (f32[8,40,128]{2,1,0:T(8,128)S(1)}, f32[8,40,128]{2,1,0:T(8,128)S(1)}, u32[]{:S(2)}, u32[]{:S(2)}) collective-permute-start(f32[8,40,128]{2,1,0:T(8,128)S(1)} %all-to-all-done.part_ref), channel_id=1, source_target_pairs={{0,2},{2,0},{1,3},{3,1},{4,6},{6,4},{5,7},{7,5},{8,10},{10,8},{9,1... | collective-permute-start | bytes 491528 | tf_op jit(solution)/shard_map/ppermute | solution.py:300
  38.8 14.3 %all-to-all-start.1 = ((f32[16,16,256]{2,1,0:T(8,128)}), f32[16,16,256]{2,1,0:T(8,128)S(1)}, u32[]{:S(2)}, u32[]{:S(2)}) async-start(f32[16,16,256]{2,1,0:T(8,128)} %group.1), calls=%async_computation.1 | async-start | bytes 524288 | tf_op jit(solution)/shard_map/all_to_all | solution.py:302

commit v7 on v6

--- a/solution.py
+++ b/solution.py
@@ -85,35 +85,43 @@
 
 
 def up_kernel(pts_hbm, chg_hbm, mor_hbm, skl_hbm, skb_hbm, srt_ref, pack_ref, *scratch):
-    pts_ref, chg_ref, mor_ref, skl_ref, skb_ref, sems = scratch
-    copies = [
-        pltpu.make_async_copy(src, dst, sems.at[i])
-        for i, (src, dst) in enumerate(
-            ((skl_hbm, skl_ref), (skb_hbm, skb_ref), (pts_hbm, pts_ref), (mor_hbm, mor_ref), (chg_hbm, chg_ref))
-        )
-    ]
+    pts_ref, chg_ref, mor_ref, skl_ref, skb_ref, kh_ref, kl_ref, sems = scratch
+    pairs = ((skl_hbm, skl_ref), (skb_hbm, skb_ref), (mor_hbm, mor_ref), (pts_hbm, pts_ref), (chg_hbm, chg_ref))
+    copies = [pltpu.make_async_copy(src, dst, sems.at[i]) for i, (src, dst) in enumerate(pairs)]
     for c in copies:
         c.start()
-    for c in copies:
+    copies[0].wait()
+    copies[1].wait()
+    ft_block = feat_tgt(skb_ref[...])
+    for q in range(LEAVES_DEV):
+        col = slice(q * T, (q + 1) * T)
+        kh, kl = tile(feat_src(skl_ref[:, col]), ft_block)
+        kh_ref[col, :] = kh
+        kl_ref[col, :] = kl
+    for c in copies[2:]:
         c.wait()
     n = chg_ref.shape[1]
     rows = jnp.concatenate([chg_ref[...], pts_ref[...], jnp.zeros((5, n), f32)], axis=0)
     a, b, c = split3(rows)
     parts = jnp.concatenate([a, b, c], axis=0).astype(bf16)
     row = lax.broadcasted_iota(jnp.int32, (n, T), 0)
-    ft_block = feat_tgt(skb_ref[...])
-    total = jnp.zeros((VEC, T), f32)
-    for q in range(LEAVES_DEV):
-        col = slice(q * T, (q + 1) * T)
-        skel = skl_ref[:, col]
+    sorts = []
+    for q in range(LEAVES_DEV):
+        col = slice(q * T, (q + 1) * T)
         hot = (row == mor_ref[:, col]).astype(f32).astype(bf16)
         s = dg(parts, hot, 1, 0)
         srt = s[:ROWS] + s[ROWS : 2 * ROWS] + s[2 * ROWS :]
+        if q == 0:
+            srt = jnp.concatenate([srt[: VEC + 3], skb_ref[...], srt[VEC + 6 :]], axis=0)
         srt_ref[:, col] = srt
+        sorts.append(s)
+    total = jnp.zeros((VEC, T), f32)
+    for q in range(LEAVES_DEV):
+        col = slice(q * T, (q + 1) * T)
+        s = sorts[q]
         vv = jnp.concatenate([s[:VEC], s[ROWS : ROWS + VEC] + s[2 * ROWS : 2 * ROWS + VEC]], axis=0).astype(bf16)
-        lw = times(vv, tile(feat_src(srt[VEC : VEC + 3]), feat_tgt(skel)))
-        total = total + times(stack2(gain(T) * lw), tile(feat_src(skel), ft_block))
-    srt_ref[VEC + 3 : VEC + 6, :T] = skb_ref[...]
+        lw = times(vv, tile(feat_src(srt_ref[VEC : VEC + 3, col]), feat_tgt(skl_ref[:, col])))
+        total = total + times(stack2(gain(T) * lw), (kh_ref[col, :], kl_ref[col, :]))
     packed = pack(gain(LEAVES_DEV * T) * total, skb_ref[...])
     for z in range(pack_ref.shape[0]):
         pack_ref[z] = packed
@@ -158,25 +166,31 @@
     return ref[:VEC, col], ref[VEC : VEC + 3, col]
 
 
-def uses(nbr_ref, cnt_ref, q, source):
-    count = jnp.int32(0)
-    for k in range(nbr_ref.shape[1]):
-        hit = jnp.logical_and(nbr_ref[q, k] == source, cnt_ref[q] > k)
-        count = count + hit.astype(jnp.int32)
-    return count
-
-
-def side_near(nbr_ref, cnt_ref, blk_ref, on_right, fts, acc):
+def slots(nbr_ref, cnt_ref):
+    shape = nbr_ref.shape
+    leaves = (shape[0], shape[0])
+    diagonal = lax.broadcasted_iota(jnp.int32, leaves, 0) == lax.broadcasted_iota(jnp.int32, leaves, 1)
+    count = jnp.sum(jnp.where(diagonal, cnt_ref[...].astype(f32), 0.0), axis=1, keepdims=True)
+    used = lax.broadcasted_iota(jnp.int32, shape, 1).astype(f32) < count
+    return jnp.where(used, nbr_ref[...], -(1 << 24))
+
+
+def uses(table, source):
+    return jnp.sum(jnp.where(table == source, 1.0, 0.0), axis=1, keepdims=True)
+
+
+def side_near(table, blk_ref, on_right, fts, acc):
     first = first_leaf() + jnp.where(on_right, LEAVES_DEV, -LEAVES_DEV)
     for d in range(LEAVES_DEV):
         (v0, x0), (v1, x1) = leaf(blk_ref, d), leaf(blk_ref, LEAVES_DEV - 1 - d)
         v = jnp.where(on_right, v0, v1)
         fs = feat_src(jnp.where(on_right, x0, x1))
         source = first + jnp.where(on_right, d, LEAVES_DEV - 1 - d)
+        m = uses(table, source)
         for e in range(d, LEAVES_DEV):
             q0, q1 = e, LEAVES_DEV - 1 - e
-            m = jnp.where(on_right, uses(nbr_ref, cnt_ref, q0, source), uses(nbr_ref, cnt_ref, q1, source))
-            r = times(stack2(m.astype(f32) * v), tile(fs, jnp.where(on_right, fts[q0], fts[q1])))
+            times_used = jnp.where(on_right, m[q0 : q0 + 1], m[q1 : q1 + 1])
+            r = times(stack2(times_used * v), tile(fs, jnp.where(on_right, fts[q0], fts[q1])))
             acc[q0] = acc[q0] + jnp.where(on_right, r, 0.0)
             acc[q1] = acc[q1] + jnp.where(on_right, 0.0, r)
 
@@ -184,16 +198,17 @@
 def near_kernel(nbr_ref, cnt_ref, sib_ref, mid_ref, near_ref):
     on_right = lax.axis_index("core") == 0
     first = first_leaf()
+    table = slots(nbr_ref, cnt_ref)
     fts = [feat_tgt(leaf(mid_ref, q)[1]) for q in range(LEAVES_DEV)]
     acc = [jnp.zeros((VEC, T), f32) for _ in range(LEAVES_DEV)]
     for j in range(LEAVES_DEV):
         v, x = leaf(mid_ref, j)
         fs = feat_src(x)
+        m = uses(table, first + j)
         for q in range(LEAVES_DEV):
-            m = 1 if j == q else uses(nbr_ref, cnt_ref, q, first + j)
-            vv = stack2(v if j == q else m.astype(f32) * v)
+            vv = stack2(v if j == q else m[q : q + 1] * v)
             acc[q] = acc[q] + times(vv, tile(fs, fts[q]))
-    side_near(nbr_ref, cnt_ref, sib_ref, on_right, fts, acc)
+    side_near(table, sib_ref, on_right, fts, acc)
     for q in range(LEAVES_DEV):
         near_ref[:, q * T : (q + 1) * T] = gain(T) * acc[q]
 
@@ -221,7 +236,7 @@
     bl_ref[...] = kl
     fts = [feat_tgt(leaf(mid_ref, q)[1]) for q in range(LEAVES_DEV)]
     acc = [jnp.zeros((VEC, T), f32) for _ in range(LEAVES_DEV)]
-    side_near(nbr_ref, cnt_ref, adj_ref, lax.axis_index("core") == 1, fts, acc)
+    side_near(slots(nbr_ref, cnt_ref), adj_ref, lax.axis_index("core") == 1, fts, acc)
     for q in range(LEAVES_DEV):
         col = slice(q * T, (q + 1) * T)
         all_ref[:, col] = near_ref[:, col] + gain(T) * acc[q]
@@ -276,13 +291,15 @@
     n_z8 = lax.axis_size("z8")
     n = points.shape[1]
     axes = ("grp", "z8", "zp", "core")
+    counts = counts.reshape(1, LEAVES_DEV)
     inputs = (points, charges, morton.reshape(1, n), skel_leaf, skel_block)
     srt, packed = pl.pallas_call(
         up_kernel,
         out_shape=(shape(ROWS, n), shape(n_z8, PACK, HALF)),
         in_specs=[pl.BlockSpec(memory_space=pltpu.HBM)] * 5,
         out_specs=(VM, VM),
-        scratch_shapes=[pltpu.VMEM(x.shape, x.dtype) for x in inputs] + [pltpu.SemaphoreType.DMA((5,))],
+        scratch_shapes=[pltpu.VMEM(x.shape, x.dtype) for x in inputs]
+        + [pltpu.VMEM((n, T), bf16), pltpu.VMEM((n, T), bf16), pltpu.SemaphoreType.DMA((5,))],
         compiler_params=pltpu.CompilerParams(vmem_limit_bytes=60 << 20),
         name="up",
     )(*inputs)
@@ -292,7 +309,7 @@
     sib = lax.ppermute(srt, "core", swap)
     half_shape = shape(T, n, dtype=bf16)
     mh, ml = kernel(pre_kernel, "pre", (half_shape, half_shape), 0, 3, tiles=12)(skel_block, skel_leaf, srt)
-    near = kernel(near_kernel, "near", shape(VEC, n), 2, 2, tiles=26)(neighbours, counts, sib, srt)
+    near = kernel(near_kernel, "near", shape(VEC, n), 0, 4, tiles=26)(neighbours, counts, sib, srt)
     srt, near, mh, ml = lax.optimization_barrier((srt, near, mh, ml))
     odd = range(1, whole - 1, 2)
     adj = lax.ppermute(srt, axes, [(i, i + 1) for i in odd] + [(i + 1, i) for i in odd])
@@ -301,7 +318,7 @@
     gw = kernel(group_kernel, "group", shape(n_groups, VEC, T), 0, 2, tiles=30)(part, skel_group)
     gws = lax.all_to_all(gw, "grp", 0, 0, tiled=False)
     square = shape(T, T, dtype=bf16)
-    peer, bh, bl, near = kernel(peer_kernel, "peer", (shape(2, VEC, T), square, square, shape(VEC, n)), 2, 8, tiles=43)(
+    peer, bh, bl, near = kernel(peer_kernel, "peer", (shape(2, VEC, T), square, square, shape(VEC, n)), 0, 10, tiles=43)(
         neighbours, counts, part, other, skel_block, sib, skel_group, adj, srt, near
     )
     mine = kernel(field_kernel, "field", shape(2 * VEC, T), 0, 3, tiles=20)(gws, skel_group, peer)

time: 65.9 us -> 65.3 us (level)
  Pallas kernels: 16 us -> 14.5 us
  transfers between devices with their start and end apart: 5 -> 5, of which waited for: 2 -> 2; matrix products, arithmetic and copies ran while one was open for 0% -> 0% of each run, Pallas kernels for 15% -> 13%
where the time goes in v7:
time: 65.3 us; the launch traced here: 64.9 us
  starting transfers between devices  31.5 us (48%)
  Pallas kernels  14.5 us (22%)
  blocking collectives  9.76 us (15%)
  waiting for transfers between devices  8.38 us (13%)
  local copies, waits for them, and re-layouts  0.66 us (1%)
    all_to_all x1, starting transfers between devices, body(): part = lax.all_to_all(packed, 'z8', 0, 0, tiled=False)  15.8 us
    all_gather x1, blocking collectives, body(): cell = lax.all_gather(mine, ('zp', 'core'), axis=0, tiled=False)  9.76 us
    all_to_all x1, starting transfers between devices, body(): gws = lax.all_to_all(gw, 'grp', 0, 0, tiled=False)  6.75 us
    all_to_all x1, waiting for transfers between devices, body(): part = lax.all_to_all(packed, 'z8', 0, 0, tiled=False)  4.38 us
    all_to_all x1, waiting for transfers between devices, body(): gws = lax.all_to_all(gw, 'grp', 0, 0, tiled=False)  3.99 us
    pallas_call x1, Pallas kernels, body(): kernel(peer_kernel, 'peer', (shape(2, VEC, T), square, square, shape(VEC,...  3.53 us
    ppermute x1, starting transfers between devices, body(): other = lax.ppermute(part, 'zp', swap)  3.51 us
    pallas_call x1, Pallas kernels, body(): pl.pallas_call(up_kernel, out_shape=(shape(ROWS, n), shape(n_z8, PACK, HA...  3.46 us
  transfers between devices with their start and end apart: 5, of which 2 were waited for; matrix products, arithmetic and copies ran while one was open for 0% of the time, Pallas kernels for 13%

profile of v7, /device:TPU:1, one launch (start us, length us, event | category | flops | bytes accessed | tf_op | source)
XLA Modules:
  0.0 64.9 jit_solution(10861465504223691170)
XLA Ops:
  0.0 3.5 %up.1 = (f32[24,1024]{1,0:T(8,128)}, f32[8,40,128]{2,1,0:T(8,128)}) custom-call(f32[3,1024]{1,0:T(4,128)} %pts_hbm.1, f32[16,1024]{1,0:T(8,128)} %chg_hbm.1, s32[1,1024]{1,0:T(1,128)} %bitcast.6, f32[3,1024]{1,0:T(4,128)} %skl_ref.1, f32[3,256]{1,0:T(4,128)} %skb_ref.3), custom_call_target="tpu_custom_call" | custom-call | tf_op jit(solution)/shard_map/up/pallas_call | solution.py:296
  3.5 0.0 copy-start
  3.5 0.0 copy-start.1
  3.5 15.8 %all-to-all-start = ((f32[8,40,128]{2,1,0:T(8,128)}), f32[8,40,128]{2,1,0:T(8,128)S(1)}, u32[]{:S(2)}, u32[]{:S(2)}) async-start(f32[8,40,128]{2,1,0:T(8,128)} %get-tuple-element.21), calls=%async_computation | async-start | bytes 327680 | tf_op jit(solution)/shard_map/all_to_all | solution.py:306
  19.3 0.0 copy-done.2
  19.3 0.0 copy-start.4
  19.3 2.9 %collective-permute-start = (f32[24,1024]{1,0:T(8,128)S(1)}, f32[24,1024]{1,0:T(8,128)S(1)}, u32[]{:S(2)}, u32[]{:S(2)}) collective-permute-start(f32[24,1024]{1,0:T(8,128)S(1)} %copy-done.2), channel_id=1, source_target_pairs={{0,1},{1,0},{2,3},{3,2},{4,5},{5,4},{6,7},{7,6},{8,9},{9,8},{10,11... | collective-permute-start | bytes 294920 | tf_op jit(solution)/shard_map/ppermute | solution.py:309
  22.2 1.2 %pre.1 = (bf16[256,1024]{1,0:T(8,128)(2,1)S(1)}, bf16[256,1024]{1,0:T(8,128)(2,1)S(1)}) custom-call(f32[3,256]{1,0:T(4,128)S(1)} %copy-done.1, f32[3,1024]{1,0:T(4,128)S(1)} %copy-done, f32[24,1024]{1,0:T(8,128)S(1)} %copy-done.2), custom_call_target="tpu_custom_call" | custom-call | flops 1200000000 | bytes 3145728 | tf_op jit(solution)/shard_map/pre/pallas_call | solution.py:311
  23.4 0.0 copy-start.5
  23.4 0.0 collective-permute-done.sib_ref.sibling_ref
  23.4 0.6 copy-done.5
  24.1 2.1 %near.1.near_ref = f32[16,1024]{1,0:T(8,128)S(1)} custom-call(s32[4,8]{1,0:T(4,128)S(1)} %copy-done.4, s32[1,4]{1,0:T(1,128)S(1)} %bitcast.4, f32[24,1024]{1,0:T(8,128)S(1)} %collective-permute-done.sib_ref.sibling_ref, f32[24,1024]{1,0:T(8,128)S(1)} %copy-done.2), custom_call_target="tpu_custom_call" | custom-call | flops 2600000000 | bytes 6815744 | tf_op jit(solution)/shard_map/near/pallas_call | solution.py:312
  26.2 2.5 %collective-permute-start.2 = (f32[24,1024]{1,0:T(8,128)S(1)}, f32[24,1024]{1,0:T(8,128)S(1)}, u32[]{:S(2)}, u32[]{:S(2)}) collective-permute-start(f32[24,1024]{1,0:T(8,128)S(1)} %copy-done.2), channel_id=1, source_target_pairs={{1,2},{3,4},{5,6},{7,8},{9,10},{11,12},{13,14},{15,16},{17,18},{19... | collective-permute-start | bytes 294920 | tf_op jit(solution)/shard_map/ppermute | solution.py:315
  28.8 4.4 %all-to-all-done.part_ref = f32[8,40,128]{2,1,0:T(8,128)S(1)} async-done(((f32[8,40,128]{2,1,0:T(8,128)}), f32[8,40,128]{2,1,0:T(8,128)S(1)}, u32[]{:S(2)}, u32[]{:S(2)}) %all-to-all-start) | async-done | bytes 163872 | tf_op jit(solution)/shard_map/all_to_all | solution.py:306
  33.1 3.5 %collective-permute-start.1 = (f32[8,40,128]{2,1,0:T(8,128)S(1)}, f32[8,40,128]{2,1,0:T(8,128)S(1)}, u32[]{:S(2)}, u32[]{:S(2)}) collective-permute-start(f32[8,40,128]{2,1,0:T(8,128)S(1)} %all-to-all-done.part_ref), channel_id=1, source_target_pairs={{0,2},{2,0},{1,3},{3,1},{4,6},{6,4},{5,7},{7,5},{8,10},{10,8},{9,1... | collective-permute-start | bytes 491528 | tf_op jit(solution)/shard_map/ppermute | solution.py:317
  36.7 1.6 %group.1 = f32[16,16,256]{2,1,0:T(8,128)} custom-call(f32[8,40,128]{2,1,0:T(8,128)S(1)} %all-to-all-done.part_ref, f32[3,4096]{1,0:T(4,128)S(1)} %copy-done.3), custom_call_target="tpu_custom_call" | custom-call | flops 3000000000 | bytes 7864320 | tf_op jit(solution)/shard_map/group/pallas_call | solution.py:318
  38.3 6.8 %all-to-all-start.1 = ((f32[16,16,256]{2,1,0:T(8,128)}), f32[16,16,256]{2,1,0:T(8,128)S(1)}, u32[]{:S(2)}, u32[]{:S(2)}) async-start(f32[16,16,256]{2,1,0:T(8,128)} %group.1), calls=%async_computation.1 | async-start | bytes 524288 | tf_op jit(solution)/shard_map/all_to_all | solution.py:319
  45.0 0.0 collective-permute-done.2.adj_ref
  45.1 0.0 collective-permute-done.1.other_ref
  45.1 3.5 %peer.1 = (f32[2,16,256]{2,1,0:T(8,128)S(1)}, bf16[256,256]{1,0:T(8,128)(2,1)S(1)}, bf16[256,256]{1,0:T(8,128)(2,1)S(1)}, f32[16,1024]{1,0:T(8,128)S(1)}) custom-call(s32[4,8]{1,0:T(4,128)S(1)} %copy-done.4, s32[1,4]{1,0:T(1,128)S(1)} %bitcast.5, f32[8,40,128]{2,1,0:T(8,128)S(1)} %all-to-all-done.part_ref, ...), custom_call_target="tpu_custom_call" | custom-call | flops 4300000256 | bytes 11272192 | tf_op jit(solution)/shard_map/peer/pallas_call | solution.py:321
  48.6 4.0 %all-to-all-done.1.gws_ref = f32[16,16,256]{2,1,0:T(8,128)S(1)} async-done(((f32[16,16,256]{2,1,0:T(8,128)}), f32[16,16,256]{2,1,0:T(8,128)S(1)}, u32[]{:S(2)}, u32[]{:S(2)}) %all-to-all-start.1) | async-done | bytes 262176 | tf_op jit(solution)/shard_map/all_to_all | solution.py:319
  52.6 1.4 %field.1 = f32[32,256]{1,0:T(8,128)S(1)} custom-call(f32[16,16,256]{2,1,0:T(8,128)S(1)} %all-to-all-done.1.gws_ref, f32[3,4096]{1,0:T(4,128)S(1)} %copy-done.3, f32[2,16,256]{2,1,0:T(8,128)S(1)} %get-tuple-element.31.peer_ref), custom_call_target="tpu_custom_call" | custom-call | flops 2000000000 | bytes 5242880 | tf_op jit(solution)/shard_map/field/pallas_call | solution.py:324
  54.0 9.8 %all-gather = f32[128,256]{1,0:T(8,128)S(1)} all-gather(f32[32,256]{1,0:T(8,128)S(1)} %field.1), channel_id=2, replica_groups=mesh['grp'=16,'z8'=8,'zp'=2,'core'=2] {'zp','core'}, dimensions={0}, use_global_device_ids=true | all-gather | bytes 163840 | tf_op jit(solution)/shard_map/all_gather | solution.py:325
  63.8 1.1 %down.1 = f32[16,1024]{1,0:T(8,128)} custom-call(f32[4,32,256]{2,1,0:T(8,128)S(1)} %bitcast.3, f32[2,16,256]{2,1,0:T(8,128)S(1)} %get-tuple-element.31.peer_ref, bf16[256,256]{1,0:T(8,128)(2,1)S(1)} %get-tuple-element.32.bh_ref, bf16[256,256]{1,0:T(8,128)(2,1)S(1)} %get-tuple-element.33.bl_ref, bf16[256,1024]{1,0:T(8,128)(2,1)S(1)} %get-tuple-element.34.mh_ref, ...), custom_call_target="tpu_custom_call" | custom-call | flops 100000000 | bytes 262144 | tf_op jit(solution)/shard_map/down/pallas_call | solution.py:326
  (6 shorter events, 0.0 us)
Async XLA Ops:
  3.5 15.8 %copy-start.2 = (f32[24,1024]{1,0:T(8,128)S(1)}, f32[24,1024]{1,0:T(8,128)}, u32[]{:S(2)}) copy-start(f32[24,1024]{1,0:T(8,128)} %get-tuple-element.29.mid_ref) | copy-start | bytes 294916
  3.5 18.7 %copy-start = (f32[3,1024]{1,0:T(4,128)S(1)}, f32[3,1024]{1,0:T(4,128)}, u32[]{:S(2)}) copy-start(f32[3,1024]{1,0:T(4,128)} %skl_ref.1) | copy-start | bytes 36868
  3.5 18.7 %copy-start.1 = (f32[3,256]{1,0:T(4,128)S(1)}, f32[3,256]{1,0:T(4,128)}, u32[]{:S(2)}) copy-start(f32[3,256]{1,0:T(4,128)} %skb_ref.3) | copy-start | bytes 9220
  3.5 29.6 %all-to-all-start = ((f32[8,40,128]{2,1,0:T(8,128)}), f32[8,40,128]{2,1,0:T(8,128)S(1)}, u32[]{:S(2)}, u32[]{:S(2)}) async-start(f32[8,40,128]{2,1,0:T(8,128)} %get-tuple-element.21), calls=%async_computation | async-start | bytes 327680 | tf_op jit(solution)/shard_map/all_to_all | solution.py:306
  19.3 4.1 %copy-start.4 = (s32[4,8]{1,0:T(4,128)S(1)}, s32[4,8]{1,0:T(4,128)}, u32[]{:S(2)}) copy-start(s32[4,8]{1,0:T(4,128)} %nbr_ref.3) | copy-start | bytes 388
  19.3 4.1 %collective-permute-start = (f32[24,1024]{1,0:T(8,128)S(1)}, f32[24,1024]{1,0:T(8,128)S(1)}, u32[]{:S(2)}, u32[]{:S(2)}) collective-permute-start(f32[24,1024]{1,0:T(8,128)S(1)} %copy-done.2), channel_id=1, source_target_pairs={{0,1},{1,0},{2,3},{3,2},{4,5},{5,4},{6,7},{7,6},{8,9},{9,8},{10,11... | collective-permute-start | bytes 294920 | tf_op jit(solution)/shard_map/ppermute | solution.py:309
  23.4 0.7 %copy-start.5 = (s32[4]{0:T(128)S(1)}, s32[4]{0:T(128)}, u32[]{:S(2)}) copy-start(s32[4]{0:T(128)} %param.12) | copy-start | bytes 52
  24.1 12.6 %copy-start.3 = (f32[3,4096]{1,0:T(4,128)S(1)}, f32[3,4096]{1,0:T(4,128)}, u32[]{:S(2)}) copy-start(f32[3,4096]{1,0:T(4,128)} %skg_ref.5) | copy-start | bytes 147460
  26.2 18.8 %collective-permute-start.2 = (f32[24,1024]{1,0:T(8,128)S(1)}, f32[24,1024]{1,0:T(8,128)S(1)}, u32[]{:S(2)}, u32[]{:S(2)}) collective-permute-start(f32[24,1024]{1,0:T(8,128)S(1)} %copy-done.2), channel_id=1, source_target_pairs={{1,2},{3,4},{5,6},{7,8},{9,10},{11,12},{13,14},{15,16},{17,18},{19... | collective-permute-start | bytes 294920 | tf_op jit(solution)/shard_map/ppermute | solution.py:315
  33.1 11.9 %collective-permute-start.1 = (f32[8,40,128]{2,1,0:T(8,128)S(1)}, f32[8,40,128]{2,1,0:T(8,128)S(1)}, u32[]{:S(2)}, u32[]{:S(2)}) collective-permute-start(f32[8,40,128]{2,1,0:T(8,128)S(1)} %all-to-all-done.part_ref), channel_id=1, source_target_pairs={{0,2},{2,0},{1,3},{3,1},{4,6},{6,4},{5,7},{7,5},{8,10},{10,8},{9,1... | collective-permute-start | bytes 491528 | tf_op jit(solution)/shard_map/ppermute | solution.py:317
  38.3 14.3 %all-to-all-start.1 = ((f32[16,16,256]{2,1,0:T(8,128)}), f32[16,16,256]{2,1,0:T(8,128)S(1)}, u32[]{:S(2)}, u32[]{:S(2)}) async-start(f32[16,16,256]{2,1,0:T(8,128)} %group.1), calls=%async_computation.1 | async-start | bytes 524288 | tf_op jit(solution)/shard_map/all_to_all | solution.py:319

commit v8 on v7

--- a/solution.py
+++ b/solution.py
@@ -144,16 +144,6 @@
     total = gain(4 * part_ref.shape[0] * T) * raised(part_ref, skg_ref)
     for g in range(gw_ref.shape[0]):
         gw_ref[g] = total
-
-
-def pre_kernel(skb_ref, skl_ref, mid_ref, mh_ref, ml_ref):
-    fs_block = feat_src(skb_ref[...])
-    for q in range(LEAVES_DEV):
-        col = slice(q * T, (q + 1) * T)
-        ah, al = tile(fs_block, feat_tgt(skl_ref[:, col]))
-        bh, bl = tile(feat_src(skl_ref[:, col]), feat_tgt(mid_ref[VEC : VEC + 3, col]))
-        both = dg(ah, bh, 1, 0) + dg(al, bh, 1, 0) + dg(ah, bl, 1, 0)
-        mh_ref[:, col], ml_ref[:, col] = split2(gain(T) * gain(T) * both)
 
 
 def first_leaf():
@@ -195,11 +185,17 @@
             acc[q1] = acc[q1] + jnp.where(on_right, 0.0, r)
 
 
-def near_kernel(nbr_ref, cnt_ref, sib_ref, mid_ref, near_ref):
-    on_right = lax.axis_index("core") == 0
+def near_kernel(nbr_ref, cnt_ref, mid_ref, skb_ref, skl_ref, near_ref, mh_ref, ml_ref):
     first = first_leaf()
     table = slots(nbr_ref, cnt_ref)
     fts = [feat_tgt(leaf(mid_ref, q)[1]) for q in range(LEAVES_DEV)]
+    fs_block = feat_src(skb_ref[...])
+    for q in range(LEAVES_DEV):
+        col = slice(q * T, (q + 1) * T)
+        ah, al = tile(fs_block, feat_tgt(skl_ref[:, col]))
+        bh, bl = tile(feat_src(skl_ref[:, col]), fts[q])
+        both = dg(ah, bh, 1, 0) + dg(al, bh, 1, 0) + dg(ah, bl, 1, 0)
+        mh_ref[:, col], ml_ref[:, col] = split2(gain(T) * gain(T) * both)
     acc = [jnp.zeros((VEC, T), f32) for _ in range(LEAVES_DEV)]
     for j in range(LEAVES_DEV):
         v, x = leaf(mid_ref, j)
@@ -208,7 +204,6 @@
         for q in range(LEAVES_DEV):
             vv = stack2(v if j == q else m[q : q + 1] * v)
             acc[q] = acc[q] + times(vv, tile(fs, fts[q]))
-    side_near(table, sib_ref, on_right, fts, acc)
     for q in range(LEAVES_DEV):
         near_ref[:, q * T : (q + 1) * T] = gain(T) * acc[q]
 
@@ -236,7 +231,9 @@
     bl_ref[...] = kl
     fts = [feat_tgt(leaf(mid_ref, q)[1]) for q in range(LEAVES_DEV)]
     acc = [jnp.zeros((VEC, T), f32) for _ in range(LEAVES_DEV)]
-    side_near(slots(nbr_ref, cnt_ref), adj_ref, lax.axis_index("core") == 1, fts, acc)
+    table = slots(nbr_ref, cnt_ref)
+    side_near(table, sibling_ref, lax.axis_index("core") == 0, fts, acc)
+    side_near(table, adj_ref, lax.axis_index("core") == 1, fts, acc)
     for q in range(LEAVES_DEV):
         col = slice(q * T, (q + 1) * T)
         all_ref[:, col] = near_ref[:, col] + gain(T) * acc[q]
@@ -307,9 +304,10 @@
     whole = n_groups * n_z8 * 4
     swap = [(0, 1), (1, 0)]
     sib = lax.ppermute(srt, "core", swap)
-    half_shape = shape(T, n, dtype=bf16)
-    mh, ml = kernel(pre_kernel, "pre", (half_shape, half_shape), 0, 3, tiles=12)(skel_block, skel_leaf, srt)
-    near = kernel(near_kernel, "near", shape(VEC, n), 0, 4, tiles=26)(neighbours, counts, sib, srt)
+    operator = shape(T, n, dtype=bf16)
+    near, mh, ml = kernel(near_kernel, "near", (shape(VEC, n), operator, operator), 0, 5, tiles=28)(
+        neighbours, counts, srt, skel_block, skel_leaf
+    )
     srt, near, mh, ml = lax.optimization_barrier((srt, near, mh, ml))
     odd = range(1, whole - 1, 2)
     adj = lax.ppermute(srt, axes, [(i, i + 1) for i in odd] + [(i + 1, i) for i in odd])
@@ -318,7 +316,7 @@
     gw = kernel(group_kernel, "group", shape(n_groups, VEC, T), 0, 2, tiles=30)(part, skel_group)
     gws = lax.all_to_all(gw, "grp", 0, 0, tiled=False)
     square = shape(T, T, dtype=bf16)
-    peer, bh, bl, near = kernel(peer_kernel, "peer", (shape(2, VEC, T), square, square, shape(VEC, n)), 0, 10, tiles=43)(
+    peer, bh, bl, near = kernel(peer_kernel, "peer", (shape(2, VEC, T), square, square, shape(VEC, n)), 0, 10, tiles=53)(
         neighbours, counts, part, other, skel_block, sib, skel_group, adj, srt, near
     )
     mine = kernel(field_kernel, "field", shape(2 * VEC, T), 0, 3, tiles=20)(gws, skel_group, peer)

time: 65.3 us -> 65.3 us (level)
    all_to_all x1, waiting for transfers between devices: 4.38 us -> 5.59 us  [body(): part = lax.all_to_all(packed, 'z8', 0, 0, tiled=False)]
    all_to_all x1, waiting for transfers between devices: 3.99 us -> 3.29 us  [body(): gws = lax.all_to_all(gw, 'grp', 0, 0, tiled=False)]
    pallas_call x1, Pallas kernels: 3.53 us -> 4.22 us  [body(): kernel(peer_kernel, 'peer', (shape(2, VEC, T), square, square, shape(VEC,...]
    pallas_call x2 -> x1, Pallas kernels: 3.35 us -> 2.75 us  [body(): kernel(near_kernel, 'near', (shape(VEC, n), operator, operator), 0, 5, ti...]
where the time goes in v8:
time: 65.3 us; the launch traced here: 64.9 us
  starting transfers between devices  31.4 us (48%)
  Pallas kernels  14.6 us (22%)
  blocking collectives  9.81 us (15%)
  waiting for transfers between devices  8.89 us (14%)
    all_to_all x1, starting transfers between devices, body(): part = lax.all_to_all(packed, 'z8', 0, 0, tiled=False)  15.8 us
    all_gather x1, blocking collectives, body(): cell = lax.all_gather(mine, ('zp', 'core'), axis=0, tiled=False)  9.81 us
    all_to_all x1, starting transfers between devices, body(): gws = lax.all_to_all(gw, 'grp', 0, 0, tiled=False)  6.76 us
    all_to_all x1, waiting for transfers between devices, body(): part = lax.all_to_all(packed, 'z8', 0, 0, tiled=False)  5.59 us
    pallas_call x1, Pallas kernels, body(): kernel(peer_kernel, 'peer', (shape(2, VEC, T), square, square, shape(VEC,...  4.22 us
    ppermute x1, starting transfers between devices, body(): other = lax.ppermute(part, 'zp', swap)  3.46 us
    pallas_call x1, Pallas kernels, body(): pl.pallas_call(up_kernel, out_shape=(shape(ROWS, n), shape(n_z8, PACK, HA...  3.46 us
    all_to_all x1, waiting for transfers between devices, body(): gws = lax.all_to_all(gw, 'grp', 0, 0, tiled=False)  3.29 us
  transfers between devices with their start and end apart: 5, of which 2 were waited for; matrix products, arithmetic and copies ran while one was open for 0% of the time, Pallas kernels for 13%

profile of v8, /device:TPU:1, one launch (start us, length us, event | category | flops | bytes accessed | tf_op | source)
XLA Modules:
  0.0 64.9 jit_solution(6067786915649982194)
XLA Ops:
  0.0 3.5 %up.1 = (f32[24,1024]{1,0:T(8,128)}, f32[8,40,128]{2,1,0:T(8,128)}) custom-call(f32[3,1024]{1,0:T(4,128)} %pts_hbm.1, f32[16,1024]{1,0:T(8,128)} %chg_hbm.1, s32[1,1024]{1,0:T(1,128)} %bitcast.6, f32[3,1024]{1,0:T(4,128)} %skl_ref.1, f32[3,256]{1,0:T(4,128)} %skb_ref.3), custom_call_target="tpu_custom_call" | custom-call | tf_op jit(solution)/shard_map/up/pallas_call | solution.py:293
  3.5 0.0 copy-start
  3.5 0.0 copy-start.1
  3.5 15.8 %all-to-all-start = ((f32[8,40,128]{2,1,0:T(8,128)}), f32[8,40,128]{2,1,0:T(8,128)S(1)}, u32[]{:S(2)}, u32[]{:S(2)}) async-start(f32[8,40,128]{2,1,0:T(8,128)} %get-tuple-element.22), calls=%async_computation | async-start | bytes 327680 | tf_op jit(solution)/shard_map/all_to_all | solution.py:303
  19.3 0.0 copy-start.5
  19.3 2.9 %collective-permute-start.1 = (f32[24,1024]{1,0:T(8,128)S(1)}, f32[24,1024]{1,0:T(8,128)S(1)}, u32[]{:S(2)}, u32[]{:S(2)}) collective-permute-start(f32[24,1024]{1,0:T(8,128)S(1)} %copy-done.2), channel_id=1, source_target_pairs={{0,1},{1,0},{2,3},{3,2},{4,5},{5,4},{6,7},{7,6},{8,9},{9,8},{10,11... | collective-permute-start | bytes 294920 | tf_op jit(solution)/shard_map/ppermute | solution.py:306
  22.2 0.0 copy-done
  22.2 0.0 copy-done.1
  22.2 0.0 copy-done.4
  22.2 0.0 copy-start.3
  22.2 2.8 %near.1 = (f32[16,1024]{1,0:T(8,128)S(1)}, bf16[256,1024]{1,0:T(8,128)(2,1)S(1)}, bf16[256,1024]{1,0:T(8,128)(2,1)S(1)}) custom-call(s32[4,8]{1,0:T(4,128)S(1)} %copy-done.4, s32[1,4]{1,0:T(1,128)S(1)} %bitcast.4, f32[24,1024]{1,0:T(8,128)S(1)} %copy-done.2, f32[3,256]{1,0:T(4,128)S(1)} %copy-done.1, f32[3,1024]{1,0:T(4,128)S(1)} %copy-done), custom_call_target="tpu_custom_call" | custom-call | flops 2800000000 | bytes 7340032 | tf_op jit(solution)/shard_map/near/pallas_call | solution.py:308
  25.0 2.5 %collective-permute-start.2 = (f32[24,1024]{1,0:T(8,128)S(1)}, f32[24,1024]{1,0:T(8,128)S(1)}, u32[]{:S(2)}, u32[]{:S(2)}) collective-permute-start(f32[24,1024]{1,0:T(8,128)S(1)} %copy-done.2), channel_id=1, source_target_pairs={{1,2},{3,4},{5,6},{7,8},{9,10},{11,12},{13,14},{15,16},{17,18},{19... | collective-permute-start | bytes 294920 | tf_op jit(solution)/shard_map/ppermute | solution.py:313
  27.5 5.6 %all-to-all-done.part_ref = f32[8,40,128]{2,1,0:T(8,128)S(1)} async-done(((f32[8,40,128]{2,1,0:T(8,128)}), f32[8,40,128]{2,1,0:T(8,128)S(1)}, u32[]{:S(2)}, u32[]{:S(2)}) %all-to-all-start) | async-done | bytes 163872 | tf_op jit(solution)/shard_map/all_to_all | solution.py:303
  33.1 3.5 %collective-permute-start = (f32[8,40,128]{2,1,0:T(8,128)S(1)}, f32[8,40,128]{2,1,0:T(8,128)S(1)}, u32[]{:S(2)}, u32[]{:S(2)}) collective-permute-start(f32[8,40,128]{2,1,0:T(8,128)S(1)} %all-to-all-done.part_ref), channel_id=1, source_target_pairs={{0,2},{2,0},{1,3},{3,1},{4,6},{6,4},{5,7},{7,5},{8,10},{10,8},{9,1... | collective-permute-start | bytes 491528 | tf_op jit(solution)/shard_map/ppermute | solution.py:315
  36.6 1.6 %group.1 = f32[16,16,256]{2,1,0:T(8,128)} custom-call(f32[8,40,128]{2,1,0:T(8,128)S(1)} %all-to-all-done.part_ref, f32[3,4096]{1,0:T(4,128)S(1)} %copy-done.3), custom_call_target="tpu_custom_call" | custom-call | flops 3000000000 | bytes 7864320 | tf_op jit(solution)/shard_map/group/pallas_call | solution.py:316
  38.2 6.8 %all-to-all-start.1 = ((f32[16,16,256]{2,1,0:T(8,128)}), f32[16,16,256]{2,1,0:T(8,128)S(1)}, u32[]{:S(2)}, u32[]{:S(2)}) async-start(f32[16,16,256]{2,1,0:T(8,128)} %group.1), calls=%async_computation.1 | async-start | bytes 524288 | tf_op jit(solution)/shard_map/all_to_all | solution.py:317
  45.0 0.0 collective-permute-done.1.sibling_ref
  45.0 0.0 collective-permute-done.2.adj_ref
  45.0 0.0 collective-permute-done.other_ref
  45.0 4.2 %peer.1 = (f32[2,16,256]{2,1,0:T(8,128)S(1)}, bf16[256,256]{1,0:T(8,128)(2,1)S(1)}, bf16[256,256]{1,0:T(8,128)(2,1)S(1)}, f32[16,1024]{1,0:T(8,128)S(1)}) custom-call(s32[4,8]{1,0:T(4,128)S(1)} %copy-done.4, s32[1,4]{1,0:T(1,128)S(1)} %bitcast.5, f32[8,40,128]{2,1,0:T(8,128)S(1)} %all-to-all-done.part_ref, f32[8,40,128]{2,1,0:T(8,128)S(1)} %collective-permute-done.other_ref, ...), custom_call_target="tpu_custom_call" | custom-call | flops 5299999744 | bytes 13893632 | tf_op jit(solution)/shard_map/peer/pallas_call | solution.py:319
  49.2 3.3 %all-to-all-done.1.gws_ref = f32[16,16,256]{2,1,0:T(8,128)S(1)} async-done(((f32[16,16,256]{2,1,0:T(8,128)}), f32[16,16,256]{2,1,0:T(8,128)S(1)}, u32[]{:S(2)}, u32[]{:S(2)}) %all-to-all-start.1) | async-done | bytes 262176 | tf_op jit(solution)/shard_map/all_to_all | solution.py:317
  52.5 1.4 %field.1 = f32[32,256]{1,0:T(8,128)S(1)} custom-call(f32[16,16,256]{2,1,0:T(8,128)S(1)} %all-to-all-done.1.gws_ref, f32[3,4096]{1,0:T(4,128)S(1)} %copy-done.3, f32[2,16,256]{2,1,0:T(8,128)S(1)} %get-tuple-element.33.peer_ref), custom_call_target="tpu_custom_call" | custom-call | flops 2000000000 | bytes 5242880 | tf_op jit(solution)/shard_map/field/pallas_call | solution.py:322
  54.0 9.8 %all-gather = f32[128,256]{1,0:T(8,128)S(1)} all-gather(f32[32,256]{1,0:T(8,128)S(1)} %field.1), channel_id=2, replica_groups=mesh['grp'=16,'z8'=8,'zp'=2,'core'=2] {'zp','core'}, dimensions={0}, use_global_device_ids=true | all-gather | bytes 163840 | tf_op jit(solution)/shard_map/all_gather | solution.py:323
  63.8 1.1 %down.1 = f32[16,1024]{1,0:T(8,128)} custom-call(f32[4,32,256]{2,1,0:T(8,128)S(1)} %bitcast.3, f32[2,16,256]{2,1,0:T(8,128)S(1)} %get-tuple-element.33.peer_ref, bf16[256,256]{1,0:T(8,128)(2,1)S(1)} %get-tuple-element.34.bh_ref, bf16[256,256]{1,0:T(8,128)(2,1)S(1)} %get-tuple-element.35.bl_ref, bf16[256,1024]{1,0:T(8,128)(2,1)S(1)} %get-tuple-element.36.mh_ref, ...), custom_call_target="tpu_custom_call" | custom-call | flops 100000000 | bytes 262144 | tf_op jit(solution)/shard_map/down/pallas_call | solution.py:324
  (5 shorter events, 0.0 us)
Async XLA Ops:
  3.5 15.8 %copy-start.2 = (f32[24,1024]{1,0:T(8,128)S(1)}, f32[24,1024]{1,0:T(8,128)}, u32[]{:S(2)}) copy-start(f32[24,1024]{1,0:T(8,128)} %get-tuple-element.31.mid_ref) | copy-start | bytes 294916
  3.5 18.7 %copy-start = (f32[3,1024]{1,0:T(4,128)S(1)}, f32[3,1024]{1,0:T(4,128)}, u32[]{:S(2)}) copy-start(f32[3,1024]{1,0:T(4,128)} %skl_ref.1) | copy-start | bytes 36868
  3.5 18.7 %copy-start.1 = (f32[3,256]{1,0:T(4,128)S(1)}, f32[3,256]{1,0:T(4,128)}, u32[]{:S(2)}) copy-start(f32[3,256]{1,0:T(4,128)} %skb_ref.3) | copy-start | bytes 9220
  3.5 29.6 %all-to-all-start = ((f32[8,40,128]{2,1,0:T(8,128)}), f32[8,40,128]{2,1,0:T(8,128)S(1)}, u32[]{:S(2)}, u32[]{:S(2)}) async-start(f32[8,40,128]{2,1,0:T(8,128)} %get-tuple-element.22), calls=%async_computation | async-start | bytes 327680 | tf_op jit(solution)/shard_map/all_to_all | solution.py:303
  19.3 2.9 %copy-start.4 = (s32[4,8]{1,0:T(4,128)S(1)}, s32[4,8]{1,0:T(4,128)}, u32[]{:S(2)}) copy-start(s32[4,8]{1,0:T(4,128)} %nbr_ref.3) | copy-start | bytes 388
  19.3 2.9 %copy-start.5 = (s32[4]{0:T(128)S(1)}, s32[4]{0:T(128)}, u32[]{:S(2)}) copy-start(s32[4]{0:T(128)} %param.12) | copy-start | bytes 52
  19.3 25.7 %collective-permute-start.1 = (f32[24,1024]{1,0:T(8,128)S(1)}, f32[24,1024]{1,0:T(8,128)S(1)}, u32[]{:S(2)}, u32[]{:S(2)}) collective-permute-start(f32[24,1024]{1,0:T(8,128)S(1)} %copy-done.2), channel_id=1, source_target_pairs={{0,1},{1,0},{2,3},{3,2},{4,5},{5,4},{6,7},{7,6},{8,9},{9,8},{10,11... | collective-permute-start | bytes 294920 | tf_op jit(solution)/shard_map/ppermute | solution.py:306
  22.2 14.4 %copy-start.3 = (f32[3,4096]{1,0:T(4,128)S(1)}, f32[3,4096]{1,0:T(4,128)}, u32[]{:S(2)}) copy-start(f32[3,4096]{1,0:T(4,128)} %skg_ref.5) | copy-start | bytes 147460
  25.0 20.0 %collective-permute-start.2 = (f32[24,1024]{1,0:T(8,128)S(1)}, f32[24,1024]{1,0:T(8,128)S(1)}, u32[]{:S(2)}, u32[]{:S(2)}) collective-permute-start(f32[24,1024]{1,0:T(8,128)S(1)} %copy-done.2), channel_id=1, source_target_pairs={{1,2},{3,4},{5,6},{7,8},{9,10},{11,12},{13,14},{15,16},{17,18},{19... | collective-permute-start | bytes 294920 | tf_op jit(solution)/shard_map/ppermute | solution.py:313
  33.1 11.9 %collective-permute-start = (f32[8,40,128]{2,1,0:T(8,128)S(1)}, f32[8,40,128]{2,1,0:T(8,128)S(1)}, u32[]{:S(2)}, u32[]{:S(2)}) collective-permute-start(f32[8,40,128]{2,1,0:T(8,128)S(1)} %all-to-all-done.part_ref), channel_id=1, source_target_pairs={{0,2},{2,0},{1,3},{3,1},{4,6},{6,4},{5,7},{7,5},{8,10},{10,8},{9,1... | collective-permute-start | bytes 491528 | tf_op jit(solution)/shard_map/ppermute | solution.py:315
  38.2 14.3 %all-to-all-start.1 = ((f32[16,16,256]{2,1,0:T(8,128)}), f32[16,16,256]{2,1,0:T(8,128)S(1)}, u32[]{:S(2)}, u32[]{:S(2)}) async-start(f32[16,16,256]{2,1,0:T(8,128)} %group.1), calls=%async_computation.1 | async-start | bytes 524288 | tf_op jit(solution)/shard_map/all_to_all | solution.py:317

commit v9 on v8

--- a/solution.py
+++ b/solution.py
@@ -111,8 +111,6 @@
         hot = (row == mor_ref[:, col]).astype(f32).astype(bf16)
         s = dg(parts, hot, 1, 0)
         srt = s[:ROWS] + s[ROWS : 2 * ROWS] + s[2 * ROWS :]
-        if q == 0:
-            srt = jnp.concatenate([srt[: VEC + 3], skb_ref[...], srt[VEC + 6 :]], axis=0)
         srt_ref[:, col] = srt
         sorts.append(s)
     total = jnp.zeros((VEC, T), f32)
@@ -209,30 +207,31 @@
 
 
 def peer_kernel(
-    nbr_ref, cnt_ref, part_ref, other_ref, skb_ref, sibling_ref, skg_ref, adj_ref, mid_ref, near_ref, peer_ref, bh_ref, bl_ref, all_ref
+    nbr_ref, cnt_ref, part_ref, other_ref, skb_ref, skp_ref, skg_ref, sib_ref, adj_ref, mid_ref, near_ref, *outs
 ):
+    peer_ref, bh_ref, bl_ref, all_ref = outs
     n = part_ref.shape[0]
     ft_own = feat_tgt(skb_ref[...])
-    ft_sib = feat_tgt(sibling_ref[VEC + 3 : VEC + 6, :T])
+    ft_pair = feat_tgt(skp_ref[...])
     own = jnp.zeros((VEC, T), f32)
-    sib = jnp.zeros((VEC, T), f32)
+    pair = jnp.zeros((VEC, T), f32)
     for c in range(2 * n):
         w, skel = unpack((part_ref if c < n else other_ref)[c % n])
         fs = feat_src(skel)
         vv = stack2(w)
-        sib = sib + times(vv, tile(fs, ft_sib))
+        pair = pair + times(vv, tile(fs, ft_pair))
         if c < n:
             vv = stack2(jnp.where(lax.axis_index("z8") == c, 0.0, 1.0) * w)
         own = own + times(vv, tile(fs, ft_own))
     peer_ref[0] = gain((4 * n - 1) * T) * own
-    peer_ref[1] = gain((4 * n - 1) * T) * sib
+    peer_ref[1] = gain((4 * n - 1) * T) * pair
     kh, kl = tile(feat_src(own_group(skg_ref)), ft_own)
     bh_ref[...] = kh
     bl_ref[...] = kl
     fts = [feat_tgt(leaf(mid_ref, q)[1]) for q in range(LEAVES_DEV)]
     acc = [jnp.zeros((VEC, T), f32) for _ in range(LEAVES_DEV)]
     table = slots(nbr_ref, cnt_ref)
-    side_near(table, sibling_ref, lax.axis_index("core") == 0, fts, acc)
+    side_near(table, sib_ref, lax.axis_index("core") == 0, fts, acc)
     side_near(table, adj_ref, lax.axis_index("core") == 1, fts, acc)
     for q in range(LEAVES_DEV):
         col = slice(q * T, (q + 1) * T)
@@ -254,7 +253,7 @@
 def down_kernel(cell_ref, peer_ref, bh_ref, bl_ref, mh_ref, ml_ref, near_ref, out_ref):
     group = jnp.sum(cell_ref[:, :VEC, :], axis=0)
     field = gain(T) * times(stack2(group), (bh_ref[...], bl_ref[...]))
-    field = field + peer_ref[0] + cell_ref[lax.axis_index("zp") * 2 + 1 - lax.axis_index("core"), VEC:, :]
+    field = field + peer_ref[0] + cell_ref[(1 - lax.axis_index("zp")) * 2 + lax.axis_index("core"), VEC:, :]
     out_ref[...] = near_ref[...] + times(stack2(field), (mh_ref[...], ml_ref[...]))
 
 
@@ -308,16 +307,17 @@
     near, mh, ml = kernel(near_kernel, "near", (shape(VEC, n), operator, operator), 0, 5, tiles=28)(
         neighbours, counts, srt, skel_block, skel_leaf
     )
-    srt, near, mh, ml = lax.optimization_barrier((srt, near, mh, ml))
+    srt, near, mh, ml, skel = lax.optimization_barrier((srt, near, mh, ml, skel_block))
+    pair_skel = lax.ppermute(skel, "zp", swap)
     odd = range(1, whole - 1, 2)
     adj = lax.ppermute(srt, axes, [(i, i + 1) for i in odd] + [(i + 1, i) for i in odd])
     part, near, mh, ml = lax.optimization_barrier((part, near, mh, ml))
-    other = lax.ppermute(part, "zp", swap)
+    other = lax.ppermute(part, "core", swap)
     gw = kernel(group_kernel, "group", shape(n_groups, VEC, T), 0, 2, tiles=30)(part, skel_group)
     gws = lax.all_to_all(gw, "grp", 0, 0, tiled=False)
     square = shape(T, T, dtype=bf16)
-    peer, bh, bl, near = kernel(peer_kernel, "peer", (shape(2, VEC, T), square, square, shape(VEC, n)), 0, 10, tiles=53)(
-        neighbours, counts, part, other, skel_block, sib, skel_group, adj, srt, near
+    peer, bh, bl, near = kernel(peer_kernel, "peer", (shape(2, VEC, T), square, square, shape(VEC, n)), 0, 11, tiles=53)(
+        neighbours, counts, part, other, skel_block, pair_skel, skel_group, sib, adj, srt, near
     )
     mine = kernel(field_kernel, "field", shape(2 * VEC, T), 0, 3, tiles=20)(gws, skel_group, peer)
     cell = lax.all_gather(mine, ("zp", "core"), axis=0, tiled=False)

time: 65.3 us -> 65.7 us (level)
  starting transfers between devices: 31.4 us -> 37.2 us
  blocking collectives: 9.81 us -> 6.37 us
  waiting for transfers between devices: 8.89 us -> 6.94 us
    ppermute x1 -> x2, starting transfers between devices: 3.46 us -> 8.94 us  [the longest x1 6.29 us: body(): other = lax.ppermute(part, 'core', swap)]
    all_gather x1, blocking collectives: 9.81 us -> 6.37 us  [body(): cell = lax.all_gather(mine, ('zp', 'core'), axis=0, tiled=False)]
    all_to_all x1, waiting for transfers between devices: 5.59 us -> 2.67 us  [body(): part = lax.all_to_all(packed, 'z8', 0, 0, tiled=False)]
    all_to_all x1, waiting for transfers between devices: 3.29 us -> 4.26 us  [body(): gws = lax.all_to_all(gw, 'grp', 0, 0, tiled=False)]
  transfers between devices with their start and end apart: 5 -> 6, of which waited for: 2 -> 2; matrix products, arithmetic and copies ran while one was open for 0% -> 0% of each run, Pallas kernels for 13% -> 13%
where the time goes in v9:
time: 65.7 us; the launch traced here: 65.2 us
  starting transfers between devices  37.2 us (57%)
  Pallas kernels  14.6 us (22%)
  waiting for transfers between devices  6.94 us (11%)
  blocking collectives  6.37 us (10%)
    all_to_all x1, starting transfers between devices, body(): part = lax.all_to_all(packed, 'z8', 0, 0, tiled=False)  15.8 us
    all_to_all x1, starting transfers between devices, body(): gws = lax.all_to_all(gw, 'grp', 0, 0, tiled=False)  6.75 us
    all_gather x1, blocking collectives, body(): cell = lax.all_gather(mine, ('zp', 'core'), axis=0, tiled=False)  6.37 us
    ppermute x1, starting transfers between devices, body(): other = lax.ppermute(part, 'core', swap)  6.29 us
    all_to_all x1, waiting for transfers between devices, body(): gws = lax.all_to_all(gw, 'grp', 0, 0, tiled=False)  4.26 us
    pallas_call x1, Pallas kernels, body(): kernel(peer_kernel, 'peer', (shape(2, VEC, T), square, square, shape(VEC,...  4.22 us
    pallas_call x1, Pallas kernels, body(): pl.pallas_call(up_kernel, out_shape=(shape(ROWS, n), shape(n_z8, PACK, HA...  3.47 us
    ppermute x1, starting transfers between devices, body(): sib = lax.ppermute(srt, 'core', swap)  2.86 us
  transfers between devices with their start and end apart: 6, of which 2 were waited for; matrix products, arithmetic and copies ran while one was open for 0% of the time, Pallas kernels for 13%

profile of v9, /device:TPU:1, one launch (start us, length us, event | category | flops | bytes accessed | tf_op | source)
XLA Modules:
  0.0 65.2 jit_solution(12875925127279414847)
XLA Ops:
  0.0 3.5 %up.1 = (f32[24,1024]{1,0:T(8,128)}, f32[8,40,128]{2,1,0:T(8,128)}) custom-call(f32[3,1024]{1,0:T(4,128)} %pts_hbm.1, f32[16,1024]{1,0:T(8,128)} %chg_hbm.1, s32[1,1024]{1,0:T(1,128)} %bitcast.6, f32[3,1024]{1,0:T(4,128)} %skl_ref.1, f32[3,256]{1,0:T(4,128)} %skb_ref.3), custom_call_target="tpu_custom_call" | custom-call | tf_op jit(solution)/shard_map/up/pallas_call | solution.py:292
  3.5 0.0 copy-start.2
  3.5 0.0 copy-start
  3.5 0.0 copy-start.1
  3.5 15.8 %all-to-all-start = ((f32[8,40,128]{2,1,0:T(8,128)}), f32[8,40,128]{2,1,0:T(8,128)S(1)}, u32[]{:S(2)}, u32[]{:S(2)}) async-start(f32[8,40,128]{2,1,0:T(8,128)} %get-tuple-element.23), calls=%async_computation | async-start | bytes 327680 | tf_op jit(solution)/shard_map/all_to_all | solution.py:302
  19.3 0.0 copy-start.5
  19.3 2.9 %collective-permute-start.2 = (f32[24,1024]{1,0:T(8,128)S(1)}, f32[24,1024]{1,0:T(8,128)S(1)}, u32[]{:S(2)}, u32[]{:S(2)}) collective-permute-start(f32[24,1024]{1,0:T(8,128)S(1)} %copy-done.2), channel_id=1, source_target_pairs={{0,1},{1,0},{2,3},{3,2},{4,5},{5,4},{6,7},{7,6},{8,9},{9,8},{10,11... | collective-permute-start | bytes 294920 | tf_op jit(solution)/shard_map/ppermute | solution.py:305
  22.2 0.0 copy-start.3
  22.2 2.8 %near.1 = (f32[16,1024]{1,0:T(8,128)S(1)}, bf16[256,1024]{1,0:T(8,128)(2,1)S(1)}, bf16[256,1024]{1,0:T(8,128)(2,1)S(1)}) custom-call(s32[4,8]{1,0:T(4,128)S(1)} %copy-done.4, s32[1,4]{1,0:T(1,128)S(1)} %bitcast.4, f32[24,1024]{1,0:T(8,128)S(1)} %copy-done.2, f32[3,256]{1,0:T(4,128)S(1)} %copy-done.1, f32[3,1024]{1,0:T(4,128)S(1)} %copy-done), custom_call_target="tpu_custom_call" | custom-call | flops 2800000000 | bytes 7340032 | tf_op jit(solution)/shard_map/near/pallas_call | solution.py:307
  25.0 2.6 %collective-permute-start.1 = (f32[3,256]{1,0:T(4,128)S(1)}, f32[3,256]{1,0:T(4,128)S(1)}, u32[]{:S(2)}, u32[]{:S(2)}) collective-permute-start(f32[3,256]{1,0:T(4,128)S(1)} %copy-done.1), channel_id=1, source_target_pairs={{0,2},{2,0},{1,3},{3,1},{4,6},{6,4},{5,7},{7,5},{8,10},{10,8},{9,1... | collective-permute-start | bytes 9224 | tf_op jit(solution)/shard_map/ppermute | solution.py:311
  27.7 2.8 %collective-permute-start.3 = (f32[24,1024]{1,0:T(8,128)S(1)}, f32[24,1024]{1,0:T(8,128)S(1)}, u32[]{:S(2)}, u32[]{:S(2)}) collective-permute-start(f32[24,1024]{1,0:T(8,128)S(1)} %copy-done.2), channel_id=1, source_target_pairs={{1,2},{3,4},{5,6},{7,8},{9,10},{11,12},{13,14},{15,16},{17,18},{19... | collective-permute-start | bytes 294920 | tf_op jit(solution)/shard_map/ppermute | solution.py:313
  30.5 2.7 %all-to-all-done.part_ref = f32[8,40,128]{2,1,0:T(8,128)S(1)} async-done(((f32[8,40,128]{2,1,0:T(8,128)}), f32[8,40,128]{2,1,0:T(8,128)S(1)}, u32[]{:S(2)}, u32[]{:S(2)}) %all-to-all-start) | async-done | bytes 163872 | tf_op jit(solution)/shard_map/all_to_all | solution.py:302
  33.1 6.3 %collective-permute-start = (f32[8,40,128]{2,1,0:T(8,128)S(1)}, f32[8,40,128]{2,1,0:T(8,128)S(1)}, u32[]{:S(2)}, u32[]{:S(2)}) collective-permute-start(f32[8,40,128]{2,1,0:T(8,128)S(1)} %all-to-all-done.part_ref), channel_id=1, source_target_pairs={{0,1},{1,0},{2,3},{3,2},{4,5},{5,4},{6,7},{7,6},{8,9},{9,8},{10,11... | collective-permute-start | bytes 491528 | tf_op jit(solution)/shard_map/ppermute | solution.py:315
  39.5 1.6 %group.1 = f32[16,16,256]{2,1,0:T(8,128)} custom-call(f32[8,40,128]{2,1,0:T(8,128)S(1)} %all-to-all-done.part_ref, f32[3,4096]{1,0:T(4,128)S(1)} %copy-done.3), custom_call_target="tpu_custom_call" | custom-call | flops 3000000000 | bytes 7864320 | tf_op jit(solution)/shard_map/group/pallas_call | solution.py:316
  41.1 6.8 %all-to-all-start.1 = ((f32[16,16,256]{2,1,0:T(8,128)}), f32[16,16,256]{2,1,0:T(8,128)S(1)}, u32[]{:S(2)}, u32[]{:S(2)}) async-start(f32[16,16,256]{2,1,0:T(8,128)} %group.1), calls=%async_computation.1 | async-start | bytes 524288 | tf_op jit(solution)/shard_map/all_to_all | solution.py:317
  47.8 0.0 collective-permute-done.1.skp_ref
  47.8 0.0 collective-permute-done.2.sib_ref
  47.8 0.0 collective-permute-done.3.adj_ref
  47.9 0.0 collective-permute-done.other_ref
  47.9 4.2 %peer.1 = (f32[2,16,256]{2,1,0:T(8,128)S(1)}, bf16[256,256]{1,0:T(8,128)(2,1)S(1)}, bf16[256,256]{1,0:T(8,128)(2,1)S(1)}, f32[16,1024]{1,0:T(8,128)S(1)}) custom-call(s32[4,8]{1,0:T(4,128)S(1)} %copy-done.4, s32[1,4]{1,0:T(1,128)S(1)} %bitcast.5, f32[8,40,128]{2,1,0:T(8,128)S(1)} %all-to-all-done.part_ref, f32[8,40,128]{2,1,0:T(8,128)S(1)} %collective-permute-done.other_ref, ...), custom_call_target="tpu_custom_call" | custom-call | flops 5299999744 | bytes 13893632 | tf_op jit(solution)/shard_map/peer/pallas_call | solution.py:319
  52.1 4.3 %all-to-all-done.1.gws_ref = f32[16,16,256]{2,1,0:T(8,128)S(1)} async-done(((f32[16,16,256]{2,1,0:T(8,128)}), f32[16,16,256]{2,1,0:T(8,128)S(1)}, u32[]{:S(2)}, u32[]{:S(2)}) %all-to-all-start.1) | async-done | bytes 262176 | tf_op jit(solution)/shard_map/all_to_all | solution.py:317
  56.4 1.4 %field.1 = f32[32,256]{1,0:T(8,128)S(1)} custom-call(f32[16,16,256]{2,1,0:T(8,128)S(1)} %all-to-all-done.1.gws_ref, f32[3,4096]{1,0:T(4,128)S(1)} %copy-done.3, f32[2,16,256]{2,1,0:T(8,128)S(1)} %get-tuple-element.35.peer_ref), custom_call_target="tpu_custom_call" | custom-call | flops 2000000000 | bytes 5242880 | tf_op jit(solution)/shard_map/field/pallas_call | solution.py:322
  57.8 6.4 %all-gather = f32[128,256]{1,0:T(8,128)S(1)} all-gather(f32[32,256]{1,0:T(8,128)S(1)} %field.1), channel_id=2, replica_groups=mesh['grp'=16,'z8'=8,'zp'=2,'core'=2] {'zp','core'}, dimensions={0}, use_global_device_ids=true | all-gather | bytes 163840 | tf_op jit(solution)/shard_map/all_gather | solution.py:323
  64.1 1.1 %down.1 = f32[16,1024]{1,0:T(8,128)} custom-call(f32[4,32,256]{2,1,0:T(8,128)S(1)} %bitcast.3, f32[2,16,256]{2,1,0:T(8,128)S(1)} %get-tuple-element.35.peer_ref, bf16[256,256]{1,0:T(8,128)(2,1)S(1)} %get-tuple-element.36.bh_ref, bf16[256,256]{1,0:T(8,128)(2,1)S(1)} %get-tuple-element.37.bl_ref, bf16[256,1024]{1,0:T(8,128)(2,1)S(1)} %get-tuple-element.38.mh_ref, ...), custom_call_target="tpu_custom_call" | custom-call | flops 100000000 | bytes 262144 | tf_op jit(solution)/shard_map/down/pallas_call | solution.py:324
  (7 shorter events, 0.0 us)
Async XLA Ops:
  3.5 15.8 %copy-start.2 = (f32[24,1024]{1,0:T(8,128)S(1)}, f32[24,1024]{1,0:T(8,128)}, u32[]{:S(2)}) copy-start(f32[24,1024]{1,0:T(8,128)} %get-tuple-element.33.mid_ref) | copy-start | bytes 294916
  3.5 18.7 %copy-start = (f32[3,1024]{1,0:T(4,128)S(1)}, f32[3,1024]{1,0:T(4,128)}, u32[]{:S(2)}) copy-start(f32[3,1024]{1,0:T(4,128)} %skl_ref.1) | copy-start | bytes 36868
  3.5 18.7 %copy-start.1 = (f32[3,256]{1,0:T(4,128)S(1)}, f32[3,256]{1,0:T(4,128)}, u32[]{:S(2)}) copy-start(f32[3,256]{1,0:T(4,128)} %skb_ref.3) | copy-start | bytes 9220
  3.5 29.6 %all-to-all-start = ((f32[8,40,128]{2,1,0:T(8,128)}), f32[8,40,128]{2,1,0:T(8,128)S(1)}, u32[]{:S(2)}, u32[]{:S(2)}) async-start(f32[8,40,128]{2,1,0:T(8,128)} %get-tuple-element.23), calls=%async_computation | async-start | bytes 327680 | tf_op jit(solution)/shard_map/all_to_all | solution.py:302
  19.3 2.9 %copy-start.4 = (s32[4,8]{1,0:T(4,128)S(1)}, s32[4,8]{1,0:T(4,128)}, u32[]{:S(2)}) copy-start(s32[4,8]{1,0:T(4,128)} %nbr_ref.3) | copy-start | bytes 388
  19.3 2.9 %copy-start.5 = (s32[4]{0:T(128)S(1)}, s32[4]{0:T(128)}, u32[]{:S(2)}) copy-start(s32[4]{0:T(128)} %param.12) | copy-start | bytes 52
  19.3 28.5 %collective-permute-start.2 = (f32[24,1024]{1,0:T(8,128)S(1)}, f32[24,1024]{1,0:T(8,128)S(1)}, u32[]{:S(2)}, u32[]{:S(2)}) collective-permute-start(f32[24,1024]{1,0:T(8,128)S(1)} %copy-done.2), channel_id=1, source_target_pairs={{0,1},{1,0},{2,3},{3,2},{4,5},{5,4},{6,7},{7,6},{8,9},{9,8},{10,11... | collective-permute-start | bytes 294920 | tf_op jit(solution)/shard_map/ppermute | solution.py:305
  22.2 17.2 %copy-start.3 = (f32[3,4096]{1,0:T(4,128)S(1)}, f32[3,4096]{1,0:T(4,128)}, u32[]{:S(2)}) copy-start(f32[3,4096]{1,0:T(4,128)} %skg_ref.5) | copy-start | bytes 147460
  25.0 22.8 %collective-permute-start.1 = (f32[3,256]{1,0:T(4,128)S(1)}, f32[3,256]{1,0:T(4,128)S(1)}, u32[]{:S(2)}, u32[]{:S(2)}) collective-permute-start(f32[3,256]{1,0:T(4,128)S(1)} %copy-done.1), channel_id=1, source_target_pairs={{0,2},{2,0},{1,3},{3,1},{4,6},{6,4},{5,7},{7,5},{8,10},{10,8},{9,1... | collective-permute-start | bytes 9224 | tf_op jit(solution)/shard_map/ppermute | solution.py:311
  27.7 20.2 %collective-permute-start.3 = (f32[24,1024]{1,0:T(8,128)S(1)}, f32[24,1024]{1,0:T(8,128)S(1)}, u32[]{:S(2)}, u32[]{:S(2)}) collective-permute-start(f32[24,1024]{1,0:T(8,128)S(1)} %copy-done.2), channel_id=1, source_target_pairs={{1,2},{3,4},{5,6},{7,8},{9,10},{11,12},{13,14},{15,16},{17,18},{19... | collective-permute-start | bytes 294920 | tf_op jit(solution)/shard_map/ppermute | solution.py:313
  33.1 14.7 %collective-permute-start = (f32[8,40,128]{2,1,0:T(8,128)S(1)}, f32[8,40,128]{2,1,0:T(8,128)S(1)}, u32[]{:S(2)}, u32[]{:S(2)}) collective-permute-start(f32[8,40,128]{2,1,0:T(8,128)S(1)} %all-to-all-done.part_ref), channel_id=1, source_target_pairs={{0,1},{1,0},{2,3},{3,2},{4,5},{5,4},{6,7},{7,6},{8,9},{9,8},{10,11... | collective-permute-start | bytes 491528 | tf_op jit(solution)/shard_map/ppermute | solution.py:315
  41.1 15.3 %all-to-all-start.1 = ((f32[16,16,256]{2,1,0:T(8,128)}), f32[16,16,256]{2,1,0:T(8,128)S(1)}, u32[]{:S(2)}, u32[]{:S(2)}) async-start(f32[16,16,256]{2,1,0:T(8,128)} %group.1), calls=%async_computation.1 | async-start | bytes 524288 | tf_op jit(solution)/shard_map/all_to_all | solution.py:317

commit v10 on v8

--- a/solution.py
+++ b/solution.py
@@ -104,23 +104,22 @@
     rows = jnp.concatenate([chg_ref[...], pts_ref[...], jnp.zeros((5, n), f32)], axis=0)
     a, b, c = split3(rows)
     parts = jnp.concatenate([a, b, c], axis=0).astype(bf16)
-    row = lax.broadcasted_iota(jnp.int32, (n, T), 0)
-    sorts = []
-    for q in range(LEAVES_DEV):
-        col = slice(q * T, (q + 1) * T)
-        hot = (row == mor_ref[:, col]).astype(f32).astype(bf16)
-        s = dg(parts, hot, 1, 0)
-        srt = s[:ROWS] + s[ROWS : 2 * ROWS] + s[2 * ROWS :]
-        if q == 0:
-            srt = jnp.concatenate([srt[: VEC + 3], skb_ref[...], srt[VEC + 6 :]], axis=0)
+    row = lax.broadcasted_iota(jnp.int16, (n, T), 0)
+    cols = [slice(q * T, (q + 1) * T) for q in range(LEAVES_DEV)]
+    hots = [jnp.where(row == mor_ref[:, col].astype(jnp.int16), bf16(1), bf16(0)) for col in cols]
+    sums = [dg(parts, hot, 1, 0) for hot in hots]
+    srts = [s[:ROWS] + s[ROWS : 2 * ROWS] + s[2 * ROWS :] for s in sums]
+    srts[0] = jnp.concatenate([srts[0][: VEC + 3], skb_ref[...], srts[0][VEC + 6 :]], axis=0)
+    for col, srt in zip(cols, srts):
         srt_ref[:, col] = srt
-        sorts.append(s)
+    sources = [feat_src(srt[VEC : VEC + 3]) for srt in srts]
+    targets = [feat_tgt(skl_ref[:, col]) for col in cols]
+    exponents = [dg(fs, ft, 0, 0) for fs, ft in zip(sources, targets)]
+    tiles = [split2(jnp.exp2(e)) for e in exponents]
+    splits = [(s[:VEC], s[ROWS : ROWS + VEC] + s[2 * ROWS : 2 * ROWS + VEC]) for s in sums]
+    weights = [times(jnp.concatenate(hl, axis=0).astype(bf16), kt) for hl, kt in zip(splits, tiles)]
     total = jnp.zeros((VEC, T), f32)
-    for q in range(LEAVES_DEV):
-        col = slice(q * T, (q + 1) * T)
-        s = sorts[q]
-        vv = jnp.concatenate([s[:VEC], s[ROWS : ROWS + VEC] + s[2 * ROWS : 2 * ROWS + VEC]], axis=0).astype(bf16)
-        lw = times(vv, tile(feat_src(srt_ref[VEC : VEC + 3, col]), feat_tgt(skl_ref[:, col])))
+    for col, lw in zip(cols, weights):
         total = total + times(stack2(gain(T) * lw), (kh_ref[col, :], kl_ref[col, :]))
     packed = pack(gain(LEAVES_DEV * T) * total, skb_ref[...])
     for z in range(pack_ref.shape[0]):

time: 65.3 us -> 64.9 us (level)
  no operation moved by 1% of the time
where the time goes in v10:
time: 64.9 us; the launch traced here: 64.4 us
  starting transfers between devices  31.4 us (48%)
  Pallas kernels  14.1 us (22%)
  blocking collectives  9.82 us (15%)
  waiting for transfers between devices  8.88 us (14%)
    all_to_all x1, starting transfers between devices, body(): part = lax.all_to_all(packed, 'z8', 0, 0, tiled=False)  15.8 us
    all_gather x1, blocking collectives, body(): cell = lax.all_gather(mine, ('zp', 'core'), axis=0, tiled=False)  9.82 us
    all_to_all x1, starting transfers between devices, body(): gws = lax.all_to_all(gw, 'grp', 0, 0, tiled=False)  6.75 us
    all_to_all x1, waiting for transfers between devices, body(): part = lax.all_to_all(packed, 'z8', 0, 0, tiled=False)  5.59 us
    pallas_call x1, Pallas kernels, body(): kernel(peer_kernel, 'peer', (shape(2, VEC, T), square, square, shape(VEC,...  4.22 us
    ppermute x1, starting transfers between devices, body(): other = lax.ppermute(part, 'zp', swap)  3.47 us
    all_to_all x1, waiting for transfers between devices, body(): gws = lax.all_to_all(gw, 'grp', 0, 0, tiled=False)  3.29 us
    pallas_call x1, Pallas kernels, body(): pl.pallas_call(up_kernel, out_shape=(shape(ROWS, n), shape(n_z8, PACK, HA...  3.03 us
  transfers between devices with their start and end apart: 5, of which 2 were waited for; matrix products, arithmetic and copies ran while one was open for 0% of the time, Pallas kernels for 13%

profile of v10, /device:TPU:1, one launch (start us, length us, event | category | flops | bytes accessed | tf_op | source)
XLA Modules:
  0.0 64.4 jit_solution(189376120715889672)
XLA Ops:
  0.0 3.0 %up.1 = (f32[24,1024]{1,0:T(8,128)}, f32[8,40,128]{2,1,0:T(8,128)}) custom-call(f32[3,1024]{1,0:T(4,128)} %pts_hbm.1, f32[16,1024]{1,0:T(8,128)} %chg_hbm.1, s32[1,1024]{1,0:T(1,128)} %bitcast.6, f32[3,1024]{1,0:T(4,128)} %skl_ref.1, f32[3,256]{1,0:T(4,128)} %skb_ref.3), custom_call_target="tpu_custom_call" | custom-call | tf_op jit(solution)/shard_map/up/pallas_call | solution.py:292
  3.0 0.0 copy-start.2
  3.1 0.0 copy-start
  3.1 0.0 copy-start.1
  3.1 15.8 %all-to-all-start = ((f32[8,40,128]{2,1,0:T(8,128)}), f32[8,40,128]{2,1,0:T(8,128)S(1)}, u32[]{:S(2)}, u32[]{:S(2)}) async-start(f32[8,40,128]{2,1,0:T(8,128)} %get-tuple-element.22), calls=%async_computation | async-start | bytes 327680 | tf_op jit(solution)/shard_map/all_to_all | solution.py:302
  18.9 0.0 copy-done.2
  18.9 0.0 copy-start.5
  18.9 2.9 %collective-permute-start.1 = (f32[24,1024]{1,0:T(8,128)S(1)}, f32[24,1024]{1,0:T(8,128)S(1)}, u32[]{:S(2)}, u32[]{:S(2)}) collective-permute-start(f32[24,1024]{1,0:T(8,128)S(1)} %copy-done.2), channel_id=1, source_target_pairs={{0,1},{1,0},{2,3},{3,2},{4,5},{5,4},{6,7},{7,6},{8,9},{9,8},{10,11... | collective-permute-start | bytes 294920 | tf_op jit(solution)/shard_map/ppermute | solution.py:305
  21.8 0.0 copy-start.3
  21.8 2.8 %near.1 = (f32[16,1024]{1,0:T(8,128)S(1)}, bf16[256,1024]{1,0:T(8,128)(2,1)S(1)}, bf16[256,1024]{1,0:T(8,128)(2,1)S(1)}) custom-call(s32[4,8]{1,0:T(4,128)S(1)} %copy-done.4, s32[1,4]{1,0:T(1,128)S(1)} %bitcast.4, f32[24,1024]{1,0:T(8,128)S(1)} %copy-done.2, f32[3,256]{1,0:T(4,128)S(1)} %copy-done.1, f32[3,1024]{1,0:T(4,128)S(1)} %copy-done), custom_call_target="tpu_custom_call" | custom-call | flops 2800000000 | bytes 7340032 | tf_op jit(solution)/shard_map/near/pallas_call | solution.py:307
  24.6 2.5 %collective-permute-start.2 = (f32[24,1024]{1,0:T(8,128)S(1)}, f32[24,1024]{1,0:T(8,128)S(1)}, u32[]{:S(2)}, u32[]{:S(2)}) collective-permute-start(f32[24,1024]{1,0:T(8,128)S(1)} %copy-done.2), channel_id=1, source_target_pairs={{1,2},{3,4},{5,6},{7,8},{9,10},{11,12},{13,14},{15,16},{17,18},{19... | collective-permute-start | bytes 294920 | tf_op jit(solution)/shard_map/ppermute | solution.py:312
  27.1 5.6 %all-to-all-done.part_ref = f32[8,40,128]{2,1,0:T(8,128)S(1)} async-done(((f32[8,40,128]{2,1,0:T(8,128)}), f32[8,40,128]{2,1,0:T(8,128)S(1)}, u32[]{:S(2)}, u32[]{:S(2)}) %all-to-all-start) | async-done | bytes 163872 | tf_op jit(solution)/shard_map/all_to_all | solution.py:302
  32.7 3.5 %collective-permute-start = (f32[8,40,128]{2,1,0:T(8,128)S(1)}, f32[8,40,128]{2,1,0:T(8,128)S(1)}, u32[]{:S(2)}, u32[]{:S(2)}) collective-permute-start(f32[8,40,128]{2,1,0:T(8,128)S(1)} %all-to-all-done.part_ref), channel_id=1, source_target_pairs={{0,2},{2,0},{1,3},{3,1},{4,6},{6,4},{5,7},{7,5},{8,10},{10,8},{9,1... | collective-permute-start | bytes 491528 | tf_op jit(solution)/shard_map/ppermute | solution.py:314
  36.2 0.0 copy-done.3
  36.2 1.6 %group.1 = f32[16,16,256]{2,1,0:T(8,128)} custom-call(f32[8,40,128]{2,1,0:T(8,128)S(1)} %all-to-all-done.part_ref, f32[3,4096]{1,0:T(4,128)S(1)} %copy-done.3), custom_call_target="tpu_custom_call" | custom-call | flops 3000000000 | bytes 7864320 | tf_op jit(solution)/shard_map/group/pallas_call | solution.py:315
  37.8 6.8 %all-to-all-start.1 = ((f32[16,16,256]{2,1,0:T(8,128)}), f32[16,16,256]{2,1,0:T(8,128)S(1)}, u32[]{:S(2)}, u32[]{:S(2)}) async-start(f32[16,16,256]{2,1,0:T(8,128)} %group.1), calls=%async_computation.1 | async-start | bytes 524288 | tf_op jit(solution)/shard_map/all_to_all | solution.py:316
  44.6 0.0 collective-permute-done.1.sibling_ref
  44.6 0.0 collective-permute-done.2.adj_ref
  44.6 0.0 collective-permute-done.other_ref
  44.6 4.2 %peer.1 = (f32[2,16,256]{2,1,0:T(8,128)S(1)}, bf16[256,256]{1,0:T(8,128)(2,1)S(1)}, bf16[256,256]{1,0:T(8,128)(2,1)S(1)}, f32[16,1024]{1,0:T(8,128)S(1)}) custom-call(s32[4,8]{1,0:T(4,128)S(1)} %copy-done.4, s32[1,4]{1,0:T(1,128)S(1)} %bitcast.5, f32[8,40,128]{2,1,0:T(8,128)S(1)} %all-to-all-done.part_ref, f32[8,40,128]{2,1,0:T(8,128)S(1)} %collective-permute-done.other_ref, ...), custom_call_target="tpu_custom_call" | custom-call | flops 5299999744 | bytes 13893632 | tf_op jit(solution)/shard_map/peer/pallas_call | solution.py:318
  48.8 3.3 %all-to-all-done.1.gws_ref = f32[16,16,256]{2,1,0:T(8,128)S(1)} async-done(((f32[16,16,256]{2,1,0:T(8,128)}), f32[16,16,256]{2,1,0:T(8,128)S(1)}, u32[]{:S(2)}, u32[]{:S(2)}) %all-to-all-start.1) | async-done | bytes 262176 | tf_op jit(solution)/shard_map/all_to_all | solution.py:316
  52.1 1.4 %field.1 = f32[32,256]{1,0:T(8,128)S(1)} custom-call(f32[16,16,256]{2,1,0:T(8,128)S(1)} %all-to-all-done.1.gws_ref, f32[3,4096]{1,0:T(4,128)S(1)} %copy-done.3, f32[2,16,256]{2,1,0:T(8,128)S(1)} %get-tuple-element.33.peer_ref), custom_call_target="tpu_custom_call" | custom-call | flops 2000000000 | bytes 5242880 | tf_op jit(solution)/shard_map/field/pallas_call | solution.py:321
  53.5 9.8 %all-gather = f32[128,256]{1,0:T(8,128)S(1)} all-gather(f32[32,256]{1,0:T(8,128)S(1)} %field.1), channel_id=2, replica_groups=mesh['grp'=16,'z8'=8,'zp'=2,'core'=2] {'zp','core'}, dimensions={0}, use_global_device_ids=true | all-gather | bytes 163840 | tf_op jit(solution)/shard_map/all_gather | solution.py:322
  63.4 1.1 %down.1 = f32[16,1024]{1,0:T(8,128)} custom-call(f32[4,32,256]{2,1,0:T(8,128)S(1)} %bitcast.3, f32[2,16,256]{2,1,0:T(8,128)S(1)} %get-tuple-element.33.peer_ref, bf16[256,256]{1,0:T(8,128)(2,1)S(1)} %get-tuple-element.34.bh_ref, bf16[256,256]{1,0:T(8,128)(2,1)S(1)} %get-tuple-element.35.bl_ref, bf16[256,1024]{1,0:T(8,128)(2,1)S(1)} %get-tuple-element.36.mh_ref, ...), custom_call_target="tpu_custom_call" | custom-call | flops 100000000 | bytes 262144 | tf_op jit(solution)/shard_map/down/pallas_call | solution.py:323
  (5 shorter events, 0.0 us)
Async XLA Ops:
  3.0 15.8 %copy-start.2 = (f32[24,1024]{1,0:T(8,128)S(1)}, f32[24,1024]{1,0:T(8,128)}, u32[]{:S(2)}) copy-start(f32[24,1024]{1,0:T(8,128)} %get-tuple-element.31.mid_ref) | copy-start | bytes 294916
  3.1 18.7 %copy-start = (f32[3,1024]{1,0:T(4,128)S(1)}, f32[3,1024]{1,0:T(4,128)}, u32[]{:S(2)}) copy-start(f32[3,1024]{1,0:T(4,128)} %skl_ref.1) | copy-start | bytes 36868
  3.1 18.7 %copy-start.1 = (f32[3,256]{1,0:T(4,128)S(1)}, f32[3,256]{1,0:T(4,128)}, u32[]{:S(2)}) copy-start(f32[3,256]{1,0:T(4,128)} %skb_ref.3) | copy-start | bytes 9220
  3.1 29.6 %all-to-all-start = ((f32[8,40,128]{2,1,0:T(8,128)}), f32[8,40,128]{2,1,0:T(8,128)S(1)}, u32[]{:S(2)}, u32[]{:S(2)}) async-start(f32[8,40,128]{2,1,0:T(8,128)} %get-tuple-element.22), calls=%async_computation | async-start | bytes 327680 | tf_op jit(solution)/shard_map/all_to_all | solution.py:302
  18.9 2.9 %copy-start.4 = (s32[4,8]{1,0:T(4,128)S(1)}, s32[4,8]{1,0:T(4,128)}, u32[]{:S(2)}) copy-start(s32[4,8]{1,0:T(4,128)} %nbr_ref.3) | copy-start | bytes 388
  18.9 2.9 %copy-start.5 = (s32[4]{0:T(128)S(1)}, s32[4]{0:T(128)}, u32[]{:S(2)}) copy-start(s32[4]{0:T(128)} %param.12) | copy-start | bytes 52
  18.9 25.7 %collective-permute-start.1 = (f32[24,1024]{1,0:T(8,128)S(1)}, f32[24,1024]{1,0:T(8,128)S(1)}, u32[]{:S(2)}, u32[]{:S(2)}) collective-permute-start(f32[24,1024]{1,0:T(8,128)S(1)} %copy-done.2), channel_id=1, source_target_pairs={{0,1},{1,0},{2,3},{3,2},{4,5},{5,4},{6,7},{7,6},{8,9},{9,8},{10,11... | collective-permute-start | bytes 294920 | tf_op jit(solution)/shard_map/ppermute | solution.py:305
  21.8 14.4 %copy-start.3 = (f32[3,4096]{1,0:T(4,128)S(1)}, f32[3,4096]{1,0:T(4,128)}, u32[]{:S(2)}) copy-start(f32[3,4096]{1,0:T(4,128)} %skg_ref.5) | copy-start | bytes 147460
  24.6 20.0 %collective-permute-start.2 = (f32[24,1024]{1,0:T(8,128)S(1)}, f32[24,1024]{1,0:T(8,128)S(1)}, u32[]{:S(2)}, u32[]{:S(2)}) collective-permute-start(f32[24,1024]{1,0:T(8,128)S(1)} %copy-done.2), channel_id=1, source_target_pairs={{1,2},{3,4},{5,6},{7,8},{9,10},{11,12},{13,14},{15,16},{17,18},{19... | collective-permute-start | bytes 294920 | tf_op jit(solution)/shard_map/ppermute | solution.py:312
  32.7 11.9 %collective-permute-start = (f32[8,40,128]{2,1,0:T(8,128)S(1)}, f32[8,40,128]{2,1,0:T(8,128)S(1)}, u32[]{:S(2)}, u32[]{:S(2)}) collective-permute-start(f32[8,40,128]{2,1,0:T(8,128)S(1)} %all-to-all-done.part_ref), channel_id=1, source_target_pairs={{0,2},{2,0},{1,3},{3,1},{4,6},{6,4},{5,7},{7,5},{8,10},{10,8},{9,1... | collective-permute-start | bytes 491528 | tf_op jit(solution)/shard_map/ppermute | solution.py:314
  37.8 14.3 %all-to-all-start.1 = ((f32[16,16,256]{2,1,0:T(8,128)}), f32[16,16,256]{2,1,0:T(8,128)S(1)}, u32[]{:S(2)}, u32[]{:S(2)}) async-start(f32[16,16,256]{2,1,0:T(8,128)} %group.1), calls=%async_computation.1 | async-start | bytes 524288 | tf_op jit(solution)/shard_map/all_to_all | solution.py:316

commit v11 on v10

--- a/solution.py
+++ b/solution.py
@@ -168,48 +168,66 @@
     return jnp.sum(jnp.where(table == source, 1.0, 0.0), axis=1, keepdims=True)
 
 
-def side_near(table, blk_ref, on_right, fts, acc):
+def side_near(table, blk_ref, on_right, fts):
     first = first_leaf() + jnp.where(on_right, LEAVES_DEV, -LEAVES_DEV)
+    targets = [jnp.where(on_right, fts[e], fts[LEAVES_DEV - 1 - e]) for e in range(LEAVES_DEV)]
+    acc = [jnp.zeros((VEC, T), f32) for _ in range(LEAVES_DEV)]
     for d in range(LEAVES_DEV):
         (v0, x0), (v1, x1) = leaf(blk_ref, d), leaf(blk_ref, LEAVES_DEV - 1 - d)
         v = jnp.where(on_right, v0, v1)
         fs = feat_src(jnp.where(on_right, x0, x1))
-        source = first + jnp.where(on_right, d, LEAVES_DEV - 1 - d)
-        m = uses(table, source)
+        m = uses(table, first + jnp.where(on_right, d, LEAVES_DEV - 1 - d))
         for e in range(d, LEAVES_DEV):
             q0, q1 = e, LEAVES_DEV - 1 - e
             times_used = jnp.where(on_right, m[q0 : q0 + 1], m[q1 : q1 + 1])
-            r = times(stack2(times_used * v), tile(fs, jnp.where(on_right, fts[q0], fts[q1])))
-            acc[q0] = acc[q0] + jnp.where(on_right, r, 0.0)
-            acc[q1] = acc[q1] + jnp.where(on_right, 0.0, r)
+            acc[e] = acc[e] + times(stack2(times_used * v), tile(fs, targets[e]))
+    return acc
 
 
 def near_kernel(nbr_ref, cnt_ref, mid_ref, skb_ref, skl_ref, near_ref, mh_ref, ml_ref):
     first = first_leaf()
     table = slots(nbr_ref, cnt_ref)
+    leaves = range(LEAVES_DEV)
+    cols = [slice(q * T, (q + 1) * T) for q in leaves]
+    own = [leaf(mid_ref, q) for q in leaves]
+    fts = [feat_tgt(x) for _, x in own]
+    fss = [feat_src(x) for _, x in own]
+    fs_block = feat_src(skb_ref[...])
+    skl_t = [feat_tgt(skl_ref[:, col]) for col in cols]
+    skl_s = [feat_src(skl_ref[:, col]) for col in cols]
+    used = [uses(table, first + j) for j in leaves]
+    lower = [tile(fs_block, ft) for ft in skl_t]
+    spread = [tile(fs, ft) for fs, ft in zip(skl_s, fts)]
+    operator = []
+    for (ah, al), (bh, bl) in zip(lower, spread):
+        both = dg(ah, bh, 1, 0) + dg(al, bh, 1, 0) + dg(ah, bl, 1, 0)
+        operator.append(split2(gain(T) * gain(T) * both))
+    acc = [jnp.zeros((VEC, T), f32) for _ in leaves]
+    for j in leaves:
+        v = own[j][0]
+        tiles = [tile(fss[j], ft) for ft in fts]
+        weighted = [stack2(v if j == q else used[j][q : q + 1] * v) for q in leaves]
+        for q in leaves:
+            acc[q] = acc[q] + times(weighted[q], tiles[q])
+    for q, col in enumerate(cols):
+        near_ref[:, col] = gain(T) * acc[q]
+        mh_ref[:, col], ml_ref[:, col] = operator[q]
+
+
+def peer_kernel(
+    nbr_ref, cnt_ref, part_ref, other_ref, skb_ref, sibling_ref, skg_ref, adj_ref, mid_ref, near_ref, *outs
+):
+    peer_ref, bh_ref, bl_ref, all_ref = outs
+    table = slots(nbr_ref, cnt_ref)
     fts = [feat_tgt(leaf(mid_ref, q)[1]) for q in range(LEAVES_DEV)]
-    fs_block = feat_src(skb_ref[...])
+    core0 = lax.axis_index("core") == 0
+    sib_near = side_near(table, sibling_ref, core0, fts)
+    adj_near = side_near(table, adj_ref, jnp.logical_not(core0), fts)
     for q in range(LEAVES_DEV):
+        p = LEAVES_DEV - 1 - q
+        total = jnp.where(core0, sib_near[q] + adj_near[p], sib_near[p] + adj_near[q])
         col = slice(q * T, (q + 1) * T)
-        ah, al = tile(fs_block, feat_tgt(skl_ref[:, col]))
-        bh, bl = tile(feat_src(skl_ref[:, col]), fts[q])
-        both = dg(ah, bh, 1, 0) + dg(al, bh, 1, 0) + dg(ah, bl, 1, 0)
-        mh_ref[:, col], ml_ref[:, col] = split2(gain(T) * gain(T) * both)
-    acc = [jnp.zeros((VEC, T), f32) for _ in range(LEAVES_DEV)]
-    for j in range(LEAVES_DEV):
-        v, x = leaf(mid_ref, j)
-        fs = feat_src(x)
-        m = uses(table, first + j)
-        for q in range(LEAVES_DEV):
-            vv = stack2(v if j == q else m[q : q + 1] * v)
-            acc[q] = acc[q] + times(vv, tile(fs, fts[q]))
-    for q in range(LEAVES_DEV):
-        near_ref[:, q * T : (q + 1) * T] = gain(T) * acc[q]
-
-
-def peer_kernel(
-    nbr_ref, cnt_ref, part_ref, other_ref, skb_ref, sibling_ref, skg_ref, adj_ref, mid_ref, near_ref, peer_ref, bh_ref, bl_ref, all_ref
-):
+        all_ref[:, col] = near_ref[:, col] + gain(T) * total
     n = part_ref.shape[0]
     ft_own = feat_tgt(skb_ref[...])
     ft_sib = feat_tgt(sibling_ref[VEC + 3 : VEC + 6, :T])
@@ -228,14 +246,6 @@
     kh, kl = tile(feat_src(own_group(skg_ref)), ft_own)
     bh_ref[...] = kh
     bl_ref[...] = kl
-    fts = [feat_tgt(leaf(mid_ref, q)[1]) for q in range(LEAVES_DEV)]
-    acc = [jnp.zeros((VEC, T), f32) for _ in range(LEAVES_DEV)]
-    table = slots(nbr_ref, cnt_ref)
-    side_near(table, sibling_ref, lax.axis_index("core") == 0, fts, acc)
-    side_near(table, adj_ref, lax.axis_index("core") == 1, fts, acc)
-    for q in range(LEAVES_DEV):
-        col = slice(q * T, (q + 1) * T)
-        all_ref[:, col] = near_ref[:, col] + gain(T) * acc[q]
 
 
 def field_kernel(gws_ref, skg_ref, peer_ref, part_ref):

time: 64.9 us -> 64.9 us (level)
  waiting for transfers between devices: 8.88 us -> 9.57 us
  transfers between devices with their start and end apart: 5 -> 5, of which waited for: 2 -> 2; matrix products, arithmetic and copies ran while one was open for 0% -> 0% of each run, Pallas kernels for 13% -> 12%
where the time goes in v11:
time: 64.9 us; the launch traced here: 64.4 us
  starting transfers between devices  31.4 us (48%)
  Pallas kernels  13.5 us (21%)
  blocking collectives  9.82 us (15%)
  waiting for transfers between devices  9.57 us (15%)
    all_to_all x1, starting transfers between devices, body(): part = lax.all_to_all(packed, 'z8', 0, 0, tiled=False)  15.8 us
    all_gather x1, blocking collectives, body(): cell = lax.all_gather(mine, ('zp', 'core'), axis=0, tiled=False)  9.82 us
    all_to_all x1, starting transfers between devices, body(): gws = lax.all_to_all(gw, 'grp', 0, 0, tiled=False)  6.75 us
    all_to_all x1, waiting for transfers between devices, body(): part = lax.all_to_all(packed, 'z8', 0, 0, tiled=False)  6.04 us
    pallas_call x1, Pallas kernels, body(): kernel(peer_kernel, 'peer', (shape(2, VEC, T), square, square, shape(VEC,...  3.99 us
    all_to_all x1, waiting for transfers between devices, body(): gws = lax.all_to_all(gw, 'grp', 0, 0, tiled=False)  3.52 us
    ppermute x1, starting transfers between devices, body(): other = lax.ppermute(part, 'zp', swap)  3.45 us
    pallas_call x1, Pallas kernels, body(): pl.pallas_call(up_kernel, out_shape=(shape(ROWS, n), shape(n_z8, PACK, HA...  3.03 us
  transfers between devices with their start and end apart: 5, of which 2 were waited for; matrix products, arithmetic and copies ran while one was open for 0% of the time, Pallas kernels for 12%

profile of v11, /device:TPU:1, one launch (start us, length us, event | category | flops | bytes accessed | tf_op | source)
XLA Modules:
  0.0 64.4 jit_solution(7453424318029132635)
XLA Ops:
  0.0 3.0 %up.1 = (f32[24,1024]{1,0:T(8,128)}, f32[8,40,128]{2,1,0:T(8,128)}) custom-call(f32[3,1024]{1,0:T(4,128)} %pts_hbm.1, f32[16,1024]{1,0:T(8,128)} %chg_hbm.1, s32[1,1024]{1,0:T(1,128)} %bitcast.6, f32[3,1024]{1,0:T(4,128)} %skl_ref.1, f32[3,256]{1,0:T(4,128)} %skb_ref.3), custom_call_target="tpu_custom_call" | custom-call | tf_op jit(solution)/shard_map/up/pallas_call | solution.py:302
  3.0 0.0 copy-start.2
  3.1 0.0 copy-start
  3.1 0.0 copy-start.1
  3.1 15.8 %all-to-all-start = ((f32[8,40,128]{2,1,0:T(8,128)}), f32[8,40,128]{2,1,0:T(8,128)S(1)}, u32[]{:S(2)}, u32[]{:S(2)}) async-start(f32[8,40,128]{2,1,0:T(8,128)} %get-tuple-element.22), calls=%async_computation | async-start | bytes 327680 | tf_op jit(solution)/shard_map/all_to_all | solution.py:312
  18.9 0.0 copy-done.2
  18.9 0.0 copy-start.5
  18.9 2.9 %collective-permute-start.1 = (f32[24,1024]{1,0:T(8,128)S(1)}, f32[24,1024]{1,0:T(8,128)S(1)}, u32[]{:S(2)}, u32[]{:S(2)}) collective-permute-start(f32[24,1024]{1,0:T(8,128)S(1)} %copy-done.2), channel_id=1, source_target_pairs={{0,1},{1,0},{2,3},{3,2},{4,5},{5,4},{6,7},{7,6},{8,9},{9,8},{10,11... | collective-permute-start | bytes 294920 | tf_op jit(solution)/shard_map/ppermute | solution.py:315
  21.8 0.0 copy-done
  21.8 0.0 copy-start.3
  21.8 2.3 %near.1 = (f32[16,1024]{1,0:T(8,128)S(1)}, bf16[256,1024]{1,0:T(8,128)(2,1)S(1)}, bf16[256,1024]{1,0:T(8,128)(2,1)S(1)}) custom-call(s32[4,8]{1,0:T(4,128)S(1)} %copy-done.4, s32[1,4]{1,0:T(1,128)S(1)} %bitcast.4, f32[24,1024]{1,0:T(8,128)S(1)} %copy-done.2, f32[3,256]{1,0:T(4,128)S(1)} %copy-done.1, f32[3,1024]{1,0:T(4,128)S(1)} %copy-done), custom_call_target="tpu_custom_call" | custom-call | flops 2800000000 | bytes 7340032 | tf_op jit(solution)/shard_map/near/pallas_call | solution.py:317
  24.1 2.5 %collective-permute-start.2 = (f32[24,1024]{1,0:T(8,128)S(1)}, f32[24,1024]{1,0:T(8,128)S(1)}, u32[]{:S(2)}, u32[]{:S(2)}) collective-permute-start(f32[24,1024]{1,0:T(8,128)S(1)} %copy-done.2), channel_id=1, source_target_pairs={{1,2},{3,4},{5,6},{7,8},{9,10},{11,12},{13,14},{15,16},{17,18},{19... | collective-permute-start | bytes 294920 | tf_op jit(solution)/shard_map/ppermute | solution.py:322
  26.7 6.0 %all-to-all-done.part_ref = f32[8,40,128]{2,1,0:T(8,128)S(1)} async-done(((f32[8,40,128]{2,1,0:T(8,128)}), f32[8,40,128]{2,1,0:T(8,128)S(1)}, u32[]{:S(2)}, u32[]{:S(2)}) %all-to-all-start) | async-done | bytes 163872 | tf_op jit(solution)/shard_map/all_to_all | solution.py:312
  32.7 3.5 %collective-permute-start = (f32[8,40,128]{2,1,0:T(8,128)S(1)}, f32[8,40,128]{2,1,0:T(8,128)S(1)}, u32[]{:S(2)}, u32[]{:S(2)}) collective-permute-start(f32[8,40,128]{2,1,0:T(8,128)S(1)} %all-to-all-done.part_ref), channel_id=1, source_target_pairs={{0,2},{2,0},{1,3},{3,1},{4,6},{6,4},{5,7},{7,5},{8,10},{10,8},{9,1... | collective-permute-start | bytes 491528 | tf_op jit(solution)/shard_map/ppermute | solution.py:324
  36.2 1.6 %group.1 = f32[16,16,256]{2,1,0:T(8,128)} custom-call(f32[8,40,128]{2,1,0:T(8,128)S(1)} %all-to-all-done.part_ref, f32[3,4096]{1,0:T(4,128)S(1)} %copy-done.3), custom_call_target="tpu_custom_call" | custom-call | flops 3000000000 | bytes 7864320 | tf_op jit(solution)/shard_map/group/pallas_call | solution.py:325
  37.8 6.8 %all-to-all-start.1 = ((f32[16,16,256]{2,1,0:T(8,128)}), f32[16,16,256]{2,1,0:T(8,128)S(1)}, u32[]{:S(2)}, u32[]{:S(2)}) async-start(f32[16,16,256]{2,1,0:T(8,128)} %group.1), calls=%async_computation.1 | async-start | bytes 524288 | tf_op jit(solution)/shard_map/all_to_all | solution.py:326
  44.6 0.0 collective-permute-done.1.sibling_ref
  44.6 0.0 collective-permute-done.2.adj_ref
  44.6 0.0 collective-permute-done.other_ref
  44.6 4.0 %peer.1 = (f32[2,16,256]{2,1,0:T(8,128)S(1)}, bf16[256,256]{1,0:T(8,128)(2,1)S(1)}, bf16[256,256]{1,0:T(8,128)(2,1)S(1)}, f32[16,1024]{1,0:T(8,128)S(1)}) custom-call(s32[4,8]{1,0:T(4,128)S(1)} %copy-done.4, s32[1,4]{1,0:T(1,128)S(1)} %bitcast.5, f32[8,40,128]{2,1,0:T(8,128)S(1)} %all-to-all-done.part_ref, f32[8,40,128]{2,1,0:T(8,128)S(1)} %collective-permute-done.other_ref, ...), custom_call_target="tpu_custom_call" | custom-call | flops 5299999744 | bytes 13893632 | tf_op jit(solution)/shard_map/peer/pallas_call | solution.py:328
  48.6 3.5 %all-to-all-done.1.gws_ref = f32[16,16,256]{2,1,0:T(8,128)S(1)} async-done(((f32[16,16,256]{2,1,0:T(8,128)}), f32[16,16,256]{2,1,0:T(8,128)S(1)}, u32[]{:S(2)}, u32[]{:S(2)}) %all-to-all-start.1) | async-done | bytes 262176 | tf_op jit(solution)/shard_map/all_to_all | solution.py:326
  52.1 1.4 %field.1 = f32[32,256]{1,0:T(8,128)S(1)} custom-call(f32[16,16,256]{2,1,0:T(8,128)S(1)} %all-to-all-done.1.gws_ref, f32[3,4096]{1,0:T(4,128)S(1)} %copy-done.3, f32[2,16,256]{2,1,0:T(8,128)S(1)} %get-tuple-element.33.peer_ref), custom_call_target="tpu_custom_call" | custom-call | flops 2000000000 | bytes 5242880 | tf_op jit(solution)/shard_map/field/pallas_call | solution.py:331
  53.5 9.8 %all-gather = f32[128,256]{1,0:T(8,128)S(1)} all-gather(f32[32,256]{1,0:T(8,128)S(1)} %field.1), channel_id=2, replica_groups=mesh['grp'=16,'z8'=8,'zp'=2,'core'=2] {'zp','core'}, dimensions={0}, use_global_device_ids=true | all-gather | bytes 163840 | tf_op jit(solution)/shard_map/all_gather | solution.py:332
  63.4 1.1 %down.1 = f32[16,1024]{1,0:T(8,128)} custom-call(f32[4,32,256]{2,1,0:T(8,128)S(1)} %bitcast.3, f32[2,16,256]{2,1,0:T(8,128)S(1)} %get-tuple-element.33.peer_ref, bf16[256,256]{1,0:T(8,128)(2,1)S(1)} %get-tuple-element.34.bh_ref, bf16[256,256]{1,0:T(8,128)(2,1)S(1)} %get-tuple-element.35.bl_ref, bf16[256,1024]{1,0:T(8,128)(2,1)S(1)} %get-tuple-element.36.mh_ref, ...), custom_call_target="tpu_custom_call" | custom-call | flops 100000000 | bytes 262144 | tf_op jit(solution)/shard_map/down/pallas_call | solution.py:333
  (5 shorter events, 0.0 us)
Async XLA Ops:
  3.0 15.8 %copy-start.2 = (f32[24,1024]{1,0:T(8,128)S(1)}, f32[24,1024]{1,0:T(8,128)}, u32[]{:S(2)}) copy-start(f32[24,1024]{1,0:T(8,128)} %get-tuple-element.31.mid_ref) | copy-start | bytes 294916
  3.1 18.7 %copy-start = (f32[3,1024]{1,0:T(4,128)S(1)}, f32[3,1024]{1,0:T(4,128)}, u32[]{:S(2)}) copy-start(f32[3,1024]{1,0:T(4,128)} %skl_ref.1) | copy-start | bytes 36868
  3.1 18.7 %copy-start.1 = (f32[3,256]{1,0:T(4,128)S(1)}, f32[3,256]{1,0:T(4,128)}, u32[]{:S(2)}) copy-start(f32[3,256]{1,0:T(4,128)} %skb_ref.3) | copy-start | bytes 9220
  3.1 29.6 %all-to-all-start = ((f32[8,40,128]{2,1,0:T(8,128)}), f32[8,40,128]{2,1,0:T(8,128)S(1)}, u32[]{:S(2)}, u32[]{:S(2)}) async-start(f32[8,40,128]{2,1,0:T(8,128)} %get-tuple-element.22), calls=%async_computation | async-start | bytes 327680 | tf_op jit(solution)/shard_map/all_to_all | solution.py:312
  18.9 2.9 %copy-start.4 = (s32[4,8]{1,0:T(4,128)S(1)}, s32[4,8]{1,0:T(4,128)}, u32[]{:S(2)}) copy-start(s32[4,8]{1,0:T(4,128)} %nbr_ref.3) | copy-start | bytes 388
  18.9 2.9 %copy-start.5 = (s32[4]{0:T(128)S(1)}, s32[4]{0:T(128)}, u32[]{:S(2)}) copy-start(s32[4]{0:T(128)} %param.12) | copy-start | bytes 52
  18.9 25.7 %collective-permute-start.1 = (f32[24,1024]{1,0:T(8,128)S(1)}, f32[24,1024]{1,0:T(8,128)S(1)}, u32[]{:S(2)}, u32[]{:S(2)}) collective-permute-start(f32[24,1024]{1,0:T(8,128)S(1)} %copy-done.2), channel_id=1, source_target_pairs={{0,1},{1,0},{2,3},{3,2},{4,5},{5,4},{6,7},{7,6},{8,9},{9,8},{10,11... | collective-permute-start | bytes 294920 | tf_op jit(solution)/shard_map/ppermute | solution.py:315
  21.8 14.4 %copy-start.3 = (f32[3,4096]{1,0:T(4,128)S(1)}, f32[3,4096]{1,0:T(4,128)}, u32[]{:S(2)}) copy-start(f32[3,4096]{1,0:T(4,128)} %skg_ref.5) | copy-start | bytes 147460
  24.1 20.4 %collective-permute-start.2 = (f32[24,1024]{1,0:T(8,128)S(1)}, f32[24,1024]{1,0:T(8,128)S(1)}, u32[]{:S(2)}, u32[]{:S(2)}) collective-permute-start(f32[24,1024]{1,0:T(8,128)S(1)} %copy-done.2), channel_id=1, source_target_pairs={{1,2},{3,4},{5,6},{7,8},{9,10},{11,12},{13,14},{15,16},{17,18},{19... | collective-permute-start | bytes 294920 | tf_op jit(solution)/shard_map/ppermute | solution.py:322
  32.7 11.9 %collective-permute-start = (f32[8,40,128]{2,1,0:T(8,128)S(1)}, f32[8,40,128]{2,1,0:T(8,128)S(1)}, u32[]{:S(2)}, u32[]{:S(2)}) collective-permute-start(f32[8,40,128]{2,1,0:T(8,128)S(1)} %all-to-all-done.part_ref), channel_id=1, source_target_pairs={{0,2},{2,0},{1,3},{3,1},{4,6},{6,4},{5,7},{7,5},{8,10},{10,8},{9,1... | collective-permute-start | bytes 491528 | tf_op jit(solution)/shard_map/ppermute | solution.py:324
  37.8 14.3 %all-to-all-start.1 = ((f32[16,16,256]{2,1,0:T(8,128)}), f32[16,16,256]{2,1,0:T(8,128)S(1)}, u32[]{:S(2)}, u32[]{:S(2)}) async-start(f32[16,16,256]{2,1,0:T(8,128)} %group.1), calls=%async_computation.1 | async-start | bytes 524288 | tf_op jit(solution)/shard_map/all_to_all | solution.py:326

commit v12 on v10

--- a/solution.py
+++ b/solution.py
@@ -109,9 +109,13 @@
     hots = [jnp.where(row == mor_ref[:, col].astype(jnp.int16), bf16(1), bf16(0)) for col in cols]
     sums = [dg(parts, hot, 1, 0) for hot in hots]
     srts = [s[:ROWS] + s[ROWS : 2 * ROWS] + s[2 * ROWS :] for s in sums]
-    srts[0] = jnp.concatenate([srts[0][: VEC + 3], skb_ref[...], srts[0][VEC + 6 :]], axis=0)
-    for col, srt in zip(cols, srts):
-        srt_ref[:, col] = srt
+    for c in range(2):
+        low, high = srts[c], srts[2 + c]
+        last = skb_ref[2:3, :] if c == 0 else jnp.zeros((1, T), f32)
+        srt_ref[:VEC, cols[c]] = low[:VEC]
+        srt_ref[VEC : 2 * VEC, cols[c]] = high[:VEC]
+        rest = [low[VEC : VEC + 3], skb_ref[c : c + 1, :], high[VEC : VEC + 3], last]
+        srt_ref[2 * VEC :, cols[c]] = jnp.concatenate(rest, axis=0)
     sources = [feat_src(srt[VEC : VEC + 3]) for srt in srts]
     targets = [feat_tgt(skl_ref[:, col]) for col in cols]
     exponents = [dg(fs, ft, 0, 0) for fs, ft in zip(sources, targets)]
@@ -151,8 +155,10 @@
 
 
 def leaf(ref, j):
-    col = slice(j * T, (j + 1) * T)
-    return ref[:VEC, col], ref[VEC : VEC + 3, col]
+    half, side = j // 2, j % 2
+    col = slice(side * T, (side + 1) * T)
+    point = 2 * VEC + 4 * half
+    return ref[half * VEC : (half + 1) * VEC, col], ref[point : point + 3, col]
 
 
 def slots(nbr_ref, cnt_ref):
@@ -212,7 +218,8 @@
 ):
     n = part_ref.shape[0]
     ft_own = feat_tgt(skb_ref[...])
-    ft_sib = feat_tgt(sibling_ref[VEC + 3 : VEC + 6, :T])
+    x, y, z = sibling_ref[35:36, :T], sibling_ref[35:36, T:], sibling_ref[39:40, :T]
+    ft_sib = feat_tgt(jnp.concatenate([x, y, z], axis=0))
     own = jnp.zeros((VEC, T), f32)
     sib = jnp.zeros((VEC, T), f32)
     for c in range(2 * n):
@@ -291,7 +298,7 @@
     inputs = (points, charges, morton.reshape(1, n), skel_leaf, skel_block)
     srt, packed = pl.pallas_call(
         up_kernel,
-        out_shape=(shape(ROWS, n), shape(n_z8, PACK, HALF)),
+        out_shape=(shape(PACK, n // 2), shape(n_z8, PACK, HALF)),
         in_specs=[pl.BlockSpec(memory_space=pltpu.HBM)] * 5,
         out_specs=(VM, VM),
         scratch_shapes=[pltpu.VMEM(x.shape, x.dtype) for x in inputs]

time: 64.9 us -> 64.9 us (level)
  no operation moved by 1% of the time
where the time goes in v12:
time: 64.9 us; the launch traced here: 64.4 us
  starting transfers between devices  31.4 us (48%)
  Pallas kernels  14.1 us (22%)
  blocking collectives  9.81 us (15%)
  waiting for transfers between devices  8.88 us (14%)
    all_to_all x1, starting transfers between devices, body(): part = lax.all_to_all(packed, 'z8', 0, 0, tiled=False)  15.8 us
    all_gather x1, blocking collectives, body(): cell = lax.all_gather(mine, ('zp', 'core'), axis=0, tiled=False)  9.81 us
    all_to_all x1, starting transfers between devices, body(): gws = lax.all_to_all(gw, 'grp', 0, 0, tiled=False)  6.74 us
    all_to_all x1, waiting for transfers between devices, body(): part = lax.all_to_all(packed, 'z8', 0, 0, tiled=False)  5.59 us
    pallas_call x1, Pallas kernels, body(): kernel(peer_kernel, 'peer', (shape(2, VEC, T), square, square, shape(VEC,...  4.23 us
    ppermute x1, starting transfers between devices, body(): other = lax.ppermute(part, 'zp', swap)  3.48 us
    all_to_all x1, waiting for transfers between devices, body(): gws = lax.all_to_all(gw, 'grp', 0, 0, tiled=False)  3.28 us
    pallas_call x1, Pallas kernels, body(): pl.pallas_call(up_kernel, out_shape=(shape(PACK, n // 2), shape(n_z8, PAC...  3.04 us
  transfers between devices with their start and end apart: 5, of which 2 were waited for; matrix products, arithmetic and copies ran while one was open for 0% of the time, Pallas kernels for 13%

profile of v12, /device:TPU:1, one launch (start us, length us, event | category | flops | bytes accessed | tf_op | source)
XLA Modules:
  0.0 64.4 jit_solution(91861556522629783)
XLA Ops:
  0.0 3.0 %up.1 = (f32[40,512]{1,0:T(8,128)}, f32[8,40,128]{2,1,0:T(8,128)}) custom-call(f32[3,1024]{1,0:T(4,128)} %pts_hbm.1, f32[16,1024]{1,0:T(8,128)} %chg_hbm.1, s32[1,1024]{1,0:T(1,128)} %bitcast.6, f32[3,1024]{1,0:T(4,128)} %skl_ref.1, f32[3,256]{1,0:T(4,128)} %skb_ref.3), custom_call_target="tpu_custom_call" | custom-call | tf_op jit(solution)/shard_map/up/pallas_call | solution.py:299
  3.0 0.0 copy-start.2
  3.1 0.0 copy-start
  3.1 0.0 copy-start.1
  3.1 15.8 %all-to-all-start = ((f32[8,40,128]{2,1,0:T(8,128)}), f32[8,40,128]{2,1,0:T(8,128)S(1)}, u32[]{:S(2)}, u32[]{:S(2)}) async-start(f32[8,40,128]{2,1,0:T(8,128)} %get-tuple-element.22), calls=%async_computation | async-start | bytes 327680 | tf_op jit(solution)/shard_map/all_to_all | solution.py:309
  18.9 0.0 copy-done.2
  18.9 0.0 copy-start.5
  18.9 2.9 %collective-permute-start.1 = (f32[40,512]{1,0:T(8,128)S(1)}, f32[40,512]{1,0:T(8,128)S(1)}, u32[]{:S(2)}, u32[]{:S(2)}) collective-permute-start(f32[40,512]{1,0:T(8,128)S(1)} %copy-done.2), channel_id=1, source_target_pairs={{0,1},{1,0},{2,3},{3,2},{4,5},{5,4},{6,7},{7,6},{8,9},{9,8},{10,11... | collective-permute-start | bytes 245768 | tf_op jit(solution)/shard_map/ppermute | solution.py:312
  21.8 0.0 copy-done
  21.8 0.0 copy-start.3
  21.8 2.8 %near.1 = (f32[16,1024]{1,0:T(8,128)S(1)}, bf16[256,1024]{1,0:T(8,128)(2,1)S(1)}, bf16[256,1024]{1,0:T(8,128)(2,1)S(1)}) custom-call(s32[4,8]{1,0:T(4,128)S(1)} %copy-done.4, s32[1,4]{1,0:T(1,128)S(1)} %bitcast.4, f32[40,512]{1,0:T(8,128)S(1)} %copy-done.2, f32[3,256]{1,0:T(4,128)S(1)} %copy-done.1, f32[3,1024]{1,0:T(4,128)S(1)} %copy-done), custom_call_target="tpu_custom_call" | custom-call | flops 2800000000 | bytes 7340032 | tf_op jit(solution)/shard_map/near/pallas_call | solution.py:314
  24.6 2.5 %collective-permute-start.2 = (f32[40,512]{1,0:T(8,128)S(1)}, f32[40,512]{1,0:T(8,128)S(1)}, u32[]{:S(2)}, u32[]{:S(2)}) collective-permute-start(f32[40,512]{1,0:T(8,128)S(1)} %copy-done.2), channel_id=1, source_target_pairs={{1,2},{3,4},{5,6},{7,8},{9,10},{11,12},{13,14},{15,16},{17,18},{19... | collective-permute-start | bytes 245768 | tf_op jit(solution)/shard_map/ppermute | solution.py:319
  27.1 5.6 %all-to-all-done.part_ref = f32[8,40,128]{2,1,0:T(8,128)S(1)} async-done(((f32[8,40,128]{2,1,0:T(8,128)}), f32[8,40,128]{2,1,0:T(8,128)S(1)}, u32[]{:S(2)}, u32[]{:S(2)}) %all-to-all-start) | async-done | bytes 163872 | tf_op jit(solution)/shard_map/all_to_all | solution.py:309
  32.7 3.5 %collective-permute-start = (f32[8,40,128]{2,1,0:T(8,128)S(1)}, f32[8,40,128]{2,1,0:T(8,128)S(1)}, u32[]{:S(2)}, u32[]{:S(2)}) collective-permute-start(f32[8,40,128]{2,1,0:T(8,128)S(1)} %all-to-all-done.part_ref), channel_id=1, source_target_pairs={{0,2},{2,0},{1,3},{3,1},{4,6},{6,4},{5,7},{7,5},{8,10},{10,8},{9,1... | collective-permute-start | bytes 491528 | tf_op jit(solution)/shard_map/ppermute | solution.py:321
  36.2 1.6 %group.1 = f32[16,16,256]{2,1,0:T(8,128)} custom-call(f32[8,40,128]{2,1,0:T(8,128)S(1)} %all-to-all-done.part_ref, f32[3,4096]{1,0:T(4,128)S(1)} %copy-done.3), custom_call_target="tpu_custom_call" | custom-call | flops 3000000000 | bytes 7864320 | tf_op jit(solution)/shard_map/group/pallas_call | solution.py:322
  37.8 6.7 %all-to-all-start.1 = ((f32[16,16,256]{2,1,0:T(8,128)}), f32[16,16,256]{2,1,0:T(8,128)S(1)}, u32[]{:S(2)}, u32[]{:S(2)}) async-start(f32[16,16,256]{2,1,0:T(8,128)} %group.1), calls=%async_computation.1 | async-start | bytes 524288 | tf_op jit(solution)/shard_map/all_to_all | solution.py:323
  44.6 0.0 collective-permute-done.1.sibling_ref
  44.6 0.0 collective-permute-done.2.adj_ref
  44.6 0.0 collective-permute-done.other_ref
  44.6 4.2 %peer.1 = (f32[2,16,256]{2,1,0:T(8,128)S(1)}, bf16[256,256]{1,0:T(8,128)(2,1)S(1)}, bf16[256,256]{1,0:T(8,128)(2,1)S(1)}, f32[16,1024]{1,0:T(8,128)S(1)}) custom-call(s32[4,8]{1,0:T(4,128)S(1)} %copy-done.4, s32[1,4]{1,0:T(1,128)S(1)} %bitcast.5, f32[8,40,128]{2,1,0:T(8,128)S(1)} %all-to-all-done.part_ref, f32[8,40,128]{2,1,0:T(8,128)S(1)} %collective-permute-done.other_ref, ...), custom_call_target="tpu_custom_call" | custom-call | flops 5299999744 | bytes 13893632 | tf_op jit(solution)/shard_map/peer/pallas_call | solution.py:325
  48.8 3.3 %all-to-all-done.1.gws_ref = f32[16,16,256]{2,1,0:T(8,128)S(1)} async-done(((f32[16,16,256]{2,1,0:T(8,128)}), f32[16,16,256]{2,1,0:T(8,128)S(1)}, u32[]{:S(2)}, u32[]{:S(2)}) %all-to-all-start.1) | async-done | bytes 262176 | tf_op jit(solution)/shard_map/all_to_all | solution.py:323
  52.1 1.4 %field.1 = f32[32,256]{1,0:T(8,128)S(1)} custom-call(f32[16,16,256]{2,1,0:T(8,128)S(1)} %all-to-all-done.1.gws_ref, f32[3,4096]{1,0:T(4,128)S(1)} %copy-done.3, f32[2,16,256]{2,1,0:T(8,128)S(1)} %get-tuple-element.33.peer_ref), custom_call_target="tpu_custom_call" | custom-call | flops 2000000000 | bytes 5242880 | tf_op jit(solution)/shard_map/field/pallas_call | solution.py:328
  53.5 9.8 %all-gather = f32[128,256]{1,0:T(8,128)S(1)} all-gather(f32[32,256]{1,0:T(8,128)S(1)} %field.1), channel_id=2, replica_groups=mesh['grp'=16,'z8'=8,'zp'=2,'core'=2] {'zp','core'}, dimensions={0}, use_global_device_ids=true | all-gather | bytes 163840 | tf_op jit(solution)/shard_map/all_gather | solution.py:329
  63.4 1.1 %down.1 = f32[16,1024]{1,0:T(8,128)} custom-call(f32[4,32,256]{2,1,0:T(8,128)S(1)} %bitcast.3, f32[2,16,256]{2,1,0:T(8,128)S(1)} %get-tuple-element.33.peer_ref, bf16[256,256]{1,0:T(8,128)(2,1)S(1)} %get-tuple-element.34.bh_ref, bf16[256,256]{1,0:T(8,128)(2,1)S(1)} %get-tuple-element.35.bl_ref, bf16[256,1024]{1,0:T(8,128)(2,1)S(1)} %get-tuple-element.36.mh_ref, ...), custom_call_target="tpu_custom_call" | custom-call | flops 100000000 | bytes 262144 | tf_op jit(solution)/shard_map/down/pallas_call | solution.py:330
  (5 shorter events, 0.0 us)
Async XLA Ops:
  3.0 15.8 %copy-start.2 = (f32[40,512]{1,0:T(8,128)S(1)}, f32[40,512]{1,0:T(8,128)}, u32[]{:S(2)}) copy-start(f32[40,512]{1,0:T(8,128)} %get-tuple-element.31.mid_ref) | copy-start | bytes 245764
  3.1 18.7 %copy-start = (f32[3,1024]{1,0:T(4,128)S(1)}, f32[3,1024]{1,0:T(4,128)}, u32[]{:S(2)}) copy-start(f32[3,1024]{1,0:T(4,128)} %skl_ref.1) | copy-start | bytes 36868
  3.1 18.7 %copy-start.1 = (f32[3,256]{1,0:T(4,128)S(1)}, f32[3,256]{1,0:T(4,128)}, u32[]{:S(2)}) copy-start(f32[3,256]{1,0:T(4,128)} %skb_ref.3) | copy-start | bytes 9220
  3.1 29.6 %all-to-all-start = ((f32[8,40,128]{2,1,0:T(8,128)}), f32[8,40,128]{2,1,0:T(8,128)S(1)}, u32[]{:S(2)}, u32[]{:S(2)}) async-start(f32[8,40,128]{2,1,0:T(8,128)} %get-tuple-element.22), calls=%async_computation | async-start | bytes 327680 | tf_op jit(solution)/shard_map/all_to_all | solution.py:309
  18.9 2.9 %copy-start.4 = (s32[4,8]{1,0:T(4,128)S(1)}, s32[4,8]{1,0:T(4,128)}, u32[]{:S(2)}) copy-start(s32[4,8]{1,0:T(4,128)} %nbr_ref.3) | copy-start | bytes 388
  18.9 2.9 %copy-start.5 = (s32[4]{0:T(128)S(1)}, s32[4]{0:T(128)}, u32[]{:S(2)}) copy-start(s32[4]{0:T(128)} %param.12) | copy-start | bytes 52
  18.9 25.7 %collective-permute-start.1 = (f32[40,512]{1,0:T(8,128)S(1)}, f32[40,512]{1,0:T(8,128)S(1)}, u32[]{:S(2)}, u32[]{:S(2)}) collective-permute-start(f32[40,512]{1,0:T(8,128)S(1)} %copy-done.2), channel_id=1, source_target_pairs={{0,1},{1,0},{2,3},{3,2},{4,5},{5,4},{6,7},{7,6},{8,9},{9,8},{10,11... | collective-permute-start | bytes 245768 | tf_op jit(solution)/shard_map/ppermute | solution.py:312
  21.8 14.4 %copy-start.3 = (f32[3,4096]{1,0:T(4,128)S(1)}, f32[3,4096]{1,0:T(4,128)}, u32[]{:S(2)}) copy-start(f32[3,4096]{1,0:T(4,128)} %skg_ref.5) | copy-start | bytes 147460
  24.6 20.0 %collective-permute-start.2 = (f32[40,512]{1,0:T(8,128)S(1)}, f32[40,512]{1,0:T(8,128)S(1)}, u32[]{:S(2)}, u32[]{:S(2)}) collective-permute-start(f32[40,512]{1,0:T(8,128)S(1)} %copy-done.2), channel_id=1, source_target_pairs={{1,2},{3,4},{5,6},{7,8},{9,10},{11,12},{13,14},{15,16},{17,18},{19... | collective-permute-start | bytes 245768 | tf_op jit(solution)/shard_map/ppermute | solution.py:319
  32.7 11.9 %collective-permute-start = (f32[8,40,128]{2,1,0:T(8,128)S(1)}, f32[8,40,128]{2,1,0:T(8,128)S(1)}, u32[]{:S(2)}, u32[]{:S(2)}) collective-permute-start(f32[8,40,128]{2,1,0:T(8,128)S(1)} %all-to-all-done.part_ref), channel_id=1, source_target_pairs={{0,2},{2,0},{1,3},{3,1},{4,6},{6,4},{5,7},{7,5},{8,10},{10,8},{9,1... | collective-permute-start | bytes 491528 | tf_op jit(solution)/shard_map/ppermute | solution.py:321
  37.8 14.3 %all-to-all-start.1 = ((f32[16,16,256]{2,1,0:T(8,128)}), f32[16,16,256]{2,1,0:T(8,128)S(1)}, u32[]{:S(2)}, u32[]{:S(2)}) async-start(f32[16,16,256]{2,1,0:T(8,128)} %group.1), calls=%async_computation.1 | async-start | bytes 524288 | tf_op jit(solution)/shard_map/all_to_all | solution.py:323

commit v13 on v10

--- a/solution.py
+++ b/solution.py
@@ -168,20 +168,20 @@
     return jnp.sum(jnp.where(table == source, 1.0, 0.0), axis=1, keepdims=True)
 
 
-def side_near(table, blk_ref, on_right, fts, acc):
+def side_near(table, blk_ref, on_right, fts):
     first = first_leaf() + jnp.where(on_right, LEAVES_DEV, -LEAVES_DEV)
+    targets = [jnp.where(on_right, fts[e], fts[LEAVES_DEV - 1 - e]) for e in range(LEAVES_DEV)]
+    acc = [jnp.zeros((VEC, T), f32) for _ in range(LEAVES_DEV)]
     for d in range(LEAVES_DEV):
         (v0, x0), (v1, x1) = leaf(blk_ref, d), leaf(blk_ref, LEAVES_DEV - 1 - d)
         v = jnp.where(on_right, v0, v1)
         fs = feat_src(jnp.where(on_right, x0, x1))
-        source = first + jnp.where(on_right, d, LEAVES_DEV - 1 - d)
-        m = uses(table, source)
+        m = uses(table, first + jnp.where(on_right, d, LEAVES_DEV - 1 - d))
         for e in range(d, LEAVES_DEV):
             q0, q1 = e, LEAVES_DEV - 1 - e
             times_used = jnp.where(on_right, m[q0 : q0 + 1], m[q1 : q1 + 1])
-            r = times(stack2(times_used * v), tile(fs, jnp.where(on_right, fts[q0], fts[q1])))
-            acc[q0] = acc[q0] + jnp.where(on_right, r, 0.0)
-            acc[q1] = acc[q1] + jnp.where(on_right, 0.0, r)
+            acc[e] = acc[e] + times(stack2(times_used * v), tile(fs, targets[e]))
+    return acc
 
 
 def near_kernel(nbr_ref, cnt_ref, mid_ref, skb_ref, skl_ref, near_ref, mh_ref, ml_ref):
@@ -208,8 +208,19 @@
 
 
 def peer_kernel(
-    nbr_ref, cnt_ref, part_ref, other_ref, skb_ref, sibling_ref, skg_ref, adj_ref, mid_ref, near_ref, peer_ref, bh_ref, bl_ref, all_ref
+    nbr_ref, cnt_ref, part_ref, other_ref, skb_ref, sibling_ref, skg_ref, adj_ref, mid_ref, near_ref, *outs
 ):
+    peer_ref, bh_ref, bl_ref, all_ref = outs
+    table = slots(nbr_ref, cnt_ref)
+    fts = [feat_tgt(leaf(mid_ref, q)[1]) for q in range(LEAVES_DEV)]
+    core0 = lax.axis_index("core") == 0
+    sib_near = side_near(table, sibling_ref, core0, fts)
+    adj_near = side_near(table, adj_ref, jnp.logical_not(core0), fts)
+    for q in range(LEAVES_DEV):
+        p = LEAVES_DEV - 1 - q
+        total = jnp.where(core0, sib_near[q] + adj_near[p], sib_near[p] + adj_near[q])
+        col = slice(q * T, (q + 1) * T)
+        all_ref[:, col] = near_ref[:, col] + gain(T) * total
     n = part_ref.shape[0]
     ft_own = feat_tgt(skb_ref[...])
     ft_sib = feat_tgt(sibling_ref[VEC + 3 : VEC + 6, :T])
@@ -228,14 +239,6 @@
     kh, kl = tile(feat_src(own_group(skg_ref)), ft_own)
     bh_ref[...] = kh
     bl_ref[...] = kl
-    fts = [feat_tgt(leaf(mid_ref, q)[1]) for q in range(LEAVES_DEV)]
-    acc = [jnp.zeros((VEC, T), f32) for _ in range(LEAVES_DEV)]
-    table = slots(nbr_ref, cnt_ref)
-    side_near(table, sibling_ref, lax.axis_index("core") == 0, fts, acc)
-    side_near(table, adj_ref, lax.axis_index("core") == 1, fts, acc)
-    for q in range(LEAVES_DEV):
-        col = slice(q * T, (q + 1) * T)
-        all_ref[:, col] = near_ref[:, col] + gain(T) * acc[q]
 
 
 def field_kernel(gws_ref, skg_ref, peer_ref, part_ref):

time: 64.9 us -> 64.9 us (level)
  no operation moved by 1% of the time
where the time goes in v13:
time: 64.9 us; the launch traced here: 64.4 us
  starting transfers between devices  31.4 us (48%)
  Pallas kernels  13.9 us (21%)
  blocking collectives  9.82 us (15%)
  waiting for transfers between devices  9.12 us (14%)
    all_to_all x1, starting transfers between devices, body(): part = lax.all_to_all(packed, 'z8', 0, 0, tiled=False)  15.8 us
    all_gather x1, blocking collectives, body(): cell = lax.all_gather(mine, ('zp', 'core'), axis=0, tiled=False)  9.82 us
    all_to_all x1, starting transfers between devices, body(): gws = lax.all_to_all(gw, 'grp', 0, 0, tiled=False)  6.75 us
    all_to_all x1, waiting for transfers between devices, body(): part = lax.all_to_all(packed, 'z8', 0, 0, tiled=False)  5.59 us
    pallas_call x1, Pallas kernels, body(): kernel(peer_kernel, 'peer', (shape(2, VEC, T), square, square, shape(VEC,...  3.98 us
    all_to_all x1, waiting for transfers between devices, body(): gws = lax.all_to_all(gw, 'grp', 0, 0, tiled=False)  3.53 us
    ppermute x1, starting transfers between devices, body(): other = lax.ppermute(part, 'zp', swap)  3.47 us
    pallas_call x1, Pallas kernels, body(): pl.pallas_call(up_kernel, out_shape=(shape(ROWS, n), shape(n_z8, PACK, HA...  3.03 us
  transfers between devices with their start and end apart: 5, of which 2 were waited for; matrix products, arithmetic and copies ran while one was open for 0% of the time, Pallas kernels for 13%

profile of v13, /device:TPU:1, one launch (start us, length us, event | category | flops | bytes accessed | tf_op | source)
XLA Modules:
  0.0 64.4 jit_solution(13607410763149358572)
XLA Ops:
  0.0 3.0 %up.1 = (f32[24,1024]{1,0:T(8,128)}, f32[8,40,128]{2,1,0:T(8,128)}) custom-call(f32[3,1024]{1,0:T(4,128)} %pts_hbm.1, f32[16,1024]{1,0:T(8,128)} %chg_hbm.1, s32[1,1024]{1,0:T(1,128)} %bitcast.6, f32[3,1024]{1,0:T(4,128)} %skl_ref.1, f32[3,256]{1,0:T(4,128)} %skb_ref.3), custom_call_target="tpu_custom_call" | custom-call | tf_op jit(solution)/shard_map/up/pallas_call | solution.py:295
  3.0 0.0 copy-start.2
  3.1 0.0 copy-start
  3.1 0.0 copy-start.1
  3.1 15.8 %all-to-all-start = ((f32[8,40,128]{2,1,0:T(8,128)}), f32[8,40,128]{2,1,0:T(8,128)S(1)}, u32[]{:S(2)}, u32[]{:S(2)}) async-start(f32[8,40,128]{2,1,0:T(8,128)} %get-tuple-element.22), calls=%async_computation | async-start | bytes 327680 | tf_op jit(solution)/shard_map/all_to_all | solution.py:305
  18.9 0.0 copy-done.2
  18.9 0.0 copy-start.5
  18.9 2.9 %collective-permute-start.1 = (f32[24,1024]{1,0:T(8,128)S(1)}, f32[24,1024]{1,0:T(8,128)S(1)}, u32[]{:S(2)}, u32[]{:S(2)}) collective-permute-start(f32[24,1024]{1,0:T(8,128)S(1)} %copy-done.2), channel_id=1, source_target_pairs={{0,1},{1,0},{2,3},{3,2},{4,5},{5,4},{6,7},{7,6},{8,9},{9,8},{10,11... | collective-permute-start | bytes 294920 | tf_op jit(solution)/shard_map/ppermute | solution.py:308
  21.8 0.0 copy-start.3
  21.8 2.8 %near.1 = (f32[16,1024]{1,0:T(8,128)S(1)}, bf16[256,1024]{1,0:T(8,128)(2,1)S(1)}, bf16[256,1024]{1,0:T(8,128)(2,1)S(1)}) custom-call(s32[4,8]{1,0:T(4,128)S(1)} %copy-done.4, s32[1,4]{1,0:T(1,128)S(1)} %bitcast.4, f32[24,1024]{1,0:T(8,128)S(1)} %copy-done.2, f32[3,256]{1,0:T(4,128)S(1)} %copy-done.1, f32[3,1024]{1,0:T(4,128)S(1)} %copy-done), custom_call_target="tpu_custom_call" | custom-call | flops 2800000000 | bytes 7340032 | tf_op jit(solution)/shard_map/near/pallas_call | solution.py:310
  24.6 2.5 %collective-permute-start.2 = (f32[24,1024]{1,0:T(8,128)S(1)}, f32[24,1024]{1,0:T(8,128)S(1)}, u32[]{:S(2)}, u32[]{:S(2)}) collective-permute-start(f32[24,1024]{1,0:T(8,128)S(1)} %copy-done.2), channel_id=1, source_target_pairs={{1,2},{3,4},{5,6},{7,8},{9,10},{11,12},{13,14},{15,16},{17,18},{19... | collective-permute-start | bytes 294920 | tf_op jit(solution)/shard_map/ppermute | solution.py:315
  27.1 5.6 %all-to-all-done.part_ref = f32[8,40,128]{2,1,0:T(8,128)S(1)} async-done(((f32[8,40,128]{2,1,0:T(8,128)}), f32[8,40,128]{2,1,0:T(8,128)S(1)}, u32[]{:S(2)}, u32[]{:S(2)}) %all-to-all-start) | async-done | bytes 163872 | tf_op jit(solution)/shard_map/all_to_all | solution.py:305
  32.7 3.5 %collective-permute-start = (f32[8,40,128]{2,1,0:T(8,128)S(1)}, f32[8,40,128]{2,1,0:T(8,128)S(1)}, u32[]{:S(2)}, u32[]{:S(2)}) collective-permute-start(f32[8,40,128]{2,1,0:T(8,128)S(1)} %all-to-all-done.part_ref), channel_id=1, source_target_pairs={{0,2},{2,0},{1,3},{3,1},{4,6},{6,4},{5,7},{7,5},{8,10},{10,8},{9,1... | collective-permute-start | bytes 491528 | tf_op jit(solution)/shard_map/ppermute | solution.py:317
  36.2 0.0 copy-done.3
  36.2 1.6 %group.1 = f32[16,16,256]{2,1,0:T(8,128)} custom-call(f32[8,40,128]{2,1,0:T(8,128)S(1)} %all-to-all-done.part_ref, f32[3,4096]{1,0:T(4,128)S(1)} %copy-done.3), custom_call_target="tpu_custom_call" | custom-call | flops 3000000000 | bytes 7864320 | tf_op jit(solution)/shard_map/group/pallas_call | solution.py:318
  37.8 6.8 %all-to-all-start.1 = ((f32[16,16,256]{2,1,0:T(8,128)}), f32[16,16,256]{2,1,0:T(8,128)S(1)}, u32[]{:S(2)}, u32[]{:S(2)}) async-start(f32[16,16,256]{2,1,0:T(8,128)} %group.1), calls=%async_computation.1 | async-start | bytes 524288 | tf_op jit(solution)/shard_map/all_to_all | solution.py:319
  44.6 0.0 collective-permute-done.1.sibling_ref
  44.6 0.0 collective-permute-done.2.adj_ref
  44.6 0.0 collective-permute-done.other_ref
  44.6 4.0 %peer.1 = (f32[2,16,256]{2,1,0:T(8,128)S(1)}, bf16[256,256]{1,0:T(8,128)(2,1)S(1)}, bf16[256,256]{1,0:T(8,128)(2,1)S(1)}, f32[16,1024]{1,0:T(8,128)S(1)}) custom-call(s32[4,8]{1,0:T(4,128)S(1)} %copy-done.4, s32[1,4]{1,0:T(1,128)S(1)} %bitcast.5, f32[8,40,128]{2,1,0:T(8,128)S(1)} %all-to-all-done.part_ref, f32[8,40,128]{2,1,0:T(8,128)S(1)} %collective-permute-done.other_ref, ...), custom_call_target="tpu_custom_call" | custom-call | flops 5299999744 | bytes 13893632 | tf_op jit(solution)/shard_map/peer/pallas_call | solution.py:321
  48.6 3.5 %all-to-all-done.1.gws_ref = f32[16,16,256]{2,1,0:T(8,128)S(1)} async-done(((f32[16,16,256]{2,1,0:T(8,128)}), f32[16,16,256]{2,1,0:T(8,128)S(1)}, u32[]{:S(2)}, u32[]{:S(2)}) %all-to-all-start.1) | async-done | bytes 262176 | tf_op jit(solution)/shard_map/all_to_all | solution.py:319
  52.1 1.4 %field.1 = f32[32,256]{1,0:T(8,128)S(1)} custom-call(f32[16,16,256]{2,1,0:T(8,128)S(1)} %all-to-all-done.1.gws_ref, f32[3,4096]{1,0:T(4,128)S(1)} %copy-done.3, f32[2,16,256]{2,1,0:T(8,128)S(1)} %get-tuple-element.33.peer_ref), custom_call_target="tpu_custom_call" | custom-call | flops 2000000000 | bytes 5242880 | tf_op jit(solution)/shard_map/field/pallas_call | solution.py:324
  53.5 9.8 %all-gather = f32[128,256]{1,0:T(8,128)S(1)} all-gather(f32[32,256]{1,0:T(8,128)S(1)} %field.1), channel_id=2, replica_groups=mesh['grp'=16,'z8'=8,'zp'=2,'core'=2] {'zp','core'}, dimensions={0}, use_global_device_ids=true | all-gather | bytes 163840 | tf_op jit(solution)/shard_map/all_gather | solution.py:325
  63.4 1.1 %down.1 = f32[16,1024]{1,0:T(8,128)} custom-call(f32[4,32,256]{2,1,0:T(8,128)S(1)} %bitcast.3, f32[2,16,256]{2,1,0:T(8,128)S(1)} %get-tuple-element.33.peer_ref, bf16[256,256]{1,0:T(8,128)(2,1)S(1)} %get-tuple-element.34.bh_ref, bf16[256,256]{1,0:T(8,128)(2,1)S(1)} %get-tuple-element.35.bl_ref, bf16[256,1024]{1,0:T(8,128)(2,1)S(1)} %get-tuple-element.36.mh_ref, ...), custom_call_target="tpu_custom_call" | custom-call | flops 100000000 | bytes 262144 | tf_op jit(solution)/shard_map/down/pallas_call | solution.py:326
  (5 shorter events, 0.0 us)
Async XLA Ops:
  3.0 15.8 %copy-start.2 = (f32[24,1024]{1,0:T(8,128)S(1)}, f32[24,1024]{1,0:T(8,128)}, u32[]{:S(2)}) copy-start(f32[24,1024]{1,0:T(8,128)} %get-tuple-element.31.mid_ref) | copy-start | bytes 294916
  3.1 18.7 %copy-start = (f32[3,1024]{1,0:T(4,128)S(1)}, f32[3,1024]{1,0:T(4,128)}, u32[]{:S(2)}) copy-start(f32[3,1024]{1,0:T(4,128)} %skl_ref.1) | copy-start | bytes 36868
  3.1 18.7 %copy-start.1 = (f32[3,256]{1,0:T(4,128)S(1)}, f32[3,256]{1,0:T(4,128)}, u32[]{:S(2)}) copy-start(f32[3,256]{1,0:T(4,128)} %skb_ref.3) | copy-start | bytes 9220
  3.1 29.6 %all-to-all-start = ((f32[8,40,128]{2,1,0:T(8,128)}), f32[8,40,128]{2,1,0:T(8,128)S(1)}, u32[]{:S(2)}, u32[]{:S(2)}) async-start(f32[8,40,128]{2,1,0:T(8,128)} %get-tuple-element.22), calls=%async_computation | async-start | bytes 327680 | tf_op jit(solution)/shard_map/all_to_all | solution.py:305
  18.9 2.9 %copy-start.4 = (s32[4,8]{1,0:T(4,128)S(1)}, s32[4,8]{1,0:T(4,128)}, u32[]{:S(2)}) copy-start(s32[4,8]{1,0:T(4,128)} %nbr_ref.3) | copy-start | bytes 388
  18.9 2.9 %copy-start.5 = (s32[4]{0:T(128)S(1)}, s32[4]{0:T(128)}, u32[]{:S(2)}) copy-start(s32[4]{0:T(128)} %param.12) | copy-start | bytes 52
  18.9 25.7 %collective-permute-start.1 = (f32[24,1024]{1,0:T(8,128)S(1)}, f32[24,1024]{1,0:T(8,128)S(1)}, u32[]{:S(2)}, u32[]{:S(2)}) collective-permute-start(f32[24,1024]{1,0:T(8,128)S(1)} %copy-done.2), channel_id=1, source_target_pairs={{0,1},{1,0},{2,3},{3,2},{4,5},{5,4},{6,7},{7,6},{8,9},{9,8},{10,11... | collective-permute-start | bytes 294920 | tf_op jit(solution)/shard_map/ppermute | solution.py:308
  21.8 14.4 %copy-start.3 = (f32[3,4096]{1,0:T(4,128)S(1)}, f32[3,4096]{1,0:T(4,128)}, u32[]{:S(2)}) copy-start(f32[3,4096]{1,0:T(4,128)} %skg_ref.5) | copy-start | bytes 147460
  24.6 20.0 %collective-permute-start.2 = (f32[24,1024]{1,0:T(8,128)S(1)}, f32[24,1024]{1,0:T(8,128)S(1)}, u32[]{:S(2)}, u32[]{:S(2)}) collective-permute-start(f32[24,1024]{1,0:T(8,128)S(1)} %copy-done.2), channel_id=1, source_target_pairs={{1,2},{3,4},{5,6},{7,8},{9,10},{11,12},{13,14},{15,16},{17,18},{19... | collective-permute-start | bytes 294920 | tf_op jit(solution)/shard_map/ppermute | solution.py:315
  32.7 11.9 %collective-permute-start = (f32[8,40,128]{2,1,0:T(8,128)S(1)}, f32[8,40,128]{2,1,0:T(8,128)S(1)}, u32[]{:S(2)}, u32[]{:S(2)}) collective-permute-start(f32[8,40,128]{2,1,0:T(8,128)S(1)} %all-to-all-done.part_ref), channel_id=1, source_target_pairs={{0,2},{2,0},{1,3},{3,1},{4,6},{6,4},{5,7},{7,5},{8,10},{10,8},{9,1... | collective-permute-start | bytes 491528 | tf_op jit(solution)/shard_map/ppermute | solution.py:317
  37.8 14.3 %all-to-all-start.1 = ((f32[16,16,256]{2,1,0:T(8,128)}), f32[16,16,256]{2,1,0:T(8,128)S(1)}, u32[]{:S(2)}, u32[]{:S(2)}) async-start(f32[16,16,256]{2,1,0:T(8,128)} %group.1), calls=%async_computation.1 | async-start | bytes 524288 | tf_op jit(solution)/shard_map/all_to_all | solution.py:319
